TPU v7x, 256 devices: a whole 4x4x8 slice. The times are simulated.
256 devices in a mesh: dp: 2 (over core), tile: 32 (over x, z), chan: 4 (over y).
Axes of the slice: x: 4, y: 4, z: 8, core: 2. Of those that a mesh axis runs over, the one named last changes fastest.
Arguments:
- pixels: float32 [48, 65536], P(None, ('dp', 'tile')), may hold values from -6 to 6
- tile_slide: int32 [1024], P(('dp', 'tile')), may hold values from 0 to 63, as said below
- tile_count: int32 [64], P(('dp', 'tile')), may hold values from 8 to 16, as said below
- w_patch: float32 [96, 48], P('chan'), may hold values from -0.875 to 0.875
- b_patch: float32 [96], P('chan'), may hold values from -3 to 3
- dw_kernel: float32 [96, 49], P('chan'), may hold values from -0.875 to 0.875
- dw_bias: float32 [96], P('chan'), may hold values from -3 to 3
- layernorm_gain: float32 [96], P('chan'), may hold values from 0.25 to 1.75
- layernorm_bias: float32 [96], P('chan'), may hold values from -3 to 3
- w_up: float32 [384, 96], P('chan'), may hold values from -0.625 to 0.625
- b_up: float32 [384], P('chan'), may hold values from -3 to 3
- w_down: float32 [384, 96], P('chan'), may hold values from -0.3125 to 0.3125
- b_down: float32 [96], P('chan'), may hold values from -3 to 3
- w_head: float32 [96], P('chan'), may hold values from -3 to 3
- target: float32 [128], P(('dp', 'tile')), may hold values from -4 to 4
Outputs:
- g_w_patch: float32 [96, 48], P('chan')
- g_b_patch: float32 [96], P('chan')
- g_dw_kernel: float32 [96, 49], P('chan')
- g_dw_bias: float32 [96], P('chan')
- g_ln_gain: float32 [96], P('chan')
- g_ln_bias: float32 [96], P('chan')
- g_w_up: float32 [384, 96], P('chan')
- g_b_up: float32 [384], P('chan')
- g_w_down: float32 [384, 96], P('chan')
- g_b_down: float32 [96], P('chan')
- g_w_head: float32 [96], P('chan')
- loss: float32 [], replicated
Inputs may be any that keep to these rules, and one draw needn't show every extreme that they name: `tile_slide`: in every slide group a run of 4 consecutive slides, neither the group's first nor its last, receives no slot; other slides may receive none too. `tile_count`: at least 8 live slots a device; some device has all 16 live in every draw.
All inputs are finite; a program needn't handle non-finite values.
Results may differ from a plain program's by a relative error of at most 0.00029.
Values sent between devices are 32-bit elements; how exact they have to be, the bound alone decides.
A program may use at most 64 MiB of HBM per device.

v0:
```python
import jax
import jax.numpy as jnp
from jax import lax
from jax.sharding import PartitionSpec as P

SIDE = 8


epsilon = 1e-06
highest = lax.Precision.HIGHEST


def depthwise(stem_grid, kernel, bias):
    side_len = stem_grid.shape[-1]
    padded = jnp.pad(stem_grid, ((0, 0), (0, 0), (3, 3), (3, 3)))
    total = jnp.zeros_like(stem_grid)
    for kernel_row in range(7):
        for kernel_col in range(7):
            weight_tap = kernel[:, kernel_row * 7 + kernel_col][:, None, None, None]
            total = (
                total
                + weight_tap
                * padded[
                    :, :, kernel_row : kernel_row + side_len, kernel_col : kernel_col + side_len
                ]
            )
    return total + bias[:, None, None, None]


def stem_local(w_patch, b_patch, dw_kernel, dw_bias, pixels):
    local_width = w_patch.shape[0]
    tile_num = pixels.shape[1] // (SIDE * SIDE)
    stem = jnp.dot(w_patch, pixels, precision=highest) + b_patch[:, None]
    mixed_features = depthwise(
        stem.reshape(local_width, tile_num, SIDE, SIDE), dw_kernel, dw_bias
    ).reshape(local_width, -1)
    return (stem, mixed_features)


def channel_pool(stem, layer_out, b_down, onehot, tile_num):
    local_width = stem.shape[0]
    features = stem + layer_out + b_down[:, None]
    pooled = jnp.mean(features.reshape(local_width, tile_num, SIDE * SIDE), axis=2)
    return jnp.dot(onehot.T, pooled.T, precision=highest)


def features_grad(onehot, d_sums_all, local_width, tile_num):
    area = SIDE * SIDE
    d_pooled = jnp.dot(onehot, d_sums_all, precision=highest).T
    return jnp.broadcast_to((d_pooled / area)[:, :, None], (local_width, tile_num, area)).reshape(
        local_width, tile_num * area
    )


def per_device(
    pixels,
    tile_slide,
    tile_count,
    w_patch,
    b_patch,
    dw_kernel,
    dw_bias,
    layernorm_gain,
    layernorm_bias,
    w_up,
    b_up,
    w_down,
    b_down,
    w_head,
    target,
):
    chan_count = lax.axis_size("chan")
    local_width = w_patch.shape[0]
    channel_width = local_width * chan_count
    tile_num = tile_slide.shape[0]
    slide_dev = target.shape[0]
    group_slides = slide_dev * lax.axis_size("tile")
    all_slides = group_slides * lax.axis_size("dp")
    live = (jnp.arange(tile_num, dtype=jnp.int32) < tile_count[0]).astype(jnp.float32)
    onehot = (tile_slide[:, None] == jnp.arange(group_slides, dtype=jnp.int32)[None, :]).astype(
        jnp.float32
    ) * live[:, None]
    slide_count = jnp.sum(onehot, axis=0)
    (stem, mixed_features), stem_pull = jax.vjp(
        lambda a, b, c, d: stem_local(a, b, c, d, pixels), w_patch, b_patch, dw_kernel, dw_bias
    )
    totals = lax.psum(
        (jnp.sum(mixed_features, axis=0), jnp.sum(mixed_features * mixed_features, axis=0)), "chan"
    )
    average_value = totals[0] / channel_width
    variance = totals[1] / channel_width - average_value * average_value
    inverse_deviation = lax.rsqrt(variance + epsilon)
    centered_input = (mixed_features - average_value) * inverse_deviation
    normalized_rows = centered_input * layernorm_gain[:, None] + layernorm_bias[:, None]
    normed_all = lax.all_gather(normalized_rows, "chan", axis=0, tiled=True)
    pre_act = jnp.dot(w_up, normed_all, precision=highest) + b_up[:, None]
    hidden, gelu_pull = jax.vjp(lambda value: jax.nn.gelu(value, approximate=False), pre_act)
    columns = w_down
    layer_out = lax.psum_scatter(
        jnp.dot(columns.T, hidden, precision=highest), "chan", scatter_dimension=0, tiled=True
    )
    slide_part = channel_pool(stem, layer_out, b_down, onehot, tile_num)
    owned_sums, owned_counts = (
        lax.psum_scatter(slide_part, "tile", scatter_dimension=0, tiled=True),
        lax.psum_scatter(slide_count, "tile", scatter_dimension=0, tiled=True),
    )
    counts = jnp.maximum(owned_counts, 1.0)
    slide_feat = owned_sums / counts[:, None]
    logit = lax.psum(jnp.dot(slide_feat, w_head, precision=highest), "chan")
    error = logit - target
    loss_part = 0.5 * jnp.sum(error * error) / all_slides
    d_logit = error / all_slides
    g_head = jnp.dot(slide_feat.T, d_logit, precision=highest)
    d_sums = d_logit[:, None] * w_head[None, :] / counts[:, None]
    d_sums_all = lax.all_gather(d_sums, "tile", axis=0, tiled=True)
    d_features = features_grad(onehot, d_sums_all, local_width, tile_num)
    g_b_down = jnp.sum(d_features, axis=1)
    d_out_all = lax.all_gather(d_features, "chan", axis=0, tiled=True)
    g_w_down = jnp.dot(hidden, d_out_all.T, precision=highest)
    d_hidden = jnp.dot(w_down, d_out_all, precision=highest)
    d_pre = gelu_pull(d_hidden)[0]
    g_w_up = jnp.dot(d_pre, normed_all.T, precision=highest)
    g_b_up = jnp.sum(d_pre, axis=1)
    columns = w_up
    normalized_gradient = lax.psum_scatter(
        jnp.dot(columns.T, d_pre, precision=highest), "chan", scatter_dimension=0, tiled=True
    )
    gain_gradient = jnp.sum(normalized_gradient * centered_input, axis=1)
    g_shift = jnp.sum(normalized_gradient, axis=1)
    centered_gradient = normalized_gradient * layernorm_gain[:, None]
    backward_sums = lax.psum(
        (jnp.sum(centered_gradient, axis=0), jnp.sum(centered_gradient * centered_input, axis=0)),
        "chan",
    )
    mixed_gradient = inverse_deviation * (
        centered_gradient
        - backward_sums[0] / channel_width
        - centered_input * (backward_sums[1] / channel_width)
    )
    g_patch, g_bpatch, g_kernel, g_dwbias = stem_pull((d_features, mixed_gradient))
    summed = lax.psum(
        (
            g_patch,
            g_bpatch,
            g_kernel,
            g_dwbias,
            gain_gradient,
            g_shift,
            g_w_up,
            g_b_up,
            g_w_down,
            g_b_down,
            g_head,
            loss_part,
        ),
        ("dp", "tile"),
    )
    return summed


def solution(mesh):
    in_specs = (
        P(None, ("dp", "tile")),
        P(("dp", "tile")),
        P(("dp", "tile")),
        P("chan", None),
        P("chan"),
        P("chan", None),
        P("chan"),
        P("chan"),
        P("chan"),
        P("chan", None),
        P("chan"),
        P("chan", None),
        P("chan"),
        P("chan"),
        P(("dp", "tile")),
    )
    out_specs = (
        P("chan", None),
        P("chan"),
        P("chan", None),
        P("chan"),
        P("chan"),
        P("chan"),
        P("chan", None),
        P("chan"),
        P("chan", None),
        P("chan"),
        P("chan"),
        P(),
    )
    return jax.shard_map(
        per_device, mesh=mesh, in_specs=in_specs, out_specs=out_specs, check_vma=False
    )
```

profile of v0, /device:TPU:1, one launch (start us, length us, event | category | flops | bytes accessed | tf_op | source)
XLA Modules:
  0.0 583.6 jit_solution(18157848405234515097)
XLA Ops:
  7.3 1.5 slice_reduce_fusion.46
  8.8 2.0 slice_reduce_fusion.48
  10.7 2.0 slice_reduce_fusion.47
  12.7 1.0 convolution_add_fusion.1
  13.9 4.0 fusion.39
  18.3 9.6 %all-reduce.104 = (f32[1024]{0:T(1024)S(1)}, f32[1024]{0:T(1024)S(1)}) all-reduce(f32[1024]{0:T(1024)S(1)} %reduce_sum.554, f32[1024]{0:T(1024)S(1)} %reduce_sum.552), channel_id=1, replica_groups=mesh['dp'=2,'tile'=32,'chan'=4] {'chan'}, use_global_device_ids=true, to_apply=%region_3.4 | all-reduce | flops 2048 | bytes 16384 | tf_op jit(solution)/shard_map/psum | solution.py:87
  28.0 10.9 %all_gather.9 = f32[96,1024]{1,0:T(8,128)S(1)} all-gather(f32[24,1024]{1,0:T(8,128)S(1)} %multiply_add_fusion), channel_id=1, replica_groups=mesh['dp'=2,'tile'=32,'chan'=4] {'chan'}, dimensions={0}, use_global_device_ids=true | all-gather | bytes 491520 | tf_op jit(solution)/shard_map/all_gather | solution.py:95
  38.9 1.3 fusion
  40.3 1.3 convolution_bitcast_fusion.2
  43.6 24.4 %reduce-scatter.3.cloned.1.call-done = f32[24,1024]{1,0:T(8,128)} async-done(((f32[96,1024]{1,0:T(8,128)}), f32[24,1024]{1,0:T(8,128)}) %reduce-scatter.3.cloned.1.call-update) | async-done | bytes 98320 | tf_op jit(solution)/shard_map/reduce_scatter | solution.py:99
  68.0 1.0 add_add_fusion.1
  69.6 115.5 %all-reduce.102 = (f32[64]{0:T(128)S(1)}, f32[64,24]{1,0:T(8,128)S(1)}) all-reduce(f32[64]{0:T(128)S(1)} %select_reduce_fusion, f32[64,24]{1,0:T(8,128)S(1)} %fusion.21), channel_id=4, replica_groups=mesh['dp'=2,'tile'=32,'chan'=4] {'tile'}, use_global_device_ids=true, to_apply=%region_8.9.clone | all-reduce | flops 1600 | bytes 12800
  185.4 7.3 %psum.121 = f32[2]{0:T(128)S(1)} all-reduce(f32[2]{0:T(128)S(1)} %convolution_bitcast_fusion.4), channel_id=1, replica_groups=mesh['dp'=2,'tile'=32,'chan'=4] {'chan'}, use_global_device_ids=true, to_apply=%region_9.10 | all-reduce | flops 2 | bytes 16 | tf_op jit(solution)/shard_map/psum | solution.py:109
  192.6 0.6 multiply_reduce_fusion.53
  193.3 30.8 %all-gather = f32[32,2,24]{2,1,0:T(2,128)S(1)} all-gather(f32[1,2,24]{2,1,0:T(2,128)S(1)} %divide_bitcast_fusion), channel_id=1, replica_groups=mesh['dp'=2,'tile'=32,'chan'=4] {'tile'}, dimensions={0}, use_global_device_ids=true | all-gather | bytes 6336 | tf_op jit(solution)/shard_map/all_gather | solution.py:115
  224.6 9.9 %all_gather.11 = f32[96,1024]{1,0:T(8,128)S(1)} all-gather(f32[24,1024]{1,0:T(8,128)S(1)} %copy.43), channel_id=1, replica_groups=mesh['dp'=2,'tile'=32,'chan'=4] {'chan'}, dimensions={0}, use_global_device_ids=true | all-gather | bytes 491520 | tf_op jit(solution)/shard_map/all_gather | solution.py:118
  234.5 0.7 fusion.41
  235.2 1.3 convolution_bitcast_fusion
  238.4 57.9 %reduce-scatter.5.cloned.1.call-done = f32[24,1024]{1,0:T(8,128)} async-done(((f32[96,1024]{1,0:T(8,128)}), f32[24,1024]{1,0:T(8,128)}) %reduce-scatter.5.cloned.1.call-update) | async-done | bytes 98320 | tf_op jit(solution)/shard_map/reduce_scatter | solution.py:125
  296.3 1.1 multiply_reduce_fusion.49
  297.4 7.4 %all-reduce.103 = (f32[1024]{0:T(1024)S(1)}, f32[1024]{0:T(1024)S(1)}) all-reduce(f32[1024]{0:T(1024)S(1)} %get-tuple-element.111, f32[1024]{0:T(1024)S(1)} %get-tuple-element.112), channel_id=1, replica_groups=mesh['dp'=2,'tile'=32,'chan'=4] {'chan'}, use_global_device_ids=true, to_apply=%region_14.15 | all-reduce | flops 2048 | bytes 16384 | tf_op jit(solution)/shard_map/psum | solution.py:131
  304.9 1.1 fusion.40
  306.2 0.8 multiply_reduce_fusion.45
  307.0 1.5 multiply_reduce_fusion.46
  308.5 1.3 multiply_reduce_fusion.47
  309.9 0.9 broadcast_multiply_fusion.2
  310.7 1.2 broadcast_multiply_fusion.1
  312.0 1.2 broadcast_multiply_fusion
  313.2 5.1 pad_add_fusion
  318.7 1.0 fusion.42
  319.8 256.4 %all-reduce.106 = (f32[24,48]{1,0:T(8,128)}, f32[24]{0:T(128)}, f32[24,49]{0,1:T(8,128)S(1)}, f32[24]{0:T(128)}, f32[24]{0:T(128)}, /*index=5*/f32[24]{0:T(128)}...) all-reduce(f32[24,48]{1,0:T(8,128)S(1)} %fusion.42, ...), channel_id=1, replica_groups=mesh['dp'=2,'tile'=32,'chan'=4] {'dp','tile'}, use_global_device_ids=true, to_apply=%region_15.16 | all-reduce | flops 21001 | bytes 168008 | tf_op jit(solution)/shard_map/psum | solution.py:141
  576.1 0.7 copy.45
  (55 shorter events, 4.8 us)
Async XLA Ops:
  7.2 5.5 copy-start
  7.2 20.7 %copy-start.3 = (f32[24]{0:T(128)S(1)}, f32[24]{0:T(128)}, u32[]{:S(2)}) copy-start(f32[24]{0:T(128)} %param.22) | copy-start | bytes 292
  7.2 20.7 %copy-start.4 = (f32[24]{0:T(128)S(1)}, f32[24]{0:T(128)}, u32[]{:S(2)}) copy-start(f32[24]{0:T(128)} %param.23) | copy-start | bytes 292
  7.2 60.8 %reduce-scatter.3.cloned.1.call-start = ((), (), s32[]{:S(2)}) async-start(), calls=%async_computation.2 | async-start | bytes 491520 | tf_op jit(solution)/shard_map/reduce_scatter | solution.py:99
  12.7 26.2 %copy-start.2 = (f32[96,96]{1,0:T(8,128)S(1)}, f32[96,96]{1,0:T(8,128)}, u32[]{:S(2)}) copy-start(f32[96,96]{1,0:T(8,128)} %param.24) | copy-start | bytes 110596
  12.7 26.2 %copy-start.8 = (f32[96]{0:T(128)S(1)}, f32[96]{0:T(128)}, u32[]{:S(2)}) copy-start(f32[96]{0:T(128)} %param.25) | copy-start | bytes 1156
  38.9 1.4 copy-start.1
  38.9 3.4 copy-start.10
  38.9 4.6 copy-start.9
  38.9 29.1 %copy-start.5 = (f32[24]{0:T(128)S(1)}, f32[24]{0:T(128)}, u32[]{:S(2)}) copy-start(f32[24]{0:T(128)} %param.27) | copy-start | bytes 292
  40.2 145.0 %copy-start.6 = (f32[24]{0:T(128)S(1)}, f32[24]{0:T(128)}, u32[]{:S(2)}) copy-start(f32[24]{0:T(128)} %param.28) | copy-start | bytes 292
  40.2 152.4 %copy-start.7 = (f32[2]{0:T(128)S(1)}, f32[2]{0:T(128)}, u32[]{:S(2)}) copy-start(f32[2]{0:T(128)} %param.29) | copy-start | bytes 28
  41.6 254.8 %reduce-scatter.5.cloned.1.call-start = ((), (), s32[]{:S(2)}) async-start(), calls=%async_computation.3 | async-start | bytes 491520 | tf_op jit(solution)/shard_map/reduce_scatter | solution.py:125
Sparse Core Ops, SparseCore 0:
  41.7 26.2 reduce-scatter.2
  236.6 59.6 reduce-scatter.4
where the time goes:
time: 584 us
  blocking collectives  448 us (77%)
  waiting for transfers between devices  82.3 us (14%)
  other arithmetic  21 us (4%)
  between operations  16.3 us (3%)
  matrix products  8.16 us (1%)
  local copies, waits for them, and re-layouts  7.87 us (1%)
    psum x1, blocking collectives, per_device(): lax.psum((g_patch, g_bpatch, g_kernel, g_dwbias, gain_gradient, g_shift,...  256 us
    unnamed x1, blocking collectives  116 us
    reduce_scatter x1, waiting for transfers between devices, per_device(): lax.psum_scatter(jnp.dot(columns.T, d_pre, precision=highest), 'chan', sc...  57.9 us
    all_gather x1, blocking collectives, per_device(): d_sums_all = lax.all_gather(d_sums, 'tile', axis=0, tiled=True)  30.8 us
    reduce_scatter x1, waiting for transfers between devices, per_device(): lax.psum_scatter(jnp.dot(columns.T, hidden, precision=highest), 'chan', s...  24.4 us
  transfers between devices with their start and end apart: 2, of which 2 were waited for; matrix products, arithmetic and copies ran while one was open for 0% of the time, Pallas kernels for 0%

commit v1 on v0

v1 whole, which is shorter than its diff:
```python
import jax
import jax.numpy as jnp
import numpy as np
from jax import lax
from jax.sharding import Mesh
from jax.sharding import PartitionSpec as P

SIDE = 8
X_SPAN = 4


epsilon = 1e-06
highest = lax.Precision.HIGHEST


def depthwise(stem_grid, kernel, bias):
    side_len = stem_grid.shape[-1]
    padded = jnp.pad(stem_grid, ((0, 0), (0, 0), (3, 3), (3, 3)))
    total = jnp.zeros_like(stem_grid)
    for kernel_row in range(7):
        for kernel_col in range(7):
            weight_tap = kernel[:, kernel_row * 7 + kernel_col][:, None, None, None]
            total = (
                total
                + weight_tap
                * padded[
                    :, :, kernel_row : kernel_row + side_len, kernel_col : kernel_col + side_len
                ]
            )
    return total + bias[:, None, None, None]


def block_pooled(params, pixels):
    w_patch, b_patch, dw_kernel, dw_bias, gain, shift, w_up, b_up, w_down, b_down = params
    width = w_patch.shape[0]
    tile_num = pixels.shape[1] // (SIDE * SIDE)
    stem = jnp.dot(w_patch, pixels, precision=highest) + b_patch[:, None]
    mixed = depthwise(stem.reshape(width, tile_num, SIDE, SIDE), dw_kernel, dw_bias).reshape(
        width, -1
    )
    average_value = jnp.mean(mixed, axis=0)
    variance = jnp.mean(mixed * mixed, axis=0) - average_value * average_value
    normed = (mixed - average_value) * lax.rsqrt(variance + epsilon) * gain[:, None] + shift[
        :, None
    ]
    pre_act = jnp.dot(w_up, normed, precision=highest) + b_up[:, None]
    hidden = jax.nn.gelu(pre_act, approximate=False)
    features = stem + jnp.dot(w_down.T, hidden, precision=highest) + b_down[:, None]
    return jnp.mean(features.reshape(width, tile_num, SIDE * SIDE), axis=2)


def psum_steps(value, axes):
    for axis in axes:
        value = lax.psum(value, axis)
    return value


def per_device(
    pixels,
    tile_slide,
    tile_count,
    w_patch,
    b_patch,
    dw_kernel,
    dw_bias,
    layernorm_gain,
    layernorm_bias,
    w_up,
    b_up,
    w_down,
    b_down,
    w_head,
    target,
):
    chan_count = lax.axis_size("chan")
    chan = lax.axis_index("chan")
    tile = lax.axis_index("tx") * lax.axis_size("tz") + lax.axis_index("tz")
    slot_count = tile_slide.shape[0]
    slots = slot_count // chan_count
    area = SIDE * SIDE
    slide_dev = target.shape[0]
    group_slides = slide_dev * lax.axis_size("tx") * lax.axis_size("tz")
    all_slides = group_slides * lax.axis_size("dp")

    shards = (
        w_patch,
        b_patch,
        dw_kernel,
        dw_bias,
        layernorm_gain,
        layernorm_bias,
        w_up,
        b_up,
        w_down,
        b_down,
        w_head,
    )
    sizes = [s.size for s in shards]
    packed = jnp.concatenate([s.reshape(1, -1) for s in shards], axis=1)
    gathered = lax.all_gather(packed, "chan", axis=0, tiled=True)
    full = []
    offset = 0
    for s, n in zip(shards, sizes):
        full.append(gathered[:, offset : offset + n].reshape((chan_count * s.shape[0],) + s.shape[1:]))
        offset += n
    params = tuple(full[:10])
    head = full[10]

    my_pixels = lax.dynamic_slice_in_dim(pixels, chan * slots * area, slots * area, axis=1)
    my_slide = lax.dynamic_slice_in_dim(tile_slide, chan * slots, slots)
    slot_index = chan * slots + jnp.arange(slots, dtype=jnp.int32)
    live = (slot_index < tile_count[0]).astype(jnp.float32)
    onehot = (my_slide[:, None] == jnp.arange(group_slides, dtype=jnp.int32)[None, :]).astype(
        jnp.float32
    ) * live[:, None]

    pooled, pull = jax.vjp(lambda p: block_pooled(p, my_pixels), params)
    slide_part = jnp.dot(onehot.T, pooled.T, precision=highest)
    placed = lax.dynamic_update_slice_in_dim(
        jnp.zeros((group_slides,), jnp.float32),
        jnp.where(chan == 0, target, 0.0),
        tile * slide_dev,
        axis=0,
    )
    slide_pack = jnp.concatenate(
        [slide_part, jnp.sum(onehot, axis=0)[:, None], placed[:, None]], axis=1
    )
    slide_pack = psum_steps(slide_pack, ("chan", "tx", "tz"))
    width = slide_part.shape[1]
    sums = slide_pack[:, :width]
    counts = jnp.maximum(slide_pack[:, width], 1.0)
    target_all = slide_pack[:, width + 1]

    slide_feat = sums / counts[:, None]
    logit = jnp.dot(slide_feat, head, precision=highest)
    error = logit - target_all
    loss_part = 0.5 * jnp.sum(error * error) / all_slides
    d_logit = error / all_slides
    g_head = jnp.dot(slide_feat.T, d_logit, precision=highest)
    d_sums = d_logit[:, None] * head[None, :] / counts[:, None]
    d_pooled = jnp.dot(onehot, d_sums, precision=highest).T
    grads = pull(d_pooled)[0]

    lead = tile == 0
    g_head = jnp.where(lead & (chan == 0), g_head, 0.0)
    flat = jnp.concatenate(
        [g.reshape(chan_count, -1) for g in grads] + [g_head.reshape(chan_count, -1)], axis=1
    )
    mine = lax.psum_scatter(flat, "chan", scatter_dimension=0, tiled=True).reshape(-1)
    mine = jnp.concatenate([mine, jnp.where(lead, loss_part, 0.0)[None]])
    mine = psum_steps(mine, ("dp", "tx", "tz"))

    outs = []
    offset = 0
    for s in shards[:10] + shards[10:]:
        n = s.size
        outs.append(mine[offset : offset + n].reshape(s.shape))
        offset += n
    outs.append(mine[offset])
    return tuple(outs)


def solution(mesh):
    devices = np.asarray(mesh.devices)
    dp, tiles, chan = devices.shape
    grid = Mesh(devices.reshape(dp, X_SPAN, tiles // X_SPAN, chan), ("dp", "tx", "tz", "chan"))
    rows = ("dp", "tx", "tz")
    in_specs = (
        P(None, rows),
        P(rows),
        P(rows),
        P("chan", None),
        P("chan"),
        P("chan", None),
        P("chan"),
        P("chan"),
        P("chan"),
        P("chan", None),
        P("chan"),
        P("chan", None),
        P("chan"),
        P("chan"),
        P(rows),
    )
    out_specs = (
        P("chan", None),
        P("chan"),
        P("chan", None),
        P("chan"),
        P("chan"),
        P("chan"),
        P("chan", None),
        P("chan"),
        P("chan", None),
        P("chan"),
        P("chan"),
        P(),
    )
    return jax.shard_map(
        per_device, mesh=grid, in_specs=in_specs, out_specs=out_specs, check_vma=False
    )
```

time: 584 us -> 345 us (0.59)
  blocking collectives: 448 us -> 62.8 us
  waiting for transfers between devices: 82.3 us -> 205 us
  local copies, waits for them, and re-layouts: 7.87 us -> 32 us
  other arithmetic: 21 us -> 13.9 us
    psum x4 -> x3, blocking collectives: 281 us -> 51.1 us  [psum_steps(): value = lax.psum(value, axis)]
    psum x0 -> x3, waiting for transfers between devices: none -> 149 us  [psum_steps(): value = lax.psum(value, axis)]
    unnamed x1 -> x0, blocking collectives: 116 us -> none
    reduce_scatter x2 -> x0, waiting for transfers between devices: 82.3 us -> none  [the longest x1 57.9 us: per_device(): lax.psum_scatter(jnp.dot(columns.T, d_pre, precision=highest), 'chan', sc...]
    unnamed x2 -> x5, waiting for transfers between devices: 0.03 us -> 56.1 us
    all_gather x3 -> x1, blocking collectives: 51.6 us -> 11.7 us  [per_device(): gathered = lax.all_gather(packed, 'chan', axis=0, tiled=True)]
    reshape x3 -> x27, local copies, waits for them, and re-layouts: 0.43 us -> 12.5 us  [the longest x10 4.56 us: per_device(): g.reshape(chan_count, -1)]
    unnamed x24 -> x284, local copies, waits for them, and re-layouts: 1.32 us -> 9.53 us
  transfers between devices with their start and end apart: 2 -> 4, of which waited for: 2 -> 4; matrix products, arithmetic and copies ran while one was open for 0% -> 0% of each run, Pallas kernels for 0% -> 0%
where the time goes in v1:
time: 345 us; the launch traced here: 340 us
  waiting for transfers between devices  205 us (59%)
  blocking collectives  62.8 us (18%)
  local copies, waits for them, and re-layouts  32 us (9%)
  between operations  17 us (5%)
  other arithmetic  13.9 us (4%)
  matrix products  8.51 us (2%)
    psum x3, waiting for transfers between devices, psum_steps(): value = lax.psum(value, axis)  149 us
    unnamed x5, waiting for transfers between devices  56.1 us
    psum x3, blocking collectives, psum_steps(): value = lax.psum(value, axis)  51.1 us
    all_gather x1, blocking collectives, per_device(): gathered = lax.all_gather(packed, 'chan', axis=0, tiled=True)  11.7 us
    unnamed x284, local copies, waits for them, and re-layouts  9.53 us
  transfers between devices with their start and end apart: 4, of which 4 were waited for; matrix products, arithmetic and copies ran while one was open for 0% of the time, Pallas kernels for 0%

profile of v1, /device:TPU:1, one launch (start us, length us, event | category | flops | bytes accessed | tf_op | source)
XLA Modules:
  0.0 339.6 jit_solution(16680903880030789067)
XLA Ops:
  7.3 0.8 reshape.479
  8.2 0.9 reshape.485
  10.3 11.7 %all-gather = f32[4,1,21000]{2,1,0:T(1,128)S(1)} all-gather(f32[1,1,21000]{2,1,0:T(1,128)S(1)} %bitcast.167), channel_id=1, replica_groups=mesh['dp'=2,'tx'=4,'tz'=8,'chan'=4] {'chan'}, dimensions={0}, use_global_device_ids=true | all-gather | bytes 420000 | tf_op jit(solution)/shard_map/all_gather | solution.py:100
  28.8 0.9 multiply_reduce_fusion.48
  30.1 1.3 fusion.3
  32.5 12.9 %psum.42 = f32[64,98]{1,0:T(8,128)S(1)} all-reduce(f32[64,98]{1,0:T(8,128)S(1)} %pad_maximum_fusion.1), channel_id=1, replica_groups=mesh['dp'=2,'tx'=4,'tz'=8,'chan'=4] {'chan'}, use_global_device_ids=true, to_apply=%region_4.5 | all-reduce | flops 6272 | bytes 50176 | tf_op jit(solution)/shard_map/psum | solution.py:54
  45.5 12.6 %psum.43 = f32[64,98]{1,0:T(8,128)S(1)} all-reduce(f32[64,98]{1,0:T(8,128)S(1)} %psum.42), channel_id=1, replica_groups=mesh['dp'=2,'tx'=4,'tz'=8,'chan'=4] {'tx'}, use_global_device_ids=true, to_apply=%region_5.6 | all-reduce | flops 6272 | bytes 50176 | tf_op jit(solution)/shard_map/psum | solution.py:54
  58.1 25.6 %psum.44 = f32[64,98]{1,0:T(8,128)S(1)} all-reduce(f32[64,98]{1,0:T(8,128)S(1)} %psum.43), channel_id=1, replica_groups=mesh['dp'=2,'tx'=4,'tz'=8,'chan'=4] {'tz'}, use_global_device_ids=true, to_apply=%region_6.7 | all-reduce | flops 6272 | bytes 50176 | tf_op jit(solution)/shard_map/psum | solution.py:54
  83.8 1.4 broadcast_multiply_fusion.52
  86.0 0.8 fusion.9
  86.8 1.2 fusion.56
  88.2 1.1 multiply_reduce_fusion.49
  89.4 0.8 fusion.11
  90.2 0.7 fusion.50
  91.0 0.8 multiply_reduce_fusion.45
  91.8 1.0 multiply_reduce_fusion.46
  92.8 0.9 multiply_reduce_fusion.47
  94.7 1.2 broadcast_multiply_fusion.1
  96.0 1.5 broadcast_multiply_fusion
  106.8 1.5 pad_add_fusion.7
  108.3 0.8 copy.121
  109.2 0.7 reshape.503
  110.0 3.2 pad_add_fusion
  115.2 1.1 concatenate.14
  118.3 56.1 %all-reduce.111.cloned.1.call-done = f32[4,21000]{1,0:T(4,128)} async-done(((f32[4,21000]{1,0:T(4,128)}), f32[4,21000]{1,0:T(4,128)}) %all-reduce.111.cloned.1.call-update) | async-done | bytes 336016
  174.3 1.9 dynamic-slice_reduce_fusion
  176.2 0.7 pad_maximum_fusion
  177.0 31.6 %all-reduce.105.cloned.1.call-done = f32[21001]{0:T(1024)} async-done(((f32[21001]{0:T(1024)}), f32[21001]{0:T(1024)}) %all-reduce.105.cloned.1.call-update) | async-done | bytes 84020 | tf_op jit(solution)/shard_map/psum | solution.py:54
  208.6 46.4 %all-reduce.107.cloned.1.call-done = f32[21001]{0:T(1024)} async-done(((f32[21001]{0:T(1024)}), f32[21001]{0:T(1024)}) %all-reduce.107.cloned.1.call-update) | async-done | bytes 84020 | tf_op jit(solution)/shard_map/psum | solution.py:54
  255.1 71.0 %all-reduce.109.cloned.1.call-done = f32[21001]{0:T(1024)} async-done(((f32[21001]{0:T(1024)}), f32[21001]{0:T(1024)}) %all-reduce.109.cloned.1.call-update) | async-done | bytes 84020 | tf_op jit(solution)/shard_map/psum | solution.py:54
  326.1 0.8 slice.559
  328.9 0.9 fusion.55
  (367 shorter events, 27.7 us)
Async XLA Ops:
  7.2 20.9 %copy-start = (f32[48,1024]{1,0:T(8,128)S(1)}, f32[48,1024]{1,0:T(8,128)}, u32[]{:S(2)}) copy-start(f32[48,1024]{1,0:T(8,128)} %param.15) | copy-start | bytes 589828
  7.2 167.1 %all-reduce.111.cloned.1.call-start = ((), (), s32[]{:S(2)}) async-start(), calls=%async_computation.3 | async-start | bytes 675840
  23.3 5.2 %copy-start.22 = (f32[96]{0:T(128)}, f32[96]{0:T(128)S(1)}, u32[]{:S(2)}) copy-start(f32[96]{0:T(128)S(1)} %get-tuple-element.110) | copy-start | bytes 1156
  23.3 5.2 %copy-start.24 = (f32[96]{0:T(128)}, f32[96]{0:T(128)S(1)}, u32[]{:S(2)}) copy-start(f32[96]{0:T(128)S(1)} %get-tuple-element.111) | copy-start | bytes 1156
  23.3 5.2 %copy-start.26 = (f32[96]{0:T(128)}, f32[96]{0:T(128)S(1)}, u32[]{:S(2)}) copy-start(f32[96]{0:T(128)S(1)} %get-tuple-element.112) | copy-start | bytes 1156
  23.3 5.2 %copy-start.28 = (f32[96]{0:T(128)}, f32[96]{0:T(128)S(1)}, u32[]{:S(2)}) copy-start(f32[96]{0:T(128)S(1)} %get-tuple-element.113) | copy-start | bytes 1156
  23.3 5.2 %copy-start.30 = (f32[96]{0:T(128)}, f32[96]{0:T(128)S(1)}, u32[]{:S(2)}) copy-start(f32[96]{0:T(128)S(1)} %get-tuple-element.114) | copy-start | bytes 1156
  23.4 5.2 %copy-start.32 = (f32[96]{0:T(128)}, f32[96]{0:T(128)S(1)}, u32[]{:S(2)}) copy-start(f32[96]{0:T(128)S(1)} %get-tuple-element.115) | copy-start | bytes 1156
  23.4 5.2 %copy-start.34 = (f32[96]{0:T(128)}, f32[96]{0:T(128)S(1)}, u32[]{:S(2)}) copy-start(f32[96]{0:T(128)S(1)} %get-tuple-element.116) | copy-start | bytes 1156
  24.1 4.5 %copy-start.36 = (f32[96]{0:T(128)}, f32[96]{0:T(128)S(1)}, u32[]{:S(2)}) copy-start(f32[96]{0:T(128)S(1)} %get-tuple-element.87) | copy-start | bytes 1156
  24.1 4.5 %copy-start.38 = (f32[96]{0:T(128)}, f32[96]{0:T(128)S(1)}, u32[]{:S(2)}) copy-start(f32[96]{0:T(128)S(1)} %get-tuple-element.102) | copy-start | bytes 1156
  24.1 4.5 %copy-start.40 = (f32[96]{0:T(128)}, f32[96]{0:T(128)S(1)}, u32[]{:S(2)}) copy-start(f32[96]{0:T(128)S(1)} %get-tuple-element.103) | copy-start | bytes 1156
  24.1 4.5 %copy-start.42 = (f32[96]{0:T(128)}, f32[96]{0:T(128)S(1)}, u32[]{:S(2)}) copy-start(f32[96]{0:T(128)S(1)} %get-tuple-element.104) | copy-start | bytes 1156
  24.1 4.5 %copy-start.44 = (f32[96]{0:T(128)}, f32[96]{0:T(128)S(1)}, u32[]{:S(2)}) copy-start(f32[96]{0:T(128)S(1)} %get-tuple-element.105) | copy-start | bytes 1156
  24.1 4.5 %copy-start.50 = (f32[96]{0:T(128)}, f32[96]{0:T(128)S(1)}, u32[]{:S(2)}) copy-start(f32[96]{0:T(128)S(1)} %get-tuple-element.88) | copy-start | bytes 1156
  24.1 4.5 %copy-start.52 = (f32[96]{0:T(128)}, f32[96]{0:T(128)S(1)}, u32[]{:S(2)}) copy-start(f32[96]{0:T(128)S(1)} %get-tuple-element.89) | copy-start | bytes 1156
  24.1 4.5 %copy-start.54 = (f32[96]{0:T(128)}, f32[96]{0:T(128)S(1)}, u32[]{:S(2)}) copy-start(f32[96]{0:T(128)S(1)} %get-tuple-element.90) | copy-start | bytes 1156
  24.2 4.5 %copy-start.56 = (f32[96]{0:T(128)}, f32[96]{0:T(128)S(1)}, u32[]{:S(2)}) copy-start(f32[96]{0:T(128)S(1)} %get-tuple-element.91) | copy-start | bytes 1156
  24.2 4.5 %copy-start.58 = (f32[96]{0:T(128)}, f32[96]{0:T(128)S(1)}, u32[]{:S(2)}) copy-start(f32[96]{0:T(128)S(1)} %get-tuple-element.92) | copy-start | bytes 1156
  24.2 4.5 %copy-start.60 = (f32[96]{0:T(128)}, f32[96]{0:T(128)S(1)}, u32[]{:S(2)}) copy-start(f32[96]{0:T(128)S(1)} %get-tuple-element.93) | copy-start | bytes 1156
  24.2 4.5 %copy-start.62 = (f32[96]{0:T(128)}, f32[96]{0:T(128)S(1)}, u32[]{:S(2)}) copy-start(f32[96]{0:T(128)S(1)} %get-tuple-element.94) | copy-start | bytes 1156
  24.2 4.5 %copy-start.64 = (f32[96]{0:T(128)}, f32[96]{0:T(128)S(1)}, u32[]{:S(2)}) copy-start(f32[96]{0:T(128)S(1)} %get-tuple-element.95) | copy-start | bytes 1156
  24.2 4.5 %copy-start.66 = (f32[96]{0:T(128)}, f32[96]{0:T(128)S(1)}, u32[]{:S(2)}) copy-start(f32[96]{0:T(128)S(1)} %get-tuple-element.96) | copy-start | bytes 1156
  24.2 4.5 %copy-start.68 = (f32[96]{0:T(128)}, f32[96]{0:T(128)S(1)}, u32[]{:S(2)}) copy-start(f32[96]{0:T(128)S(1)} %get-tuple-element.97) | copy-start | bytes 1156
  24.2 4.5 %copy-start.70 = (f32[96]{0:T(128)}, f32[96]{0:T(128)S(1)}, u32[]{:S(2)}) copy-start(f32[96]{0:T(128)S(1)} %get-tuple-element.98) | copy-start | bytes 1156
  24.2 4.5 %copy-start.72 = (f32[96]{0:T(128)}, f32[96]{0:T(128)S(1)}, u32[]{:S(2)}) copy-start(f32[96]{0:T(128)S(1)} %get-tuple-element.99) | copy-start | bytes 1156
  24.2 4.5 %copy-start.74 = (f32[96]{0:T(128)}, f32[96]{0:T(128)S(1)}, u32[]{:S(2)}) copy-start(f32[96]{0:T(128)S(1)} %get-tuple-element.100) | copy-start | bytes 1156
  24.3 4.5 %copy-start.76 = (f32[96]{0:T(128)}, f32[96]{0:T(128)S(1)}, u32[]{:S(2)}) copy-start(f32[96]{0:T(128)S(1)} %get-tuple-element.101) | copy-start | bytes 1156
  25.0 3.8 %copy-start.48 = (f32[96]{0:T(128)}, f32[96]{0:T(128)S(1)}, u32[]{:S(2)}) copy-start(f32[96]{0:T(128)S(1)} %get-tuple-element.69) | copy-start | bytes 1156
  116.3 92.2 %all-reduce.105.cloned.1.call-start = ((), (), s32[]{:S(2)}) async-start(), calls=%async_computation | async-start | bytes 172032 | tf_op jit(solution)/shard_map/psum | solution.py:54
  176.9 78.1 %all-reduce.107.cloned.1.call-start = ((), (), s32[]{:S(2)}) async-start(), calls=%async_computation.1 | async-start | bytes 172032 | tf_op jit(solution)/shard_map/psum | solution.py:54
  208.5 117.5 %all-reduce.109.cloned.1.call-start = ((), (), s32[]{:S(2)}) async-start(), calls=%async_computation.2 | async-start | bytes 172032 | tf_op jit(solution)/shard_map/psum | solution.py:54
  (114 other events, 126.7 us)
Sparse Core Ops, SparseCore 0:
  116.4 57.8 all-reduce.110
  177.0 31.4 all-reduce.104
  210.8 44.1 all-reduce.106
  257.2 68.8 all-reduce.108

commit v2 on v1

--- a/solution.py
+++ b/solution.py
@@ -49,10 +49,20 @@
     return jnp.mean(features.reshape(width, tile_num, SIDE * SIDE), axis=2)
 
 
+def spread_sum(value, axis):
+    count = lax.axis_size(axis)
+    copies = jnp.broadcast_to(value[None], (count,) + value.shape)
+    return jnp.sum(lax.all_to_all(copies, axis, 0, 0, tiled=True), axis=0)
+
+
 def psum_steps(value, axes):
     for axis in axes:
-        value = lax.psum(value, axis)
+        value = spread_sum(value, axis)
     return value
+
+
+def scatter_sum(value, axis):
+    return jnp.sum(lax.all_to_all(value, axis, 0, 0, tiled=True), axis=0)
 
 
 def per_device(
@@ -146,7 +156,7 @@
     flat = jnp.concatenate(
         [g.reshape(chan_count, -1) for g in grads] + [g_head.reshape(chan_count, -1)], axis=1
     )
-    mine = lax.psum_scatter(flat, "chan", scatter_dimension=0, tiled=True).reshape(-1)
+    mine = scatter_sum(flat, "chan")
     mine = jnp.concatenate([mine, jnp.where(lead, loss_part, 0.0)[None]])
     mine = psum_steps(mine, ("dp", "tx", "tz"))
 

time: 345 us -> 153 us (0.44); the launches traced: 340 us -> 152 us
  waiting for transfers between devices: 205 us -> 14.1 us
  between operations: 17 us -> 3.85 us
  starting transfers between devices: 0.16 us -> 11.6 us
  blocking collectives: 62.8 us -> 71.3 us
  local copies, waits for them, and re-layouts: 32 us -> 27.9 us
    psum x3 -> x0, waiting for transfers between devices: 149 us -> none  [psum_steps(): value = lax.psum(value, axis)]
    all_to_all x0 -> x5, blocking collectives: none -> 59.6 us  [spread_sum(): return jnp.sum(lax.all_to_all(copies, axis, 0, 0, tiled=True), axis=0)]
    unnamed x5 -> x0, waiting for transfers between devices: 56.1 us -> none
    psum x3 -> x0, blocking collectives: 51.1 us -> none  [psum_steps(): value = lax.psum(value, axis)]
    all_to_all x0 -> x2, waiting for transfers between devices: none -> 14.1 us  [the longest x1 8.88 us: spread_sum(): return jnp.sum(lax.all_to_all(copies, axis, 0, 0, tiled=True), axis=0)]
    all_to_all x0 -> x2, starting transfers between devices: none -> 11.6 us  [the longest x1 8.19 us: spread_sum(): return jnp.sum(lax.all_to_all(copies, axis, 0, 0, tiled=True), axis=0)]
    unnamed x284 -> x279, local copies, waits for them, and re-layouts: 9.53 us -> 7.74 us
  transfers between devices with their start and end apart: 4 -> 2, of which waited for: 4 -> 2; matrix products, arithmetic and copies ran while one was open for 0% -> 0% of each run, Pallas kernels for 0% -> 0%
where the time goes in v2:
time: 153 us; the launch traced here: 152 us
  blocking collectives  71.3 us (47%)
  local copies, waits for them, and re-layouts  27.9 us (18%)
  other arithmetic  14.6 us (10%)
  waiting for transfers between devices  14.1 us (9%)
  starting transfers between devices  11.6 us (8%)
  matrix products  8.5 us (6%)
  between operations  3.85 us (3%)
    all_to_all x5, blocking collectives, spread_sum(): return jnp.sum(lax.all_to_all(copies, axis, 0, 0, tiled=True), axis=0)  59.6 us
    all_gather x1, blocking collectives, per_device(): gathered = lax.all_gather(packed, 'chan', axis=0, tiled=True)  11.7 us
    all_to_all x1, waiting for transfers between devices, spread_sum(): return jnp.sum(lax.all_to_all(copies, axis, 0, 0, tiled=True), axis=0)  8.88 us
    all_to_all x1, starting transfers between devices, spread_sum(): return jnp.sum(lax.all_to_all(copies, axis, 0, 0, tiled=True), axis=0)  8.19 us
    unnamed x279, local copies, waits for them, and re-layouts  7.74 us
    all_to_all x1, waiting for transfers between devices, scatter_sum(): return jnp.sum(lax.all_to_all(value, axis, 0, 0, tiled=True), axis=0)  5.25 us
    reshape x10, local copies, waits for them, and re-layouts, per_device(): g.reshape(chan_count, -1)  4.6 us
    all_to_all x1, starting transfers between devices, scatter_sum(): return jnp.sum(lax.all_to_all(value, axis, 0, 0, tiled=True), axis=0)  3.45 us
  transfers between devices with their start and end apart: 2, of which 2 were waited for; matrix products, arithmetic and copies ran while one was open for 0% of the time, Pallas kernels for 0%

profile of v2, /device:TPU:1, one launch (start us, length us, event | category | flops | bytes accessed | tf_op | source)
XLA Modules:
  0.0 152.0 jit_solution(17594414538506452823)
XLA Ops:
  0.7 0.8 reshape.499
  1.6 0.9 reshape.505
  3.8 11.7 %all-gather = f32[4,1,21000]{2,1,0:T(1,128)S(1)} all-gather(f32[1,1,21000]{2,1,0:T(1,128)S(1)} %bitcast.168), channel_id=1, replica_groups=mesh['dp'=2,'tx'=4,'tz'=8,'chan'=4] {'chan'}, dimensions={0}, use_global_device_ids=true | all-gather | bytes 420000 | tf_op jit(solution)/shard_map/all_gather | solution.py:110
  16.7 0.7 slice_reduce_fusion.47
  22.2 0.9 multiply_reduce_fusion.48
  23.3 1.3 fusion.3
  25.8 7.8 %all_to_all.42 = f32[4,64,98]{2,1,0:T(8,128)S(1)} all-to-all(f32[4,64,98]{2,1,0:T(8,128)S(1)} %broadcast_in_dim.226), channel_id=1, replica_groups=mesh['dp'=2,'tx'=4,'tz'=8,'chan'=4] {'chan'}, dimensions={0} | all-to-all | bytes 200704 | tf_op jit(solution)/shard_map/all_to_all | solution.py:55
  33.6 8.1 %all_to_all.43 = f32[4,64,98]{2,1,0:T(8,128)S(1)} all-to-all(f32[4,64,98]{2,1,0:T(8,128)S(1)} %broadcast_in_dim.227), channel_id=1, replica_groups=mesh['dp'=2,'tx'=4,'tz'=8,'chan'=4] {'tx'}, dimensions={0} | all-to-all | bytes 200704 | tf_op jit(solution)/shard_map/all_to_all | solution.py:55
  41.7 0.7 broadcast_in_dim.228
  42.4 8.2 %all-to-all-start.2 = ((f32[8,64,98]{2,1,0:T(8,128)}), f32[8,64,98]{2,1,0:T(8,128)S(1)}, u32[]{:S(2)}, u32[]{:S(2)}) async-start(f32[8,64,98]{2,1,0:T(8,128)} %broadcast_in_dim.228), calls=%async_computation.2 | async-start | bytes 524288 | tf_op jit(solution)/shard_map/all_to_all | solution.py:55
  51.1 8.9 %all-to-all-done.2 = f32[8,64,98]{2,1,0:T(8,128)S(1)} async-done(((f32[8,64,98]{2,1,0:T(8,128)}), f32[8,64,98]{2,1,0:T(8,128)S(1)}, u32[]{:S(2)}, u32[]{:S(2)}) %all-to-all-start.2) | async-done | bytes 200736 | tf_op jit(solution)/shard_map/all_to_all | solution.py:55
  60.2 1.4 broadcast_multiply_fusion.52
  62.4 0.8 fusion.9
  63.1 1.2 fusion.56
  64.3 1.1 multiply_reduce_fusion.49
  65.5 0.8 fusion.11
  66.4 0.7 fusion.50
  67.2 0.8 multiply_reduce_fusion.45
  68.0 1.0 multiply_reduce_fusion.46
  69.0 0.9 multiply_reduce_fusion.47
  70.8 1.2 broadcast_multiply_fusion.1
  72.2 1.5 broadcast_multiply_fusion
  82.4 1.5 pad_add_fusion.7
  83.9 0.8 copy.146
  84.7 0.7 reshape.523
  85.5 3.2 %pad_add_fusion = f32[96,4,14,14]{0,3,2,1:T(8,128)S(1)} fusion(f32[96,4,8,8]{0,3,2,1:T(8,128)} %get-tuple-element.140, f32[96,4,8,8]{0,3,2,1:T(8,128)} %get-tuple-element.141, f32[96,4,8,8]{0,3,2,1:T(8,128)} %get-tuple-element.142, f32[96,4,8,8]{0,3,2,1:T(8,128)} %get-tuple-element.143, f32[96,4,8,8]{0,3,2,1:T(8,128)} %get-tuple-element.144, ...), kind=kLoop, calls=%fused_computation.58 | loop fusion | flops 3161088 | bytes 4528128 | tf_op jit(solution)/shard_map/transpose(jvp())/add_any | solution.py:26
  91.1 1.1 copy.149
  92.1 3.5 %all-to-all-start.3 = ((f32[4,1,21000]{2,1,0:T(1,128)}), f32[4,1,21000]{2,1,0:T(1,128)S(1)}, u32[]{:S(2)}, u32[]{:S(2)}) async-start(f32[4,1,21000]{2,1,0:T(1,128)} %copy.149), calls=%async_computation.3 | async-start | bytes 675840 | tf_op jit(solution)/shard_map/all_to_all | solution.py:65
  96.2 5.2 %all-to-all-done.3 = f32[4,1,21000]{2,1,0:T(1,128)S(1)} async-done(((f32[4,1,21000]{2,1,0:T(1,128)}), f32[4,1,21000]{2,1,0:T(1,128)S(1)}, u32[]{:S(2)}, u32[]{:S(2)}) %all-to-all-start.3) | async-done | bytes 336032 | tf_op jit(solution)/shard_map/all_to_all | solution.py:65
  102.0 12.8 %all_to_all.44 = f32[2,1,21001]{2,1,0:T(1,128)S(1)} all-to-all(f32[2,1,21001]{2,1,0:T(1,128)S(1)} %broadcast_in_dim.284), channel_id=1, replica_groups=mesh['dp'=2,'tx'=4,'tz'=8,'chan'=4] {'dp'}, dimensions={0} | all-to-all | bytes 336016 | tf_op jit(solution)/shard_map/all_to_all | solution.py:55
  115.2 9.3 %all_to_all.45 = f32[4,1,21001]{2,1,0:T(1,128)S(1)} all-to-all(f32[4,1,21001]{2,1,0:T(1,128)S(1)} %broadcast_in_dim.285), channel_id=1, replica_groups=mesh['dp'=2,'tx'=4,'tz'=8,'chan'=4] {'tx'}, dimensions={0} | all-to-all | bytes 672032 | tf_op jit(solution)/shard_map/all_to_all | solution.py:55
  125.2 21.6 %all_to_all.46 = f32[8,1,21001]{2,1,0:T(1,128)S(1)} all-to-all(f32[8,1,21001]{2,1,0:T(1,128)S(1)} %broadcast_in_dim.286), channel_id=1, replica_groups=mesh['dp'=2,'tx'=4,'tz'=8,'chan'=4] {'tz'}, dimensions={0} | all-to-all | bytes 1344064 | tf_op jit(solution)/shard_map/all_to_all | solution.py:55
  (368 shorter events, 27.0 us)
Async XLA Ops:
  0.6 20.8 %copy-start = (f32[48,1024]{1,0:T(8,128)S(1)}, f32[48,1024]{1,0:T(8,128)}, u32[]{:S(2)}) copy-start(f32[48,1024]{1,0:T(8,128)} %param.15) | copy-start | bytes 589828
  16.6 5.3 %copy-start.21 = (f32[96]{0:T(128)}, f32[96]{0:T(128)S(1)}, u32[]{:S(2)}) copy-start(f32[96]{0:T(128)S(1)} %get-tuple-element.110) | copy-start | bytes 1156
  16.6 5.3 %copy-start.23 = (f32[96]{0:T(128)}, f32[96]{0:T(128)S(1)}, u32[]{:S(2)}) copy-start(f32[96]{0:T(128)S(1)} %get-tuple-element.111) | copy-start | bytes 1156
  16.6 5.3 %copy-start.25 = (f32[96]{0:T(128)}, f32[96]{0:T(128)S(1)}, u32[]{:S(2)}) copy-start(f32[96]{0:T(128)S(1)} %get-tuple-element.112) | copy-start | bytes 1156
  16.6 5.3 %copy-start.27 = (f32[96]{0:T(128)}, f32[96]{0:T(128)S(1)}, u32[]{:S(2)}) copy-start(f32[96]{0:T(128)S(1)} %get-tuple-element.113) | copy-start | bytes 1156
  16.6 5.3 %copy-start.29 = (f32[96]{0:T(128)}, f32[96]{0:T(128)S(1)}, u32[]{:S(2)}) copy-start(f32[96]{0:T(128)S(1)} %get-tuple-element.114) | copy-start | bytes 1156
  16.6 5.3 %copy-start.31 = (f32[96]{0:T(128)}, f32[96]{0:T(128)S(1)}, u32[]{:S(2)}) copy-start(f32[96]{0:T(128)S(1)} %get-tuple-element.115) | copy-start | bytes 1156
  16.7 5.3 %copy-start.33 = (f32[96]{0:T(128)}, f32[96]{0:T(128)S(1)}, u32[]{:S(2)}) copy-start(f32[96]{0:T(128)S(1)} %get-tuple-element.116) | copy-start | bytes 1156
  17.4 4.6 %copy-start.35 = (f32[96]{0:T(128)}, f32[96]{0:T(128)S(1)}, u32[]{:S(2)}) copy-start(f32[96]{0:T(128)S(1)} %get-tuple-element.87) | copy-start | bytes 1156
  17.4 4.6 %copy-start.37 = (f32[96]{0:T(128)}, f32[96]{0:T(128)S(1)}, u32[]{:S(2)}) copy-start(f32[96]{0:T(128)S(1)} %get-tuple-element.102) | copy-start | bytes 1156
  17.4 4.6 %copy-start.39 = (f32[96]{0:T(128)}, f32[96]{0:T(128)S(1)}, u32[]{:S(2)}) copy-start(f32[96]{0:T(128)S(1)} %get-tuple-element.103) | copy-start | bytes 1156
  17.4 4.6 %copy-start.41 = (f32[96]{0:T(128)}, f32[96]{0:T(128)S(1)}, u32[]{:S(2)}) copy-start(f32[96]{0:T(128)S(1)} %get-tuple-element.104) | copy-start | bytes 1156
  17.4 4.6 %copy-start.43 = (f32[96]{0:T(128)}, f32[96]{0:T(128)S(1)}, u32[]{:S(2)}) copy-start(f32[96]{0:T(128)S(1)} %get-tuple-element.105) | copy-start | bytes 1156
  17.4 4.6 %copy-start.49 = (f32[96]{0:T(128)}, f32[96]{0:T(128)S(1)}, u32[]{:S(2)}) copy-start(f32[96]{0:T(128)S(1)} %get-tuple-element.88) | copy-start | bytes 1156
  17.4 4.6 %copy-start.51 = (f32[96]{0:T(128)}, f32[96]{0:T(128)S(1)}, u32[]{:S(2)}) copy-start(f32[96]{0:T(128)S(1)} %get-tuple-element.89) | copy-start | bytes 1156
  17.4 4.6 %copy-start.53 = (f32[96]{0:T(128)}, f32[96]{0:T(128)S(1)}, u32[]{:S(2)}) copy-start(f32[96]{0:T(128)S(1)} %get-tuple-element.90) | copy-start | bytes 1156
  17.4 4.6 %copy-start.55 = (f32[96]{0:T(128)}, f32[96]{0:T(128)S(1)}, u32[]{:S(2)}) copy-start(f32[96]{0:T(128)S(1)} %get-tuple-element.91) | copy-start | bytes 1156
  17.5 4.6 %copy-start.57 = (f32[96]{0:T(128)}, f32[96]{0:T(128)S(1)}, u32[]{:S(2)}) copy-start(f32[96]{0:T(128)S(1)} %get-tuple-element.92) | copy-start | bytes 1156
  17.5 4.6 %copy-start.59 = (f32[96]{0:T(128)}, f32[96]{0:T(128)S(1)}, u32[]{:S(2)}) copy-start(f32[96]{0:T(128)S(1)} %get-tuple-element.93) | copy-start | bytes 1156
  17.5 4.6 %copy-start.61 = (f32[96]{0:T(128)}, f32[96]{0:T(128)S(1)}, u32[]{:S(2)}) copy-start(f32[96]{0:T(128)S(1)} %get-tuple-element.94) | copy-start | bytes 1156
  17.5 4.6 %copy-start.63 = (f32[96]{0:T(128)}, f32[96]{0:T(128)S(1)}, u32[]{:S(2)}) copy-start(f32[96]{0:T(128)S(1)} %get-tuple-element.95) | copy-start | bytes 1156
  17.5 4.6 %copy-start.65 = (f32[96]{0:T(128)}, f32[96]{0:T(128)S(1)}, u32[]{:S(2)}) copy-start(f32[96]{0:T(128)S(1)} %get-tuple-element.96) | copy-start | bytes 1156
  17.5 4.6 %copy-start.67 = (f32[96]{0:T(128)}, f32[96]{0:T(128)S(1)}, u32[]{:S(2)}) copy-start(f32[96]{0:T(128)S(1)} %get-tuple-element.97) | copy-start | bytes 1156
  17.5 4.6 %copy-start.69 = (f32[96]{0:T(128)}, f32[96]{0:T(128)S(1)}, u32[]{:S(2)}) copy-start(f32[96]{0:T(128)S(1)} %get-tuple-element.98) | copy-start | bytes 1156
  17.5 4.6 %copy-start.71 = (f32[96]{0:T(128)}, f32[96]{0:T(128)S(1)}, u32[]{:S(2)}) copy-start(f32[96]{0:T(128)S(1)} %get-tuple-element.99) | copy-start | bytes 1156
  17.5 4.6 %copy-start.73 = (f32[96]{0:T(128)}, f32[96]{0:T(128)S(1)}, u32[]{:S(2)}) copy-start(f32[96]{0:T(128)S(1)} %get-tuple-element.100) | copy-start | bytes 1156
  17.5 4.6 %copy-start.75 = (f32[96]{0:T(128)}, f32[96]{0:T(128)S(1)}, u32[]{:S(2)}) copy-start(f32[96]{0:T(128)S(1)} %get-tuple-element.101) | copy-start | bytes 1156
  18.3 3.9 %copy-start.47 = (f32[96]{0:T(128)}, f32[96]{0:T(128)S(1)}, u32[]{:S(2)}) copy-start(f32[96]{0:T(128)S(1)} %get-tuple-element.69) | copy-start | bytes 1156
  18.3 3.9 %copy-start.77 = (f32[96]{0:T(128)}, f32[96]{0:T(128)S(1)}, u32[]{:S(2)}) copy-start(f32[96]{0:T(128)S(1)} %get-tuple-element.70) | copy-start | bytes 1156
  18.3 3.9 %copy-start.79 = (f32[96]{0:T(128)}, f32[96]{0:T(128)S(1)}, u32[]{:S(2)}) copy-start(f32[96]{0:T(128)S(1)} %get-tuple-element.84) | copy-start | bytes 1156
  42.4 17.5 %all-to-all-start.2 = ((f32[8,64,98]{2,1,0:T(8,128)}), f32[8,64,98]{2,1,0:T(8,128)S(1)}, u32[]{:S(2)}, u32[]{:S(2)}) async-start(f32[8,64,98]{2,1,0:T(8,128)} %broadcast_in_dim.228), calls=%async_computation.2 | async-start | bytes 524288 | tf_op jit(solution)/shard_map/all_to_all | solution.py:55
  92.1 9.4 %all-to-all-start.3 = ((f32[4,1,21000]{2,1,0:T(1,128)}), f32[4,1,21000]{2,1,0:T(1,128)S(1)}, u32[]{:S(2)}, u32[]{:S(2)}) async-start(f32[4,1,21000]{2,1,0:T(1,128)} %copy.149), calls=%async_computation.3 | async-start | bytes 675840 | tf_op jit(solution)/shard_map/all_to_all | solution.py:65
  (109 other events, 117.5 us)

commit v3 on v2

--- a/solution.py
+++ b/solution.py
@@ -50,7 +50,7 @@
 
 
 def spread_sum(value, axis):
-    count = lax.axis_size(axis)
+    count = lax.psum(1, axis)
     copies = jnp.broadcast_to(value[None], (count,) + value.shape)
     return jnp.sum(lax.all_to_all(copies, axis, 0, 0, tiled=True), axis=0)
 
@@ -63,6 +63,24 @@
 
 def scatter_sum(value, axis):
     return jnp.sum(lax.all_to_all(value, axis, 0, 0, tiled=True), axis=0)
+
+
+def gather_chan(shards, chan_count, spread):
+    packed = jnp.concatenate([s.reshape(1, -1) for s in shards], axis=1)
+    if spread:
+        copies = jnp.broadcast_to(packed, (chan_count, packed.shape[1]))
+        gathered = lax.all_to_all(copies, "chan", 0, 0, tiled=True)
+    else:
+        gathered = lax.all_gather(packed, "chan", axis=0, tiled=True)
+    full = []
+    offset = 0
+    for s in shards:
+        n = s.size
+        full.append(
+            gathered[:, offset : offset + n].reshape((chan_count * s.shape[0],) + s.shape[1:])
+        )
+        offset += n
+    return tuple(full)
 
 
 def per_device(
@@ -105,14 +123,9 @@
         b_down,
         w_head,
     )
-    sizes = [s.size for s in shards]
-    packed = jnp.concatenate([s.reshape(1, -1) for s in shards], axis=1)
-    gathered = lax.all_gather(packed, "chan", axis=0, tiled=True)
-    full = []
-    offset = 0
-    for s, n in zip(shards, sizes):
-        full.append(gathered[:, offset : offset + n].reshape((chan_count * s.shape[0],) + s.shape[1:]))
-        offset += n
+    full = gather_chan(shards[:6], chan_count, spread=False) + gather_chan(
+        shards[6:], chan_count, spread=True
+    )
     params = tuple(full[:10])
     head = full[10]
 
@@ -135,7 +148,7 @@
     slide_pack = jnp.concatenate(
         [slide_part, jnp.sum(onehot, axis=0)[:, None], placed[:, None]], axis=1
     )
-    slide_pack = psum_steps(slide_pack, ("chan", "tx", "tz"))
+    slide_pack = psum_steps(slide_pack, (("chan", "tx"), "tz"))
     width = slide_part.shape[1]
     sums = slide_pack[:, :width]
     counts = jnp.maximum(slide_pack[:, width], 1.0)

time: 153 us -> 155 us (1.013)
  starting transfers between devices: 11.6 us -> 16.8 us
  blocking collectives: 71.3 us -> 66.9 us
    all_to_all x0 -> x1, starting transfers between devices: none -> 5.13 us  [gather_chan(): gathered = lax.all_to_all(copies, 'chan', 0, 0, tiled=True)]
    all_to_all x5 -> x4, blocking collectives: 59.6 us -> 57 us  [spread_sum(): return jnp.sum(lax.all_to_all(copies, axis, 0, 0, tiled=True), axis=0)]
    all_gather x1, blocking collectives: 11.7 us -> 9.94 us  [gather_chan(): gathered = lax.all_gather(packed, 'chan', axis=0, tiled=True)]
    unnamed x279 -> x282, local copies, waits for them, and re-layouts: 7.74 us -> 9.01 us
  transfers between devices with their start and end apart: 2 -> 3, of which waited for: 2 -> 2; matrix products, arithmetic and copies ran while one was open for 0% -> 3% of each run, Pallas kernels for 0% -> 0%
where the time goes in v3:
time: 155 us; the launch traced here: 154 us
  blocking collectives  66.9 us (43%)
  local copies, waits for them, and re-layouts  29.3 us (19%)
  starting transfers between devices  16.8 us (11%)
  other arithmetic  14.8 us (10%)
  waiting for transfers between devices  14.1 us (9%)
  matrix products  8.53 us (6%)
  between operations  3.83 us (2%)
    all_to_all x4, blocking collectives, spread_sum(): return jnp.sum(lax.all_to_all(copies, axis, 0, 0, tiled=True), axis=0)  57 us
    all_gather x1, blocking collectives, gather_chan(): gathered = lax.all_gather(packed, 'chan', axis=0, tiled=True)  9.94 us
    unnamed x282, local copies, waits for them, and re-layouts  9.01 us
    all_to_all x1, waiting for transfers between devices, spread_sum(): return jnp.sum(lax.all_to_all(copies, axis, 0, 0, tiled=True), axis=0)  8.88 us
    all_to_all x1, starting transfers between devices, spread_sum(): return jnp.sum(lax.all_to_all(copies, axis, 0, 0, tiled=True), axis=0)  8.18 us
    all_to_all x1, waiting for transfers between devices, scatter_sum(): return jnp.sum(lax.all_to_all(value, axis, 0, 0, tiled=True), axis=0)  5.25 us
    all_to_all x1, starting transfers between devices, gather_chan(): gathered = lax.all_to_all(copies, 'chan', 0, 0, tiled=True)  5.13 us
    reshape x10, local copies, waits for them, and re-layouts, per_device(): g.reshape(chan_count, -1)  4.6 us
  transfers between devices with their start and end apart: 3, of which 2 were waited for; matrix products, arithmetic and copies ran while one was open for 3% of the time, Pallas kernels for 0%

profile of v3, /device:TPU:1, one launch (start us, length us, event | category | flops | bytes accessed | tf_op | source)
XLA Modules:
  0.0 154.3 jit_solution(12636549183111093657)
XLA Ops:
  0.7 1.0 reshape.511
  2.9 0.9 broadcast_in_dim.221
  3.8 5.1 %all-to-all-start = ((f32[4,1,18576]{2,1,0:T(1,128)}), f32[4,1,18576]{2,1,0:T(1,128)S(1)}, u32[]{:S(2)}, u32[]{:S(2)}) async-start(f32[4,1,18576]{2,1,0:T(1,128)} %broadcast_in_dim.221), calls=%async_computation | async-start | bytes 598016 | tf_op jit(solution)/shard_map/all_to_all | solution.py:72
  10.5 9.9 %all-gather = f32[4,1,2424]{2,1,0:T(1,128)S(1)} all-gather(f32[1,1,2424]{2,1,0:T(1,128)S(1)} %bitcast.173), channel_id=1, replica_groups=mesh['dp'=2,'tx'=4,'tz'=8,'chan'=4] {'chan'}, dimensions={0}, use_global_device_ids=true | all-gather | bytes 48480 | tf_op jit(solution)/shard_map/all_gather | solution.py:74
  21.3 0.7 slice_reduce_fusion.47
  26.3 0.9 multiply_reduce_fusion.48
  28.3 1.3 fusion.3
  30.7 14.5 %all_to_all.46 = f32[16,64,98]{2,1,0:T(8,128)S(1)} all-to-all(f32[16,64,98]{2,1,0:T(8,128)S(1)} %broadcast_in_dim.226), channel_id=1, replica_groups=mesh['dp'=2,'tx'=4,'tz'=8,'chan'=4] {'chan','tx'}, dimensions={0} | all-to-all | bytes 802816 | tf_op jit(solution)/shard_map/all_to_all | solution.py:55
  45.3 0.7 broadcast_in_dim.227
  46.0 8.2 %all-to-all-start.2 = ((f32[8,64,98]{2,1,0:T(8,128)}), f32[8,64,98]{2,1,0:T(8,128)S(1)}, u32[]{:S(2)}, u32[]{:S(2)}) async-start(f32[8,64,98]{2,1,0:T(8,128)} %broadcast_in_dim.227), calls=%async_computation.2 | async-start | bytes 524288 | tf_op jit(solution)/shard_map/all_to_all | solution.py:55
  54.6 8.9 %all-to-all-done.2 = f32[8,64,98]{2,1,0:T(8,128)S(1)} async-done(((f32[8,64,98]{2,1,0:T(8,128)}), f32[8,64,98]{2,1,0:T(8,128)S(1)}, u32[]{:S(2)}, u32[]{:S(2)}) %all-to-all-start.2) | async-done | bytes 200736 | tf_op jit(solution)/shard_map/all_to_all | solution.py:55
  63.7 1.4 broadcast_multiply_fusion.52
  65.9 0.8 fusion.9
  66.7 1.2 fusion.57
  67.9 1.1 multiply_reduce_fusion.49
  69.1 0.8 fusion.11
  69.9 0.7 fusion.50
  70.7 0.8 multiply_reduce_fusion.45
  71.5 1.0 multiply_reduce_fusion.46
  72.5 0.9 multiply_reduce_fusion.47
  74.4 1.2 broadcast_multiply_fusion.1
  75.7 1.5 broadcast_multiply_fusion
  85.9 1.5 pad_add_fusion.7
  87.4 0.8 copy.146
  88.3 0.7 reshape.528
  89.1 3.2 %pad_add_fusion = f32[96,4,14,14]{0,3,2,1:T(8,128)S(1)} fusion(f32[96,4,8,8]{0,3,2,1:T(8,128)} %get-tuple-element.136, f32[96,4,8,8]{0,3,2,1:T(8,128)} %get-tuple-element.137, f32[96,4,8,8]{0,3,2,1:T(8,128)} %get-tuple-element.138, f32[96,4,8,8]{0,3,2,1:T(8,128)} %get-tuple-element.139, f32[96,4,8,8]{0,3,2,1:T(8,128)} %get-tuple-element.140, ...), kind=kLoop, calls=%fused_computation.58 | loop fusion | flops 3161088 | bytes 4528128 | tf_op jit(solution)/shard_map/transpose(jvp())/add_any | solution.py:26
  94.6 1.1 copy.149
  95.7 3.5 %all-to-all-start.3 = ((f32[4,1,21000]{2,1,0:T(1,128)}), f32[4,1,21000]{2,1,0:T(1,128)S(1)}, u32[]{:S(2)}, u32[]{:S(2)}) async-start(f32[4,1,21000]{2,1,0:T(1,128)} %copy.149), calls=%async_computation.3 | async-start | bytes 675840 | tf_op jit(solution)/shard_map/all_to_all | solution.py:65
  99.8 5.2 %all-to-all-done.3 = f32[4,1,21000]{2,1,0:T(1,128)S(1)} async-done(((f32[4,1,21000]{2,1,0:T(1,128)}), f32[4,1,21000]{2,1,0:T(1,128)S(1)}, u32[]{:S(2)}, u32[]{:S(2)}) %all-to-all-start.3) | async-done | bytes 336032 | tf_op jit(solution)/shard_map/all_to_all | solution.py:65
  105.6 11.5 %all_to_all.47 = f32[2,1,21001]{2,1,0:T(1,128)S(1)} all-to-all(f32[2,1,21001]{2,1,0:T(1,128)S(1)} %broadcast_in_dim.283), channel_id=1, replica_groups=mesh['dp'=2,'tx'=4,'tz'=8,'chan'=4] {'dp'}, dimensions={0} | all-to-all | bytes 336016 | tf_op jit(solution)/shard_map/all_to_all | solution.py:55
  117.5 9.3 %all_to_all.48 = f32[4,1,21001]{2,1,0:T(1,128)S(1)} all-to-all(f32[4,1,21001]{2,1,0:T(1,128)S(1)} %broadcast_in_dim.284), channel_id=1, replica_groups=mesh['dp'=2,'tx'=4,'tz'=8,'chan'=4] {'tx'}, dimensions={0} | all-to-all | bytes 672032 | tf_op jit(solution)/shard_map/all_to_all | solution.py:55
  127.5 21.6 %all_to_all.49 = f32[8,1,21001]{2,1,0:T(1,128)S(1)} all-to-all(f32[8,1,21001]{2,1,0:T(1,128)S(1)} %broadcast_in_dim.285), channel_id=1, replica_groups=mesh['dp'=2,'tx'=4,'tz'=8,'chan'=4] {'tz'}, dimensions={0} | all-to-all | bytes 1344064 | tf_op jit(solution)/shard_map/all_to_all | solution.py:55
  (374 shorter events, 28.5 us)
Async XLA Ops:
  0.6 25.0 %copy-start = (f32[48,1024]{1,0:T(8,128)S(1)}, f32[48,1024]{1,0:T(8,128)}, u32[]{:S(2)}) copy-start(f32[48,1024]{1,0:T(8,128)} %param.15) | copy-start | bytes 589828
  3.8 5.1 %copy-start.14 = (f32[24,48]{1,0:T(8,128)S(1)}, f32[24,48]{1,0:T(8,128)}, u32[]{:S(2)}) copy-start(f32[24,48]{1,0:T(8,128)} %param.18) | copy-start | bytes 13828
  3.8 23.7 %all-to-all-start = ((f32[4,1,18576]{2,1,0:T(1,128)}), f32[4,1,18576]{2,1,0:T(1,128)S(1)}, u32[]{:S(2)}, u32[]{:S(2)}) async-start(f32[4,1,18576]{2,1,0:T(1,128)} %broadcast_in_dim.221), calls=%async_computation | async-start | bytes 598016 | tf_op jit(solution)/shard_map/all_to_all | solution.py:72
  21.2 4.8 %copy-start.22 = (f32[96]{0:T(128)}, f32[96]{0:T(128)S(1)}, u32[]{:S(2)}) copy-start(f32[96]{0:T(128)S(1)} %get-tuple-element.110) | copy-start | bytes 1156
  21.2 4.8 %copy-start.24 = (f32[96]{0:T(128)}, f32[96]{0:T(128)S(1)}, u32[]{:S(2)}) copy-start(f32[96]{0:T(128)S(1)} %get-tuple-element.111) | copy-start | bytes 1156
  21.2 4.8 %copy-start.26 = (f32[96]{0:T(128)}, f32[96]{0:T(128)S(1)}, u32[]{:S(2)}) copy-start(f32[96]{0:T(128)S(1)} %get-tuple-element.112) | copy-start | bytes 1156
  21.2 4.8 %copy-start.28 = (f32[96]{0:T(128)}, f32[96]{0:T(128)S(1)}, u32[]{:S(2)}) copy-start(f32[96]{0:T(128)S(1)} %get-tuple-element.113) | copy-start | bytes 1156
  21.2 4.8 %copy-start.30 = (f32[96]{0:T(128)}, f32[96]{0:T(128)S(1)}, u32[]{:S(2)}) copy-start(f32[96]{0:T(128)S(1)} %get-tuple-element.114) | copy-start | bytes 1156
  21.2 4.8 %copy-start.32 = (f32[96]{0:T(128)}, f32[96]{0:T(128)S(1)}, u32[]{:S(2)}) copy-start(f32[96]{0:T(128)S(1)} %get-tuple-element.115) | copy-start | bytes 1156
  21.3 4.8 %copy-start.34 = (f32[96]{0:T(128)}, f32[96]{0:T(128)S(1)}, u32[]{:S(2)}) copy-start(f32[96]{0:T(128)S(1)} %get-tuple-element.116) | copy-start | bytes 1156
  22.0 4.1 %copy-start.36 = (f32[96]{0:T(128)}, f32[96]{0:T(128)S(1)}, u32[]{:S(2)}) copy-start(f32[96]{0:T(128)S(1)} %get-tuple-element.87) | copy-start | bytes 1156
  22.0 4.1 %copy-start.38 = (f32[96]{0:T(128)}, f32[96]{0:T(128)S(1)}, u32[]{:S(2)}) copy-start(f32[96]{0:T(128)S(1)} %get-tuple-element.102) | copy-start | bytes 1156
  22.0 4.1 %copy-start.40 = (f32[96]{0:T(128)}, f32[96]{0:T(128)S(1)}, u32[]{:S(2)}) copy-start(f32[96]{0:T(128)S(1)} %get-tuple-element.103) | copy-start | bytes 1156
  22.0 4.1 %copy-start.42 = (f32[96]{0:T(128)}, f32[96]{0:T(128)S(1)}, u32[]{:S(2)}) copy-start(f32[96]{0:T(128)S(1)} %get-tuple-element.104) | copy-start | bytes 1156
  22.0 4.1 %copy-start.44 = (f32[96]{0:T(128)}, f32[96]{0:T(128)S(1)}, u32[]{:S(2)}) copy-start(f32[96]{0:T(128)S(1)} %get-tuple-element.105) | copy-start | bytes 1156
  22.0 4.1 %copy-start.50 = (f32[96]{0:T(128)}, f32[96]{0:T(128)S(1)}, u32[]{:S(2)}) copy-start(f32[96]{0:T(128)S(1)} %get-tuple-element.88) | copy-start | bytes 1156
  22.0 4.1 %copy-start.52 = (f32[96]{0:T(128)}, f32[96]{0:T(128)S(1)}, u32[]{:S(2)}) copy-start(f32[96]{0:T(128)S(1)} %get-tuple-element.89) | copy-start | bytes 1156
  22.0 4.1 %copy-start.54 = (f32[96]{0:T(128)}, f32[96]{0:T(128)S(1)}, u32[]{:S(2)}) copy-start(f32[96]{0:T(128)S(1)} %get-tuple-element.90) | copy-start | bytes 1156
  22.0 4.1 %copy-start.56 = (f32[96]{0:T(128)}, f32[96]{0:T(128)S(1)}, u32[]{:S(2)}) copy-start(f32[96]{0:T(128)S(1)} %get-tuple-element.91) | copy-start | bytes 1156
  22.1 4.1 %copy-start.58 = (f32[96]{0:T(128)}, f32[96]{0:T(128)S(1)}, u32[]{:S(2)}) copy-start(f32[96]{0:T(128)S(1)} %get-tuple-element.92) | copy-start | bytes 1156
  22.1 4.1 %copy-start.60 = (f32[96]{0:T(128)}, f32[96]{0:T(128)S(1)}, u32[]{:S(2)}) copy-start(f32[96]{0:T(128)S(1)} %get-tuple-element.93) | copy-start | bytes 1156
  22.1 4.1 %copy-start.62 = (f32[96]{0:T(128)}, f32[96]{0:T(128)S(1)}, u32[]{:S(2)}) copy-start(f32[96]{0:T(128)S(1)} %get-tuple-element.94) | copy-start | bytes 1156
  22.1 4.1 %copy-start.64 = (f32[96]{0:T(128)}, f32[96]{0:T(128)S(1)}, u32[]{:S(2)}) copy-start(f32[96]{0:T(128)S(1)} %get-tuple-element.95) | copy-start | bytes 1156
  22.1 4.1 %copy-start.66 = (f32[96]{0:T(128)}, f32[96]{0:T(128)S(1)}, u32[]{:S(2)}) copy-start(f32[96]{0:T(128)S(1)} %get-tuple-element.96) | copy-start | bytes 1156
  22.1 4.1 %copy-start.68 = (f32[96]{0:T(128)}, f32[96]{0:T(128)S(1)}, u32[]{:S(2)}) copy-start(f32[96]{0:T(128)S(1)} %get-tuple-element.97) | copy-start | bytes 1156
  22.1 4.1 %copy-start.70 = (f32[96]{0:T(128)}, f32[96]{0:T(128)S(1)}, u32[]{:S(2)}) copy-start(f32[96]{0:T(128)S(1)} %get-tuple-element.98) | copy-start | bytes 1156
  22.1 4.1 %copy-start.72 = (f32[96]{0:T(128)}, f32[96]{0:T(128)S(1)}, u32[]{:S(2)}) copy-start(f32[96]{0:T(128)S(1)} %get-tuple-element.99) | copy-start | bytes 1156
  22.1 4.1 %copy-start.74 = (f32[96]{0:T(128)}, f32[96]{0:T(128)S(1)}, u32[]{:S(2)}) copy-start(f32[96]{0:T(128)S(1)} %get-tuple-element.100) | copy-start | bytes 1156
  22.1 4.1 %copy-start.76 = (f32[96]{0:T(128)}, f32[96]{0:T(128)S(1)}, u32[]{:S(2)}) copy-start(f32[96]{0:T(128)S(1)} %get-tuple-element.101) | copy-start | bytes 1156
  46.0 17.5 %all-to-all-start.2 = ((f32[8,64,98]{2,1,0:T(8,128)}), f32[8,64,98]{2,1,0:T(8,128)S(1)}, u32[]{:S(2)}, u32[]{:S(2)}) async-start(f32[8,64,98]{2,1,0:T(8,128)} %broadcast_in_dim.227), calls=%async_computation.2 | async-start | bytes 524288 | tf_op jit(solution)/shard_map/all_to_all | solution.py:55
  85.3 3.7 %copy-start.3 = (f32[96,4,8,8]{0,3,2,1:T(8,128)S(1)}, f32[96,4,8,8]{0,3,2,1:T(8,128)}, u32[]{:S(2)}) copy-start(f32[96,4,8,8]{0,3,2,1:T(8,128)} %get-tuple-element.153) | copy-start | bytes 294916
  95.7 9.4 %all-to-all-start.3 = ((f32[4,1,21000]{2,1,0:T(1,128)}), f32[4,1,21000]{2,1,0:T(1,128)S(1)}, u32[]{:S(2)}, u32[]{:S(2)}) async-start(f32[4,1,21000]{2,1,0:T(1,128)} %copy.149), calls=%async_computation.3 | async-start | bytes 675840 | tf_op jit(solution)/shard_map/all_to_all | solution.py:65
  (111 other events, 122.3 us)

commit v4 on v3

--- a/solution.py
+++ b/solution.py
@@ -123,9 +123,7 @@
         b_down,
         w_head,
     )
-    full = gather_chan(shards[:6], chan_count, spread=False) + gather_chan(
-        shards[6:], chan_count, spread=True
-    )
+    full = gather_chan(shards, chan_count, spread=True)
     params = tuple(full[:10])
     head = full[10]
 
@@ -169,9 +167,13 @@
     flat = jnp.concatenate(
         [g.reshape(chan_count, -1) for g in grads] + [g_head.reshape(chan_count, -1)], axis=1
     )
-    mine = scatter_sum(flat, "chan")
-    mine = jnp.concatenate([mine, jnp.where(lead, loss_part, 0.0)[None]])
-    mine = psum_steps(mine, ("dp", "tx", "tz"))
+    dp_count = lax.psum(1, "dp")
+    flat = jnp.concatenate(
+        [flat, jnp.where(lead & (chan == 0), loss_part, 0.0) * jnp.ones((chan_count, 1))], axis=1
+    )
+    flat = jnp.broadcast_to(flat[None], (dp_count,) + flat.shape).reshape(-1, flat.shape[1])
+    mine = scatter_sum(flat, ("dp", "chan"))
+    mine = psum_steps(mine, ("tx", "tz"))
 
     outs = []
     offset = 0

time: 155 us -> 146 us (0.942)
  blocking collectives: 66.9 us -> 63.1 us
  starting transfers between devices: 16.8 us -> 13.2 us
    all_to_all x0 -> x1, blocking collectives: none -> 17.9 us  [scatter_sum(): return jnp.sum(lax.all_to_all(value, axis, 0, 0, tiled=True), axis=0)]
    all_to_all x4 -> x3, blocking collectives: 57 us -> 45.3 us  [spread_sum(): return jnp.sum(lax.all_to_all(copies, axis, 0, 0, tiled=True), axis=0)]
    all_gather x1 -> x0, blocking collectives: 9.94 us -> none  [gather_chan(): gathered = lax.all_gather(packed, 'chan', axis=0, tiled=True)]
    all_to_all x1 -> x0, waiting for transfers between devices: 5.25 us -> none  [scatter_sum(): return jnp.sum(lax.all_to_all(value, axis, 0, 0, tiled=True), axis=0)]
    all_to_all x1, waiting for transfers between devices: 0.01 us -> 4.19 us  [gather_chan(): gathered = lax.all_to_all(copies, 'chan', 0, 0, tiled=True)]
    all_to_all x1 -> x0, starting transfers between devices: 3.45 us -> none  [scatter_sum(): return jnp.sum(lax.all_to_all(value, axis, 0, 0, tiled=True), axis=0)]
    unnamed x282 -> x279, local copies, waits for them, and re-layouts: 9.01 us -> 7.63 us
  transfers between devices with their start and end apart: 3 -> 2, of which waited for: 2 -> 2; matrix products, arithmetic and copies ran while one was open for 3% -> 1% of each run, Pallas kernels for 0% -> 0%
where the time goes in v4:
time: 146 us; the launch traced here: 145 us
  blocking collectives  63.1 us (43%)
  local copies, waits for them, and re-layouts  28.4 us (19%)
  other arithmetic  14.8 us (10%)
  starting transfers between devices  13.2 us (9%)
  waiting for transfers between devices  13.2 us (9%)
  matrix products  8.51 us (6%)
  between operations  3.86 us (3%)
    all_to_all x3, blocking collectives, spread_sum(): return jnp.sum(lax.all_to_all(copies, axis, 0, 0, tiled=True), axis=0)  45.3 us
    all_to_all x1, blocking collectives, scatter_sum(): return jnp.sum(lax.all_to_all(value, axis, 0, 0, tiled=True), axis=0)  17.9 us
    all_to_all x1, waiting for transfers between devices, spread_sum(): return jnp.sum(lax.all_to_all(copies, axis, 0, 0, tiled=True), axis=0)  8.98 us
    all_to_all x1, starting transfers between devices, spread_sum(): return jnp.sum(lax.all_to_all(copies, axis, 0, 0, tiled=True), axis=0)  8.18 us
    unnamed x279, local copies, waits for them, and re-layouts  7.63 us
    all_to_all x1, starting transfers between devices, gather_chan(): gathered = lax.all_to_all(copies, 'chan', 0, 0, tiled=True)  5 us
    reshape x10, local copies, waits for them, and re-layouts, per_device(): g.reshape(chan_count, -1)  4.59 us
    all_to_all x1, waiting for transfers between devices, gather_chan(): gathered = lax.all_to_all(copies, 'chan', 0, 0, tiled=True)  4.19 us
  transfers between devices with their start and end apart: 2, of which 2 were waited for; matrix products, arithmetic and copies ran while one was open for 1% of the time, Pallas kernels for 0%

profile of v4, /device:TPU:1, one launch (start us, length us, event | category | flops | bytes accessed | tf_op | source)
XLA Modules:
  0.0 145.1 jit_solution(17263321501595938242)
XLA Ops:
  0.7 0.8 reshape.501
  1.6 0.9 reshape.507
  4.0 0.9 broadcast_in_dim.218
  4.9 5.0 %all-to-all-start = ((f32[4,1,21000]{2,1,0:T(1,128)}), f32[4,1,21000]{2,1,0:T(1,128)S(1)}, u32[]{:S(2)}, u32[]{:S(2)}) async-start(f32[4,1,21000]{2,1,0:T(1,128)} %broadcast_in_dim.218), calls=%async_computation | async-start | bytes 675840 | tf_op jit(solution)/shard_map/all_to_all | solution.py:72
  11.6 4.2 %all-to-all-done = f32[4,1,21000]{2,1,0:T(1,128)S(1)} async-done(((f32[4,1,21000]{2,1,0:T(1,128)}), f32[4,1,21000]{2,1,0:T(1,128)S(1)}, u32[]{:S(2)}, u32[]{:S(2)}) %all-to-all-start) | async-done | bytes 336032 | tf_op jit(solution)/shard_map/all_to_all | solution.py:72
  17.0 0.7 slice_reduce_fusion.47
  20.2 0.9 multiply_reduce_fusion.48
  21.3 1.3 fusion.3
  23.8 14.2 %all_to_all.40 = f32[16,64,98]{2,1,0:T(8,128)S(1)} all-to-all(f32[16,64,98]{2,1,0:T(8,128)S(1)} %broadcast_in_dim.223), channel_id=1, replica_groups=mesh['dp'=2,'tx'=4,'tz'=8,'chan'=4] {'chan','tx'}, dimensions={0} | all-to-all | bytes 802816 | tf_op jit(solution)/shard_map/all_to_all | solution.py:55
  38.0 0.7 broadcast_in_dim.224
  38.8 8.2 %all-to-all-start.2 = ((f32[8,64,98]{2,1,0:T(8,128)}), f32[8,64,98]{2,1,0:T(8,128)S(1)}, u32[]{:S(2)}, u32[]{:S(2)}) async-start(f32[8,64,98]{2,1,0:T(8,128)} %broadcast_in_dim.224), calls=%async_computation.2 | async-start | bytes 524288 | tf_op jit(solution)/shard_map/all_to_all | solution.py:55
  47.4 9.0 %all-to-all-done.2 = f32[8,64,98]{2,1,0:T(8,128)S(1)} async-done(((f32[8,64,98]{2,1,0:T(8,128)}), f32[8,64,98]{2,1,0:T(8,128)S(1)}, u32[]{:S(2)}, u32[]{:S(2)}) %all-to-all-start.2) | async-done | bytes 200736 | tf_op jit(solution)/shard_map/all_to_all | solution.py:55
  56.6 1.4 multiply_reduce_fusion.53
  58.8 0.8 fusion.9
  59.6 1.2 fusion.56
  60.8 1.1 multiply_reduce_fusion.49
  62.0 0.8 fusion.11
  62.8 0.7 fusion.50
  63.6 0.8 multiply_reduce_fusion.45
  64.4 1.0 multiply_reduce_fusion.46
  65.4 0.9 multiply_reduce_fusion.47
  67.3 1.2 broadcast_multiply_fusion.1
  68.6 1.5 %broadcast_multiply_fusion = (f32[96,4,8,8]{0,3,2,1:T(8,128)}, f32[96,4,8,8]{0,3,2,1:T(8,128)}, f32[96,4,8,8]{0,3,2,1:T(8,128)}, f32[96,4,8,8]{0,3,2,1:T(8,128)}...) fusion(f32[96,4,8,8]{0,3,2,1:T(8,128)S(1)} %bitcast.151, ...), kind=kLoop, calls=%fused_computation.149 | loop fusion | flops 442368 | bytes 1874688 | tf_op jit(solution)/shard_map/transpose(jvp())/mul | solution.py:25
  79.9 1.5 %pad_add_fusion.7 = f32[96,49]{0,1:T(8,128)} fusion(f32[96,1]{0,1:T(1,128)S(1)} %bitcast.177, f32[96,1]{0,1:T(1,128)S(1)} %bitcast.197, f32[96,1]{0,1:T(1,128)S(1)} %bitcast.198, f32[96,1]{0,1:T(1,128)S(1)} %bitcast.199, f32[96,1]{0,1:T(1,128)S(1)} %bitcast.200, f32[96,1]{0,1:T(1,128)S(1)} %bitcast.201, f32[96,1]{0,1:T(1,128)} %bitcast.202, ...), kind=kLoop, calls=%fused_computation.261 | loop fusion | flops 225792 | bytes 37632 | tf_op jit(solution)/shard_map/transpose(jvp())/add_any | solution.py:22
  81.4 0.8 copy.143
  82.3 0.7 reshape.525
  83.0 3.2 %pad_add_fusion = f32[96,4,14,14]{0,3,2,1:T(8,128)S(1)} fusion(f32[96,4,8,8]{0,3,2,1:T(8,128)} %get-tuple-element.140, f32[96,4,8,8]{0,3,2,1:T(8,128)} %get-tuple-element.141, f32[96,4,8,8]{0,3,2,1:T(8,128)} %get-tuple-element.142, f32[96,4,8,8]{0,3,2,1:T(8,128)} %get-tuple-element.143, f32[96,4,8,8]{0,3,2,1:T(8,128)} %get-tuple-element.144, ...), kind=kLoop, calls=%fused_computation.58 | loop fusion | flops 3161088 | bytes 4528128 | tf_op jit(solution)/shard_map/transpose(jvp())/add_any | solution.py:26
  88.8 0.8 all_to_all.30
  89.6 17.9 %all_to_all.41 = f32[8,1,21001]{2,1,0:T(1,128)S(1)} all-to-all(f32[8,1,21001]{2,1,0:T(1,128)S(1)} %all_to_all.30), channel_id=1, replica_groups=mesh['dp'=2,'tx'=4,'tz'=8,'chan'=4] {'dp','chan'}, dimensions={0} | all-to-all | bytes 1344064 | tf_op jit(solution)/shard_map/all_to_all | solution.py:65
  108.1 9.3 %all_to_all.42 = f32[4,1,21001]{2,1,0:T(1,128)S(1)} all-to-all(f32[4,1,21001]{2,1,0:T(1,128)S(1)} %broadcast_in_dim.280), channel_id=1, replica_groups=mesh['dp'=2,'tx'=4,'tz'=8,'chan'=4] {'tx'}, dimensions={0} | all-to-all | bytes 672032 | tf_op jit(solution)/shard_map/all_to_all | solution.py:55
  118.2 21.7 %all_to_all.43 = f32[8,1,21001]{2,1,0:T(1,128)S(1)} all-to-all(f32[8,1,21001]{2,1,0:T(1,128)S(1)} %broadcast_in_dim.281), channel_id=1, replica_groups=mesh['dp'=2,'tx'=4,'tz'=8,'chan'=4] {'tz'}, dimensions={0} | all-to-all | bytes 1344064 | tf_op jit(solution)/shard_map/all_to_all | solution.py:55
  143.7 0.7 reshape.537
  (365 shorter events, 26.3 us)
Async XLA Ops:
  0.6 18.8 %copy-start = (f32[48,1024]{1,0:T(8,128)S(1)}, f32[48,1024]{1,0:T(8,128)}, u32[]{:S(2)}) copy-start(f32[48,1024]{1,0:T(8,128)} %param.15) | copy-start | bytes 589828
  4.9 10.9 %all-to-all-start = ((f32[4,1,21000]{2,1,0:T(1,128)}), f32[4,1,21000]{2,1,0:T(1,128)S(1)}, u32[]{:S(2)}, u32[]{:S(2)}) async-start(f32[4,1,21000]{2,1,0:T(1,128)} %broadcast_in_dim.218), calls=%async_computation | async-start | bytes 675840 | tf_op jit(solution)/shard_map/all_to_all | solution.py:72
  16.9 3.0 %copy-start.21 = (f32[96]{0:T(128)}, f32[96]{0:T(128)S(1)}, u32[]{:S(2)}) copy-start(f32[96]{0:T(128)S(1)} %get-tuple-element.110) | copy-start | bytes 1156
  16.9 3.0 %copy-start.23 = (f32[96]{0:T(128)}, f32[96]{0:T(128)S(1)}, u32[]{:S(2)}) copy-start(f32[96]{0:T(128)S(1)} %get-tuple-element.111) | copy-start | bytes 1156
  16.9 3.0 %copy-start.25 = (f32[96]{0:T(128)}, f32[96]{0:T(128)S(1)}, u32[]{:S(2)}) copy-start(f32[96]{0:T(128)S(1)} %get-tuple-element.112) | copy-start | bytes 1156
  17.0 3.0 %copy-start.27 = (f32[96]{0:T(128)}, f32[96]{0:T(128)S(1)}, u32[]{:S(2)}) copy-start(f32[96]{0:T(128)S(1)} %get-tuple-element.113) | copy-start | bytes 1156
  17.0 3.0 %copy-start.29 = (f32[96]{0:T(128)}, f32[96]{0:T(128)S(1)}, u32[]{:S(2)}) copy-start(f32[96]{0:T(128)S(1)} %get-tuple-element.114) | copy-start | bytes 1156
  17.0 3.0 %copy-start.31 = (f32[96]{0:T(128)}, f32[96]{0:T(128)S(1)}, u32[]{:S(2)}) copy-start(f32[96]{0:T(128)S(1)} %get-tuple-element.115) | copy-start | bytes 1156
  17.0 3.0 %copy-start.33 = (f32[96]{0:T(128)}, f32[96]{0:T(128)S(1)}, u32[]{:S(2)}) copy-start(f32[96]{0:T(128)S(1)} %get-tuple-element.116) | copy-start | bytes 1156
  17.7 2.3 %copy-start.37 = (f32[96]{0:T(128)}, f32[96]{0:T(128)S(1)}, u32[]{:S(2)}) copy-start(f32[96]{0:T(128)S(1)} %get-tuple-element.102) | copy-start | bytes 1156
  17.7 2.3 %copy-start.39 = (f32[96]{0:T(128)}, f32[96]{0:T(128)S(1)}, u32[]{:S(2)}) copy-start(f32[96]{0:T(128)S(1)} %get-tuple-element.103) | copy-start | bytes 1156
  17.7 2.3 %copy-start.41 = (f32[96]{0:T(128)}, f32[96]{0:T(128)S(1)}, u32[]{:S(2)}) copy-start(f32[96]{0:T(128)S(1)} %get-tuple-element.104) | copy-start | bytes 1156
  17.7 2.3 %copy-start.43 = (f32[96]{0:T(128)}, f32[96]{0:T(128)S(1)}, u32[]{:S(2)}) copy-start(f32[96]{0:T(128)S(1)} %get-tuple-element.105) | copy-start | bytes 1156
  17.7 2.3 %copy-start.49 = (f32[96]{0:T(128)}, f32[96]{0:T(128)S(1)}, u32[]{:S(2)}) copy-start(f32[96]{0:T(128)S(1)} %get-tuple-element.88) | copy-start | bytes 1156
  17.8 2.3 %copy-start.51 = (f32[96]{0:T(128)}, f32[96]{0:T(128)S(1)}, u32[]{:S(2)}) copy-start(f32[96]{0:T(128)S(1)} %get-tuple-element.89) | copy-start | bytes 1156
  17.8 2.3 %copy-start.53 = (f32[96]{0:T(128)}, f32[96]{0:T(128)S(1)}, u32[]{:S(2)}) copy-start(f32[96]{0:T(128)S(1)} %get-tuple-element.90) | copy-start | bytes 1156
  17.8 2.3 %copy-start.55 = (f32[96]{0:T(128)}, f32[96]{0:T(128)S(1)}, u32[]{:S(2)}) copy-start(f32[96]{0:T(128)S(1)} %get-tuple-element.91) | copy-start | bytes 1156
  17.8 2.3 %copy-start.57 = (f32[96]{0:T(128)}, f32[96]{0:T(128)S(1)}, u32[]{:S(2)}) copy-start(f32[96]{0:T(128)S(1)} %get-tuple-element.92) | copy-start | bytes 1156
  17.8 2.3 %copy-start.59 = (f32[96]{0:T(128)}, f32[96]{0:T(128)S(1)}, u32[]{:S(2)}) copy-start(f32[96]{0:T(128)S(1)} %get-tuple-element.93) | copy-start | bytes 1156
  17.8 2.3 %copy-start.61 = (f32[96]{0:T(128)}, f32[96]{0:T(128)S(1)}, u32[]{:S(2)}) copy-start(f32[96]{0:T(128)S(1)} %get-tuple-element.94) | copy-start | bytes 1156
  17.8 2.3 %copy-start.63 = (f32[96]{0:T(128)}, f32[96]{0:T(128)S(1)}, u32[]{:S(2)}) copy-start(f32[96]{0:T(128)S(1)} %get-tuple-element.95) | copy-start | bytes 1156
  17.8 2.3 %copy-start.65 = (f32[96]{0:T(128)}, f32[96]{0:T(128)S(1)}, u32[]{:S(2)}) copy-start(f32[96]{0:T(128)S(1)} %get-tuple-element.96) | copy-start | bytes 1156
  38.8 17.6 %all-to-all-start.2 = ((f32[8,64,98]{2,1,0:T(8,128)}), f32[8,64,98]{2,1,0:T(8,128)S(1)}, u32[]{:S(2)}, u32[]{:S(2)}) async-start(f32[8,64,98]{2,1,0:T(8,128)} %broadcast_in_dim.224), calls=%async_computation.2 | async-start | bytes 524288 | tf_op jit(solution)/shard_map/all_to_all | solution.py:55
  79.3 3.7 %copy-start.3 = (f32[96,4,8,8]{0,3,2,1:T(8,128)S(1)}, f32[96,4,8,8]{0,3,2,1:T(8,128)}, u32[]{:S(2)}) copy-start(f32[96,4,8,8]{0,3,2,1:T(8,128)} %get-tuple-element.159) | copy-start | bytes 294916
  79.9 3.1 %copy-start.1 = (f32[96,4,8,8]{0,3,2,1:T(8,128)S(1)}, f32[96,4,8,8]{0,3,2,1:T(8,128)}, u32[]{:S(2)}) copy-start(f32[96,4,8,8]{0,3,2,1:T(8,128)} %get-tuple-element.157) | copy-start | bytes 294916
  79.9 3.1 %copy-start.2 = (f32[96,4,8,8]{0,3,2,1:T(8,128)S(1)}, f32[96,4,8,8]{0,3,2,1:T(8,128)}, u32[]{:S(2)}) copy-start(f32[96,4,8,8]{0,3,2,1:T(8,128)} %get-tuple-element.158) | copy-start | bytes 294916
  83.0 3.2 %copy-start.4 = (f32[96,4,8,8]{0,3,2,1:T(8,128)S(1)}, f32[96,4,8,8]{0,3,2,1:T(8,128)}, u32[]{:S(2)}) copy-start(f32[96,4,8,8]{0,3,2,1:T(8,128)} %get-tuple-element.134) | copy-start | bytes 294916
  83.0 3.2 %copy-start.5 = (f32[96,4,8,8]{0,3,2,1:T(8,128)S(1)}, f32[96,4,8,8]{0,3,2,1:T(8,128)}, u32[]{:S(2)}) copy-start(f32[96,4,8,8]{0,3,2,1:T(8,128)} %get-tuple-element.135) | copy-start | bytes 294916
  83.0 3.2 %copy-start.6 = (f32[96,4,8,8]{0,3,2,1:T(8,128)S(1)}, f32[96,4,8,8]{0,3,2,1:T(8,128)}, u32[]{:S(2)}) copy-start(f32[96,4,8,8]{0,3,2,1:T(8,128)} %get-tuple-element.136) | copy-start | bytes 294916
  83.0 3.2 %copy-start.7 = (f32[96,4,8,8]{0,3,2,1:T(8,128)S(1)}, f32[96,4,8,8]{0,3,2,1:T(8,128)}, u32[]{:S(2)}) copy-start(f32[96,4,8,8]{0,3,2,1:T(8,128)} %get-tuple-element.137) | copy-start | bytes 294916
  83.0 3.2 %copy-start.8 = (f32[96,4,8,8]{0,3,2,1:T(8,128)S(1)}, f32[96,4,8,8]{0,3,2,1:T(8,128)}, u32[]{:S(2)}) copy-start(f32[96,4,8,8]{0,3,2,1:T(8,128)} %get-tuple-element.138) | copy-start | bytes 294916
  83.0 3.2 %copy-start.9 = (f32[96,4,8,8]{0,3,2,1:T(8,128)S(1)}, f32[96,4,8,8]{0,3,2,1:T(8,128)}, u32[]{:S(2)}) copy-start(f32[96,4,8,8]{0,3,2,1:T(8,128)} %get-tuple-element.139) | copy-start | bytes 294916
  (109 other events, 98.9 us)

commit v5 on v2

--- a/solution.py
+++ b/solution.py
@@ -7,6 +7,7 @@
 
 SIDE = 8
 X_SPAN = 4
+LANES = 128
 
 
 epsilon = 1e-06
@@ -50,7 +51,7 @@
 
 
 def spread_sum(value, axis):
-    count = lax.axis_size(axis)
+    count = lax.psum(1, axis)
     copies = jnp.broadcast_to(value[None], (count,) + value.shape)
     return jnp.sum(lax.all_to_all(copies, axis, 0, 0, tiled=True), axis=0)
 
@@ -63,6 +64,24 @@
 
 def scatter_sum(value, axis):
     return jnp.sum(lax.all_to_all(value, axis, 0, 0, tiled=True), axis=0)
+
+
+def pack(mats, vecs):
+    blocks = [jnp.pad(m, ((0, 0), (0, 0), (0, LANES - m.shape[2]))) for m in mats]
+    rows = jnp.stack([jnp.pad(v, ((0, 0), (0, LANES - v.shape[1]))) for v in vecs], axis=1)
+    extra = (-rows.shape[1]) % 8
+    rows = jnp.pad(rows, ((0, 0), (0, extra), (0, 0)))
+    return jnp.concatenate(blocks + [rows], axis=1)
+
+
+def unpack(block, mat_shapes, vec_sizes):
+    mats = []
+    offset = 0
+    for r, m in mat_shapes:
+        mats.append(block[..., offset : offset + r, :m])
+        offset += r
+    vecs = [block[..., offset + i, :n] for i, n in enumerate(vec_sizes)]
+    return mats, vecs
 
 
 def per_device(
@@ -92,29 +111,29 @@
     group_slides = slide_dev * lax.axis_size("tx") * lax.axis_size("tz")
     all_slides = group_slides * lax.axis_size("dp")
 
-    shards = (
-        w_patch,
-        b_patch,
-        dw_kernel,
-        dw_bias,
-        layernorm_gain,
-        layernorm_bias,
-        w_up,
-        b_up,
-        w_down,
-        b_down,
-        w_head,
-    )
-    sizes = [s.size for s in shards]
-    packed = jnp.concatenate([s.reshape(1, -1) for s in shards], axis=1)
-    gathered = lax.all_gather(packed, "chan", axis=0, tiled=True)
-    full = []
-    offset = 0
-    for s, n in zip(shards, sizes):
-        full.append(gathered[:, offset : offset + n].reshape((chan_count * s.shape[0],) + s.shape[1:]))
-        offset += n
-    params = tuple(full[:10])
-    head = full[10]
+    mats = (w_patch, dw_kernel, w_up, w_down)
+    vecs = (b_patch, dw_bias, layernorm_gain, layernorm_bias, b_up, b_down, w_head)
+    mat_shapes = [m.shape for m in mats]
+    vec_sizes = [v.shape[0] for v in vecs]
+    packed = pack([m[None] for m in mats], [v[None] for v in vecs])
+    copies = jnp.broadcast_to(packed, (chan_count,) + packed.shape[1:])
+    gathered = lax.all_to_all(copies, "chan", 0, 0, tiled=True)
+    full_mats, full_vecs = unpack(gathered, mat_shapes, vec_sizes)
+    full_mats = [m.reshape(chan_count * r, c) for m, (r, c) in zip(full_mats, mat_shapes)]
+    full_vecs = [v.reshape(-1) for v in full_vecs]
+    params = (
+        full_mats[0],
+        full_vecs[0],
+        full_mats[1],
+        full_vecs[1],
+        full_vecs[2],
+        full_vecs[3],
+        full_mats[2],
+        full_vecs[4],
+        full_mats[3],
+        full_vecs[5],
+    )
+    head = full_vecs[6]
 
     my_pixels = lax.dynamic_slice_in_dim(pixels, chan * slots * area, slots * area, axis=1)
     my_slide = lax.dynamic_slice_in_dim(tile_slide, chan * slots, slots)
@@ -135,7 +154,7 @@
     slide_pack = jnp.concatenate(
         [slide_part, jnp.sum(onehot, axis=0)[:, None], placed[:, None]], axis=1
     )
-    slide_pack = psum_steps(slide_pack, ("chan", "tx", "tz"))
+    slide_pack = psum_steps(slide_pack, (("chan", "tx"), "tz"))
     width = slide_part.shape[1]
     sums = slide_pack[:, :width]
     counts = jnp.maximum(slide_pack[:, width], 1.0)
@@ -151,22 +170,34 @@
     d_pooled = jnp.dot(onehot, d_sums, precision=highest).T
     grads = pull(d_pooled)[0]
 
-    lead = tile == 0
-    g_head = jnp.where(lead & (chan == 0), g_head, 0.0)
-    flat = jnp.concatenate(
-        [g.reshape(chan_count, -1) for g in grads] + [g_head.reshape(chan_count, -1)], axis=1
-    )
-    mine = scatter_sum(flat, "chan")
-    mine = jnp.concatenate([mine, jnp.where(lead, loss_part, 0.0)[None]])
-    mine = psum_steps(mine, ("dp", "tx", "tz"))
-
-    outs = []
-    offset = 0
-    for s in shards[:10] + shards[10:]:
-        n = s.size
-        outs.append(mine[offset : offset + n].reshape(s.shape))
-        offset += n
-    outs.append(mine[offset])
+    lead = (tile == 0) & (chan == 0)
+    g_patch, g_bpatch, g_kernel, g_dwbias, g_gain, g_shift, g_up, g_bup, g_down, g_bdown = grads
+    g_mats = [g.reshape(chan_count, -1, g.shape[1]) for g in (g_patch, g_kernel, g_up, g_down)]
+    g_vecs = [
+        g.reshape(chan_count, -1)
+        for g in (g_bpatch, g_dwbias, g_gain, g_shift, g_bup, g_bdown, jnp.where(lead, g_head, 0.0))
+    ]
+    g_vecs.append(jnp.broadcast_to(jnp.where(lead, loss_part, 0.0), (chan_count, 1)))
+    flat = pack(g_mats, g_vecs)
+    dp_count = lax.psum(1, "dp")
+    flat = jnp.broadcast_to(flat[None], (dp_count,) + flat.shape).reshape((-1,) + flat.shape[1:])
+    mine = scatter_sum(flat, ("dp", "chan"))
+    mine = psum_steps(mine, ("tx", "tz"))
+    out_mats, out_vecs = unpack(mine, mat_shapes, vec_sizes + [1])
+    outs = [
+        out_mats[0],
+        out_vecs[0],
+        out_mats[1],
+        out_vecs[1],
+        out_vecs[2],
+        out_vecs[3],
+        out_mats[2],
+        out_vecs[4],
+        out_mats[3],
+        out_vecs[5],
+        out_vecs[6],
+        out_vecs[7][0],
+    ]
     return tuple(outs)
 
 

time: 153 us -> 161 us (1.052)
  blocking collectives: 71.3 us -> 76.2 us
    all_to_all x0 -> x1, blocking collectives: none -> 21.5 us  [scatter_sum(): return jnp.sum(lax.all_to_all(value, axis, 0, 0, tiled=True), axis=0)]
    all_gather x1 -> x0, blocking collectives: 11.7 us -> none  [per_device(): gathered = lax.all_gather(packed, 'chan', axis=0, tiled=True)]
    all_to_all x5 -> x3, blocking collectives: 59.6 us -> 54.7 us  [spread_sum(): return jnp.sum(lax.all_to_all(copies, axis, 0, 0, tiled=True), axis=0)]
    unnamed x279 -> x315, local copies, waits for them, and re-layouts: 7.74 us -> 12.6 us
    reshape x15 -> x3, local copies, waits for them, and re-layouts: 6.07 us -> 1.25 us  [the longest x1 0.8 us: block_pooled(): return jnp.mean(features.reshape(width, tile_num, SIDE * SIDE), axis=2)]
    reshape x10 -> x7, local copies, waits for them, and re-layouts: 4.6 us -> 0.58 us  [per_device(): g.reshape(chan_count, -1)]
    pad x0 -> x12, local copies, waits for them, and re-layouts: none -> 2.99 us  [the longest x8 2.32 us: pack(): jnp.pad(v, ((0, 0), (0, LANES - v.shape[1])))]
    another operation x0 -> x8, local copies, waits for them, and re-layouts: none -> 2.22 us  [the longest x6 2.06 us: pack(): jnp.stack([jnp.pad(v, ((0, 0), (0, LANES - v.shape[1]))) for v in vecs],...]
  transfers between devices with their start and end apart: 2 -> 2, of which waited for: 2 -> 2; matrix products, arithmetic and copies ran while one was open for 0% -> 1% of each run, Pallas kernels for 0% -> 0%
where the time goes in v5:
time: 161 us; the launch traced here: 159 us
  blocking collectives  76.2 us (47%)
  local copies, waits for them, and re-layouts  28.9 us (18%)
  other arithmetic  14.3 us (9%)
  waiting for transfers between devices  14.1 us (9%)
  starting transfers between devices  13.2 us (8%)
  matrix products  8.53 us (5%)
  between operations  4 us (2%)
    all_to_all x3, blocking collectives, spread_sum(): return jnp.sum(lax.all_to_all(copies, axis, 0, 0, tiled=True), axis=0)  54.7 us
    all_to_all x1, blocking collectives, scatter_sum(): return jnp.sum(lax.all_to_all(value, axis, 0, 0, tiled=True), axis=0)  21.5 us
    unnamed x315, local copies, waits for them, and re-layouts  12.6 us
    all_to_all x1, waiting for transfers between devices, spread_sum(): return jnp.sum(lax.all_to_all(copies, axis, 0, 0, tiled=True), axis=0)  8.98 us
    all_to_all x1, starting transfers between devices, spread_sum(): return jnp.sum(lax.all_to_all(copies, axis, 0, 0, tiled=True), axis=0)  8.18 us
    all_to_all x1, waiting for transfers between devices, per_device(): gathered = lax.all_to_all(copies, 'chan', 0, 0, tiled=True)  5.12 us
    all_to_all x1, starting transfers between devices, per_device(): gathered = lax.all_to_all(copies, 'chan', 0, 0, tiled=True)  5 us
    dot_general x3, matrix products, block_pooled(): pre_act = jnp.dot(w_up, normed, precision=highest) + b_up[:, None]  3.73 us
  transfers between devices with their start and end apart: 2, of which 2 were waited for; matrix products, arithmetic and copies ran while one was open for 1% of the time, Pallas kernels for 0%

profile of v5, /device:TPU:1, one launch (start us, length us, event | category | flops | bytes accessed | tf_op | source)
XLA Modules:
  0.0 159.2 jit_solution(16649658156724391568)
XLA Ops:
  1.4 0.7 pad_dynamic-update-slice_fusion.3
  4.1 0.7 pad_dynamic-update-slice_fusion.2
  4.8 0.8 copy-done.20
  5.6 0.8 broadcast_in_dim.268
  6.5 5.0 %all-to-all-start = ((f32[4,248,128]{2,1,0:T(8,128)}), f32[4,248,128]{2,1,0:T(8,128)S(1)}, u32[]{:S(2)}, u32[]{:S(2)}) async-start(f32[4,248,128]{2,1,0:T(8,128)} %broadcast_in_dim.268), calls=%async_computation | async-start | bytes 1015808 | tf_op jit(solution)/shard_map/all_to_all | solution.py:120
  13.8 5.1 %all-to-all-done = f32[4,248,128]{2,1,0:T(8,128)S(1)} async-done(((f32[4,248,128]{2,1,0:T(8,128)}), f32[4,248,128]{2,1,0:T(8,128)S(1)}, u32[]{:S(2)}, u32[]{:S(2)}) %all-to-all-start) | async-done | bytes 507936 | tf_op jit(solution)/shard_map/all_to_all | solution.py:120
  19.4 0.7 slice_reduce_fusion.47
  20.3 1.2 slice_reduce_fusion.48
  22.9 1.6 %multiply_reduce_fusion.48 = (f32[4,8,8]{2,1,0:T(8,128)S(1)}, f32[4,8,8]{2,1,0:T(8,128)S(1)}, f32[96,4,8,8]{0,3,2,1:T(8,128)S(1)}) fusion(f32[96]{0:T(128)S(1)} %add.539, f32[96]{0:T(128)S(1)} %get-tuple-element.75, f32[96]{0:T(128)S(1)} %get-tuple-element.76, f32[96]{0:T(128)S(1)} %get-tuple-element.77, f32[96]{0:T(128)S(1)} %get-tuple-element.78, ...), kind=kLoop, calls=%fused_computation.133 | loop fusion | flops 2481664 | bytes 217856 | tf_op jit(solution)/shard_map/jvp()/reduce_sum | solution.py:43
  25.4 2.1 %multiply_multiply_fusion.5 = (f32[384,256]{1,0:T(8,128)S(1)}, f32[384,256]{1,0:T(8,128)}, f32[384,256]{1,0:T(8,128)}) fusion(f32[384]{0:T(512)S(1)} %add.548, f32[384,96]{1,0:T(8,128)S(1)} %bitcast.220, f32[96,256]{0,1:T(8,128)S(1)} %bitcast.224), kind=kOutput, calls=%fused_computation.74 | convolution fusion | flops 119635968 | bytes 1426944 | tf_op jit(solution)/shard_map/jvp()/dot_general | solution.py:47
  28.6 14.5 %all_to_all.30 = f32[16,64,98]{2,1,0:T(8,128)S(1)} all-to-all(f32[16,64,98]{2,1,0:T(8,128)S(1)} %broadcast_in_dim.273), channel_id=1, replica_groups=mesh['dp'=2,'tx'=4,'tz'=8,'chan'=4] {'chan','tx'}, dimensions={0} | all-to-all | bytes 802816 | tf_op jit(solution)/shard_map/all_to_all | solution.py:56
  43.2 0.7 broadcast_in_dim.274
  43.9 8.2 %all-to-all-start.2 = ((f32[8,64,98]{2,1,0:T(8,128)}), f32[8,64,98]{2,1,0:T(8,128)S(1)}, u32[]{:S(2)}, u32[]{:S(2)}) async-start(f32[8,64,98]{2,1,0:T(8,128)} %broadcast_in_dim.274), calls=%async_computation.2 | async-start | bytes 524288 | tf_op jit(solution)/shard_map/all_to_all | solution.py:56
  52.5 9.0 %all-to-all-done.2 = f32[8,64,98]{2,1,0:T(8,128)S(1)} async-done(((f32[8,64,98]{2,1,0:T(8,128)}), f32[8,64,98]{2,1,0:T(8,128)S(1)}, u32[]{:S(2)}, u32[]{:S(2)}) %all-to-all-start.2) | async-done | bytes 200736 | tf_op jit(solution)/shard_map/all_to_all | solution.py:56
  61.7 1.4 multiply_reduce_fusion.53
  63.9 0.7 copy.112
  64.7 1.2 fusion.45
  65.9 1.1 multiply_reduce_fusion.49
  67.0 0.7 fusion.40
  67.8 0.8 multiply_reduce_fusion.45
  68.7 1.0 multiply_reduce_fusion.46
  69.7 0.9 multiply_reduce_fusion.47
  71.5 0.9 broadcast_multiply_fusion.2
  72.6 1.4 broadcast_multiply_fusion.1
  74.1 1.5 broadcast_multiply_fusion
  78.2 0.9 copy-done.9
  84.6 0.9 pad_add_fusion.7
  86.4 0.8 reshape.465
  87.4 3.2 %pad_add_fusion = f32[96,4,14,14]{0,3,2,1:T(8,128)S(1)} fusion(f32[96,4,8,8]{0,3,2,1:T(8,128)} %get-tuple-element.143, f32[96,4,8,8]{0,3,2,1:T(8,128)} %get-tuple-element.144, f32[96,4,8,8]{0,3,2,1:T(8,128)} %get-tuple-element.145, f32[96,4,8,8]{0,3,2,1:T(8,128)} %get-tuple-element.146, f32[96,4,8,8]{0,3,2,1:T(8,128)} %get-tuple-element.147, ...), kind=kLoop, calls=%fused_computation.58 | loop fusion | flops 3161088 | bytes 4528128 | tf_op jit(solution)/shard_map/transpose(jvp())/add_any | solution.py:27
  93.9 21.5 %all_to_all.31 = f32[8,248,128]{2,1,0:T(8,128)S(1)} all-to-all(f32[8,248,128]{2,1,0:T(8,128)S(1)} %bitcast.212), channel_id=1, replica_groups=mesh['dp'=2,'tx'=4,'tz'=8,'chan'=4] {'dp','chan'}, dimensions={0} | all-to-all | bytes 2031616 | tf_op jit(solution)/shard_map/all_to_all | solution.py:66
  115.5 11.4 %all_to_all.32 = f32[4,248,128]{2,1,0:T(8,128)S(1)} all-to-all(f32[4,248,128]{2,1,0:T(8,128)S(1)} %broadcast_in_dim.331), channel_id=1, replica_groups=mesh['dp'=2,'tx'=4,'tz'=8,'chan'=4] {'tx'}, dimensions={0} | all-to-all | bytes 1015808 | tf_op jit(solution)/shard_map/all_to_all | solution.py:56
  127.0 28.7 %all_to_all.33 = f32[8,248,128]{2,1,0:T(8,128)S(1)} all-to-all(f32[8,248,128]{2,1,0:T(8,128)S(1)} %broadcast_in_dim.332), channel_id=1, replica_groups=mesh['dp'=2,'tx'=4,'tz'=8,'chan'=4] {'tz'}, dimensions={0} | all-to-all | bytes 2031616 | tf_op jit(solution)/shard_map/all_to_all | solution.py:56
  (403 shorter events, 25.0 us)
Async XLA Ops:
  0.6 21.5 %copy-start = (f32[48,1024]{1,0:T(8,128)S(1)}, f32[48,1024]{1,0:T(8,128)}, u32[]{:S(2)}) copy-start(f32[48,1024]{1,0:T(8,128)} %param.15) | copy-start | bytes 589828
  0.7 4.1 %copy-start.19 = (f32[96,96]{1,0:T(8,128)S(1)}, f32[96,96]{1,0:T(8,128)}, u32[]{:S(2)}) copy-start(f32[96,96]{1,0:T(8,128)} %param.24) | copy-start | bytes 110596
  6.5 12.5 %all-to-all-start = ((f32[4,248,128]{2,1,0:T(8,128)}), f32[4,248,128]{2,1,0:T(8,128)S(1)}, u32[]{:S(2)}, u32[]{:S(2)}) async-start(f32[4,248,128]{2,1,0:T(8,128)} %broadcast_in_dim.268), calls=%async_computation | async-start | bytes 1015808 | tf_op jit(solution)/shard_map/all_to_all | solution.py:120
  19.4 3.1 %copy-start.24 = (f32[96]{0:T(128)}, f32[96]{0:T(128)S(1)}, u32[]{:S(2)}) copy-start(f32[96]{0:T(128)S(1)} %get-tuple-element.120) | copy-start | bytes 1156
  19.4 3.1 %copy-start.26 = (f32[96]{0:T(128)}, f32[96]{0:T(128)S(1)}, u32[]{:S(2)}) copy-start(f32[96]{0:T(128)S(1)} %get-tuple-element.121) | copy-start | bytes 1156
  19.4 3.1 %copy-start.28 = (f32[96]{0:T(128)}, f32[96]{0:T(128)S(1)}, u32[]{:S(2)}) copy-start(f32[96]{0:T(128)S(1)} %get-tuple-element.122) | copy-start | bytes 1156
  20.1 2.4 %copy-start.32 = (f32[96]{0:T(128)}, f32[96]{0:T(128)S(1)}, u32[]{:S(2)}) copy-start(f32[96]{0:T(128)S(1)} %get-tuple-element.108) | copy-start | bytes 1156
  20.2 2.4 %copy-start.34 = (f32[96]{0:T(128)}, f32[96]{0:T(128)S(1)}, u32[]{:S(2)}) copy-start(f32[96]{0:T(128)S(1)} %get-tuple-element.109) | copy-start | bytes 1156
  20.2 2.4 %copy-start.36 = (f32[96]{0:T(128)}, f32[96]{0:T(128)S(1)}, u32[]{:S(2)}) copy-start(f32[96]{0:T(128)S(1)} %get-tuple-element.110) | copy-start | bytes 1156
  20.2 2.4 %copy-start.38 = (f32[96]{0:T(128)}, f32[96]{0:T(128)S(1)}, u32[]{:S(2)}) copy-start(f32[96]{0:T(128)S(1)} %get-tuple-element.111) | copy-start | bytes 1156
  20.2 2.4 %copy-start.44 = (f32[96]{0:T(128)}, f32[96]{0:T(128)S(1)}, u32[]{:S(2)}) copy-start(f32[96]{0:T(128)S(1)} %get-tuple-element.94) | copy-start | bytes 1156
  20.2 2.4 %copy-start.46 = (f32[96]{0:T(128)}, f32[96]{0:T(128)S(1)}, u32[]{:S(2)}) copy-start(f32[96]{0:T(128)S(1)} %get-tuple-element.95) | copy-start | bytes 1156
  20.2 2.4 %copy-start.48 = (f32[96]{0:T(128)}, f32[96]{0:T(128)S(1)}, u32[]{:S(2)}) copy-start(f32[96]{0:T(128)S(1)} %get-tuple-element.96) | copy-start | bytes 1156
  20.2 2.4 %copy-start.50 = (f32[96]{0:T(128)}, f32[96]{0:T(128)S(1)}, u32[]{:S(2)}) copy-start(f32[96]{0:T(128)S(1)} %get-tuple-element.97) | copy-start | bytes 1156
  20.2 2.4 %copy-start.52 = (f32[96]{0:T(128)}, f32[96]{0:T(128)S(1)}, u32[]{:S(2)}) copy-start(f32[96]{0:T(128)S(1)} %get-tuple-element.98) | copy-start | bytes 1156
  20.2 2.4 %copy-start.54 = (f32[96]{0:T(128)}, f32[96]{0:T(128)S(1)}, u32[]{:S(2)}) copy-start(f32[96]{0:T(128)S(1)} %get-tuple-element.99) | copy-start | bytes 1156
  20.2 2.4 %copy-start.56 = (f32[96]{0:T(128)}, f32[96]{0:T(128)S(1)}, u32[]{:S(2)}) copy-start(f32[96]{0:T(128)S(1)} %get-tuple-element.100) | copy-start | bytes 1156
  20.3 2.4 %copy-start.58 = (f32[96]{0:T(128)}, f32[96]{0:T(128)S(1)}, u32[]{:S(2)}) copy-start(f32[96]{0:T(128)S(1)} %get-tuple-element.101) | copy-start | bytes 1156
  20.3 2.4 %copy-start.60 = (f32[96]{0:T(128)}, f32[96]{0:T(128)S(1)}, u32[]{:S(2)}) copy-start(f32[96]{0:T(128)S(1)} %get-tuple-element.102) | copy-start | bytes 1156
  20.3 2.4 %copy-start.62 = (f32[96]{0:T(128)}, f32[96]{0:T(128)S(1)}, u32[]{:S(2)}) copy-start(f32[96]{0:T(128)S(1)} %get-tuple-element.103) | copy-start | bytes 1156
  20.3 2.4 %copy-start.64 = (f32[96]{0:T(128)}, f32[96]{0:T(128)S(1)}, u32[]{:S(2)}) copy-start(f32[96]{0:T(128)S(1)} %get-tuple-element.104) | copy-start | bytes 1156
  43.9 17.6 %all-to-all-start.2 = ((f32[8,64,98]{2,1,0:T(8,128)}), f32[8,64,98]{2,1,0:T(8,128)S(1)}, u32[]{:S(2)}, u32[]{:S(2)}) async-start(f32[8,64,98]{2,1,0:T(8,128)} %broadcast_in_dim.274), calls=%async_computation.2 | async-start | bytes 524288 | tf_op jit(solution)/shard_map/all_to_all | solution.py:56
  61.5 3.1 %copy-start.153 = (f32[384,256]{1,0:T(8,128)S(1)}, f32[384,256]{1,0:T(8,128)}, u32[]{:S(2)}) copy-start(f32[384,256]{1,0:T(8,128)} %get-tuple-element.198) | copy-start | bytes 1179652
  61.5 3.1 %copy-start.152 = (f32[384,256]{1,0:T(8,128)S(1)}, f32[384,256]{1,0:T(8,128)}, u32[]{:S(2)}) copy-start(f32[384,256]{1,0:T(8,128)} %get-tuple-element.131) | copy-start | bytes 1179652
  74.1 2.7 %copy-start.147 = (f32[64]{0:T(128)S(1)}, f32[64]{0:T(128)}, u32[]{:S(2)}) copy-start(f32[64]{0:T(128)} %copy-done.146) | copy-start | bytes 772
  74.1 2.7 %copy-start.154 = (f32[64]{0:T(128)S(1)}, f32[64]{0:T(128)}, u32[]{:S(2)}) copy-start(f32[64]{0:T(128)} %get-tuple-element.199) | copy-start | bytes 772
  87.4 3.3 %copy-start.10 = (f32[96,4,8,8]{0,3,2,1:T(8,128)S(1)}, f32[96,4,8,8]{0,3,2,1:T(8,128)}, u32[]{:S(2)}) copy-start(f32[96,4,8,8]{0,3,2,1:T(8,128)} %get-tuple-element.137) | copy-start | bytes 294916
  87.4 3.3 %copy-start.11 = (f32[96,4,8,8]{0,3,2,1:T(8,128)S(1)}, f32[96,4,8,8]{0,3,2,1:T(8,128)}, u32[]{:S(2)}) copy-start(f32[96,4,8,8]{0,3,2,1:T(8,128)} %get-tuple-element.138) | copy-start | bytes 294916
  87.4 3.3 %copy-start.12 = (f32[96,4,8,8]{0,3,2,1:T(8,128)S(1)}, f32[96,4,8,8]{0,3,2,1:T(8,128)}, u32[]{:S(2)}) copy-start(f32[96,4,8,8]{0,3,2,1:T(8,128)} %get-tuple-element.139) | copy-start | bytes 294916
  87.4 3.3 %copy-start.13 = (f32[96,4,8,8]{0,3,2,1:T(8,128)S(1)}, f32[96,4,8,8]{0,3,2,1:T(8,128)}, u32[]{:S(2)}) copy-start(f32[96,4,8,8]{0,3,2,1:T(8,128)} %get-tuple-element.140) | copy-start | bytes 294916
  87.4 3.3 %copy-start.14 = (f32[96,4,8,8]{0,3,2,1:T(8,128)S(1)}, f32[96,4,8,8]{0,3,2,1:T(8,128)}, u32[]{:S(2)}) copy-start(f32[96,4,8,8]{0,3,2,1:T(8,128)} %get-tuple-element.141) | copy-start | bytes 294916
  87.4 3.3 %copy-start.15 = (f32[96,4,8,8]{0,3,2,1:T(8,128)S(1)}, f32[96,4,8,8]{0,3,2,1:T(8,128)}, u32[]{:S(2)}) copy-start(f32[96,4,8,8]{0,3,2,1:T(8,128)} %get-tuple-element.142) | copy-start | bytes 294916
  (125 other events, 126.4 us)

commit v6 on v4

--- a/solution.py
+++ b/solution.py
@@ -53,6 +53,12 @@
     count = lax.psum(1, axis)
     copies = jnp.broadcast_to(value[None], (count,) + value.shape)
     return jnp.sum(lax.all_to_all(copies, axis, 0, 0, tiled=True), axis=0)
+
+
+def gather_rows(value, axis):
+    count = lax.psum(1, axis)
+    copies = jnp.broadcast_to(value[None], (count,) + value.shape)
+    return lax.all_to_all(copies, axis, 0, 0, tiled=True).reshape((-1,) + value.shape[1:])
 
 
 def psum_steps(value, axes):
@@ -136,21 +142,31 @@
     ) * live[:, None]
 
     pooled, pull = jax.vjp(lambda p: block_pooled(p, my_pixels), params)
-    slide_part = jnp.dot(onehot.T, pooled.T, precision=highest)
-    placed = lax.dynamic_update_slice_in_dim(
-        jnp.zeros((group_slides,), jnp.float32),
-        jnp.where(chan == 0, target, 0.0),
-        tile * slide_dev,
-        axis=0,
-    )
-    slide_pack = jnp.concatenate(
-        [slide_part, jnp.sum(onehot, axis=0)[:, None], placed[:, None]], axis=1
-    )
-    slide_pack = psum_steps(slide_pack, (("chan", "tx"), "tz"))
-    width = slide_part.shape[1]
-    sums = slide_pack[:, :width]
-    counts = jnp.maximum(slide_pack[:, width], 1.0)
-    target_all = slide_pack[:, width + 1]
+    target_rows = jnp.zeros((slots,), jnp.float32)
+    target_rows = lax.dynamic_update_slice_in_dim(target_rows, target, 0, axis=0)
+    rows = jnp.concatenate(
+        [
+            pooled.T,
+            my_slide.astype(jnp.float32)[:, None],
+            live[:, None],
+            jnp.where(chan == 0, target_rows, 0.0)[:, None],
+        ],
+        axis=1,
+    )
+    rows = gather_rows(gather_rows(rows, ("chan", "tx")), "tz")
+    width = pooled.shape[0]
+    onehot_all = (
+        rows[:, width : width + 1] == jnp.arange(group_slides, dtype=jnp.float32)[None, :]
+    ).astype(jnp.float32) * rows[:, width + 1 : width + 2]
+    sums = jnp.dot(onehot_all.T, rows[:, :width], precision=highest)
+    counts = jnp.maximum(jnp.sum(onehot_all, axis=0), 1.0)
+    x_count = lax.psum(1, "tx")
+    z_count = lax.psum(1, "tz")
+    tile_of = np.arange(group_slides) // slide_dev
+    where = (tile_of % z_count) * (rows.shape[0] // z_count) + (tile_of // z_count) * slots + (
+        np.arange(group_slides) % slide_dev
+    )
+    target_all = rows[where, width + 2]
 
     slide_feat = sums / counts[:, None]
     logit = jnp.dot(slide_feat, head, precision=highest)

time: 146 us -> 143 us (0.979)
  blocking collectives: 63.1 us -> 60.6 us
    all_to_all x3 -> x2, blocking collectives: 45.3 us -> 31 us  [spread_sum(): return jnp.sum(lax.all_to_all(copies, axis, 0, 0, tiled=True), axis=0)]
    all_to_all x0 -> x1, blocking collectives: none -> 11.4 us  [gather_rows(): lax.all_to_all(copies, axis, 0, 0, tiled=True)]
    unnamed x279 -> x149, local copies, waits for them, and re-layouts: 7.63 us -> 7.24 us
where the time goes in v6:
time: 143 us; the launch traced here: 142 us
  blocking collectives  60.6 us (42%)
  local copies, waits for them, and re-layouts  29 us (20%)
  other arithmetic  14.6 us (10%)
  starting transfers between devices  13.2 us (9%)
  waiting for transfers between devices  12.8 us (9%)
  matrix products  8.33 us (6%)
  between operations  3.05 us (2%)
    all_to_all x2, blocking collectives, spread_sum(): return jnp.sum(lax.all_to_all(copies, axis, 0, 0, tiled=True), axis=0)  31 us
    all_to_all x1, blocking collectives, scatter_sum(): return jnp.sum(lax.all_to_all(value, axis, 0, 0, tiled=True), axis=0)  18.2 us
    all_to_all x1, blocking collectives, gather_rows(): lax.all_to_all(copies, axis, 0, 0, tiled=True)  11.4 us
    all_to_all x1, waiting for transfers between devices, gather_rows(): lax.all_to_all(copies, axis, 0, 0, tiled=True)  8.97 us
    all_to_all x1, starting transfers between devices, gather_rows(): lax.all_to_all(copies, axis, 0, 0, tiled=True)  8.19 us
    unnamed x149, local copies, waits for them, and re-layouts  7.24 us
    all_to_all x1, starting transfers between devices, gather_chan(): gathered = lax.all_to_all(copies, 'chan', 0, 0, tiled=True)  5 us
    reshape x10, local copies, waits for them, and re-layouts, per_device(): g.reshape(chan_count, -1)  4.57 us
  transfers between devices with their start and end apart: 2, of which 2 were waited for; matrix products, arithmetic and copies ran while one was open for 1% of the time, Pallas kernels for 0%

profile of v6, /device:TPU:1, one launch (start us, length us, event | category | flops | bytes accessed | tf_op | source)
XLA Modules:
  0.0 141.5 jit_solution(11332113436246710018)
XLA Ops:
  0.7 0.8 reshape.513
  1.6 0.9 reshape.519
  4.0 0.9 broadcast_in_dim.220
  4.9 5.0 %all-to-all-start = ((f32[4,1,21000]{2,1,0:T(1,128)}), f32[4,1,21000]{2,1,0:T(1,128)S(1)}, u32[]{:S(2)}, u32[]{:S(2)}) async-start(f32[4,1,21000]{2,1,0:T(1,128)} %broadcast_in_dim.220), calls=%async_computation | async-start | bytes 675840 | tf_op jit(solution)/shard_map/all_to_all | solution.py:78
  12.0 3.8 %all-to-all-done = f32[4,1,21000]{2,1,0:T(1,128)S(1)} async-done(((f32[4,1,21000]{2,1,0:T(1,128)}), f32[4,1,21000]{2,1,0:T(1,128)S(1)}, u32[]{:S(2)}, u32[]{:S(2)}) %all-to-all-start) | async-done | bytes 336032 | tf_op jit(solution)/shard_map/all_to_all | solution.py:78
  16.9 0.7 slice_reduce_fusion.49
  19.6 0.9 multiply_reduce_fusion.48
  20.7 1.3 fusion.3
  22.7 11.4 %all_to_all.40 = f32[16,4,99]{2,1,0:T(4,128)S(1)} all-to-all(f32[16,4,99]{2,1,0:T(4,128)S(1)} %broadcast_in_dim.223), channel_id=1, replica_groups=mesh['dp'=2,'tx'=4,'tz'=8,'chan'=4] {'chan','tx'}, dimensions={0} | all-to-all | bytes 50688 | tf_op jit(solution)/shard_map/all_to_all | solution.py:61
  34.1 0.7 broadcast_in_dim.225
  34.8 8.2 %all-to-all-start.2 = ((f32[8,64,99]{2,1,0:T(8,128)}), f32[8,64,99]{2,1,0:T(8,128)S(1)}, u32[]{:S(2)}, u32[]{:S(2)}) async-start(f32[8,64,99]{2,1,0:T(8,128)} %broadcast_in_dim.225), calls=%async_computation.2 | async-start | bytes 524288 | tf_op jit(solution)/shard_map/all_to_all | solution.py:61
  43.5 9.0 %all-to-all-done.2 = f32[8,64,99]{2,1,0:T(8,128)S(1)} async-done(((f32[8,64,99]{2,1,0:T(8,128)}), f32[8,64,99]{2,1,0:T(8,128)S(1)}, u32[]{:S(2)}, u32[]{:S(2)}) %all-to-all-start.2) | async-done | bytes 202784 | tf_op jit(solution)/shard_map/all_to_all | solution.py:61
  53.1 0.8 gather_fusion
  54.3 1.3 multiply_reduce_fusion.53
  56.4 0.8 fusion.11
  57.2 1.2 fusion.53
  58.4 1.1 multiply_reduce_fusion.49
  59.6 0.8 fusion.13
  60.4 0.7 fusion.47
  61.2 0.8 multiply_reduce_fusion.45
  62.0 1.0 multiply_reduce_fusion.46
  63.0 0.9 multiply_reduce_fusion.47
  64.2 1.2 broadcast_multiply_fusion.1
  65.4 1.4 %broadcast_multiply_fusion = (f32[96,4,8,8]{0,3,2,1:T(8,128)}, f32[96,4,8,8]{0,3,2,1:T(8,128)}, f32[96,4,8,8]{0,3,2,1:T(8,128)}, f32[96,4,8,8]{0,3,2,1:T(8,128)}...) fusion(f32[96,4,8,8]{0,3,2,1:T(8,128)S(1)} %bitcast.161, ...), kind=kLoop, calls=%fused_computation.160 | loop fusion | flops 442368 | bytes 1874688 | tf_op jit(solution)/shard_map/transpose(jvp())/mul | solution.py:25
  75.4 1.5 %pad_add_fusion.7 = f32[96,49]{0,1:T(8,128)} fusion(f32[96,1]{0,1:T(1,128)S(1)} %bitcast.188, f32[96,1]{0,1:T(1,128)S(1)} %bitcast.208, f32[96,1]{0,1:T(1,128)S(1)} %bitcast.209, f32[96,1]{0,1:T(1,128)S(1)} %bitcast.210, f32[96,1]{0,1:T(1,128)S(1)} %bitcast.211, f32[96,1]{0,1:T(1,128)} %bitcast.212, f32[96,1]{0,1:T(1,128)} %bitcast.213, ...), kind=kLoop, calls=%fused_computation.267 | loop fusion | flops 225792 | bytes 37632 | tf_op jit(solution)/shard_map/transpose(jvp())/add_any | solution.py:22
  76.9 0.8 copy.134
  77.8 0.7 reshape.538
  78.5 3.2 %pad_add_fusion = f32[96,4,14,14]{0,3,2,1:T(8,128)S(1)} fusion(f32[96,4,8,8]{0,3,2,1:T(8,128)} %get-tuple-element.142, f32[96,4,8,8]{0,3,2,1:T(8,128)} %get-tuple-element.143, f32[96,4,8,8]{0,3,2,1:T(8,128)} %get-tuple-element.144, f32[96,4,8,8]{0,3,2,1:T(8,128)} %get-tuple-element.145, f32[96,4,8,8]{0,3,2,1:T(8,128)} %get-tuple-element.146, ...), kind=kLoop, calls=%fused_computation.60 | loop fusion | flops 3161088 | bytes 4528128 | tf_op jit(solution)/shard_map/transpose(jvp())/add_any | solution.py:26
  84.9 0.8 all_to_all.30
  85.7 18.2 %all_to_all.41 = f32[8,1,21001]{2,1,0:T(1,128)S(1)} all-to-all(f32[8,1,21001]{2,1,0:T(1,128)S(1)} %all_to_all.30), channel_id=1, replica_groups=mesh['dp'=2,'tx'=4,'tz'=8,'chan'=4] {'dp','chan'}, dimensions={0} | all-to-all | bytes 1344064 | tf_op jit(solution)/shard_map/all_to_all | solution.py:71
  104.6 9.3 %all_to_all.42 = f32[4,1,21001]{2,1,0:T(1,128)S(1)} all-to-all(f32[4,1,21001]{2,1,0:T(1,128)S(1)} %broadcast_in_dim.282), channel_id=1, replica_groups=mesh['dp'=2,'tx'=4,'tz'=8,'chan'=4] {'tx'}, dimensions={0} | all-to-all | bytes 672032 | tf_op jit(solution)/shard_map/all_to_all | solution.py:55
  114.6 21.7 %all_to_all.43 = f32[8,1,21001]{2,1,0:T(1,128)S(1)} all-to-all(f32[8,1,21001]{2,1,0:T(1,128)S(1)} %broadcast_in_dim.283), channel_id=1, replica_groups=mesh['dp'=2,'tx'=4,'tz'=8,'chan'=4] {'tz'}, dimensions={0} | all-to-all | bytes 1344064 | tf_op jit(solution)/shard_map/all_to_all | solution.py:55
  (235 shorter events, 26.5 us)
Async XLA Ops:
  0.6 18.4 %copy-start = (f32[48,1024]{1,0:T(8,128)S(1)}, f32[48,1024]{1,0:T(8,128)}, u32[]{:S(2)}) copy-start(f32[48,1024]{1,0:T(8,128)} %param.17) | copy-start | bytes 589828
  0.7 0.8 copy-start.16
  1.5 1.0 copy-start.13
  4.9 10.9 %all-to-all-start = ((f32[4,1,21000]{2,1,0:T(1,128)}), f32[4,1,21000]{2,1,0:T(1,128)S(1)}, u32[]{:S(2)}, u32[]{:S(2)}) async-start(f32[4,1,21000]{2,1,0:T(1,128)} %broadcast_in_dim.220), calls=%async_computation | async-start | bytes 675840 | tf_op jit(solution)/shard_map/all_to_all | solution.py:78
  34.8 17.6 %all-to-all-start.2 = ((f32[8,64,99]{2,1,0:T(8,128)}), f32[8,64,99]{2,1,0:T(8,128)S(1)}, u32[]{:S(2)}, u32[]{:S(2)}) async-start(f32[8,64,99]{2,1,0:T(8,128)} %broadcast_in_dim.225), calls=%async_computation.2 | async-start | bytes 524288 | tf_op jit(solution)/shard_map/all_to_all | solution.py:61
  65.4 1.4 %copy-start.61 = (f32[96]{0:T(128)S(1)}, f32[96]{0:T(128)}, u32[]{:S(2)}) copy-start(f32[96]{0:T(128)} %broadcast_reduce_fusion) | copy-start | bytes 1156
  70.3 8.2 %copy-start.5 = (f32[96,4,8,8]{0,3,2,1:T(8,128)S(1)}, f32[96,4,8,8]{0,3,2,1:T(8,128)}, u32[]{:S(2)}) copy-start(f32[96,4,8,8]{0,3,2,1:T(8,128)} %get-tuple-element.162) | copy-start | bytes 294916
  74.4 0.7 copy-start.26
  74.4 0.7 copy-start.27
  74.4 0.7 copy-start.28
  74.4 0.7 copy-start.29
  74.4 0.7 copy-start.30
  74.4 0.7 copy-start.31
  74.5 0.7 copy-start.32
  74.5 0.7 copy-start.33
  74.5 0.7 copy-start.39
  74.6 0.7 copy-start.45
  74.7 3.7 %copy-start.4 = (f32[96,4,8,8]{0,3,2,1:T(8,128)S(1)}, f32[96,4,8,8]{0,3,2,1:T(8,128)}, u32[]{:S(2)}) copy-start(f32[96,4,8,8]{0,3,2,1:T(8,128)} %get-tuple-element.161) | copy-start | bytes 294916
  75.4 3.1 %copy-start.2 = (f32[96,4,8,8]{0,3,2,1:T(8,128)S(1)}, f32[96,4,8,8]{0,3,2,1:T(8,128)}, u32[]{:S(2)}) copy-start(f32[96,4,8,8]{0,3,2,1:T(8,128)} %get-tuple-element.159) | copy-start | bytes 294916
  75.4 3.1 %copy-start.3 = (f32[96,4,8,8]{0,3,2,1:T(8,128)S(1)}, f32[96,4,8,8]{0,3,2,1:T(8,128)}, u32[]{:S(2)}) copy-start(f32[96,4,8,8]{0,3,2,1:T(8,128)} %get-tuple-element.160) | copy-start | bytes 294916
  78.5 3.2 %copy-start.6 = (f32[96,4,8,8]{0,3,2,1:T(8,128)S(1)}, f32[96,4,8,8]{0,3,2,1:T(8,128)}, u32[]{:S(2)}) copy-start(f32[96,4,8,8]{0,3,2,1:T(8,128)} %get-tuple-element.136) | copy-start | bytes 294916
  78.5 3.2 %copy-start.7 = (f32[96,4,8,8]{0,3,2,1:T(8,128)S(1)}, f32[96,4,8,8]{0,3,2,1:T(8,128)}, u32[]{:S(2)}) copy-start(f32[96,4,8,8]{0,3,2,1:T(8,128)} %get-tuple-element.137) | copy-start | bytes 294916
  78.5 3.2 %copy-start.8 = (f32[96,4,8,8]{0,3,2,1:T(8,128)S(1)}, f32[96,4,8,8]{0,3,2,1:T(8,128)}, u32[]{:S(2)}) copy-start(f32[96,4,8,8]{0,3,2,1:T(8,128)} %get-tuple-element.138) | copy-start | bytes 294916
  78.5 3.2 %copy-start.9 = (f32[96,4,8,8]{0,3,2,1:T(8,128)S(1)}, f32[96,4,8,8]{0,3,2,1:T(8,128)}, u32[]{:S(2)}) copy-start(f32[96,4,8,8]{0,3,2,1:T(8,128)} %get-tuple-element.139) | copy-start | bytes 294916
  78.5 3.2 %copy-start.10 = (f32[96,4,8,8]{0,3,2,1:T(8,128)S(1)}, f32[96,4,8,8]{0,3,2,1:T(8,128)}, u32[]{:S(2)}) copy-start(f32[96,4,8,8]{0,3,2,1:T(8,128)} %get-tuple-element.140) | copy-start | bytes 294916
  78.5 3.2 %copy-start.11 = (f32[96,4,8,8]{0,3,2,1:T(8,128)S(1)}, f32[96,4,8,8]{0,3,2,1:T(8,128)}, u32[]{:S(2)}) copy-start(f32[96,4,8,8]{0,3,2,1:T(8,128)} %get-tuple-element.141) | copy-start | bytes 294916
  81.7 0.7 copy-start.15
  82.6 1.2 copy-start.20
  82.6 1.2 copy-start.21
  82.6 1.2 copy-start.22
  83.0 0.8 copy-start.12
  83.1 0.7 copy-start.19
  (44 other events, 29.3 us)

commit v7 on v6

--- a/solution.py
+++ b/solution.py
@@ -7,6 +7,8 @@
 
 SIDE = 8
 X_SPAN = 4
+MAT = (0, 2, 6, 8, 7)
+SMALL = (1, 3, 4, 5, 9, 10)
 
 
 epsilon = 1e-06
@@ -129,7 +131,26 @@
         b_down,
         w_head,
     )
-    full = gather_chan(shards, chan_count, spread=True)
+    packed = jnp.concatenate(
+        [shards[i].reshape(1, -1) for i in MAT]
+        + [jnp.stack([shards[i] for i in SMALL]).reshape(1, -1)],
+        axis=1,
+    )
+    copies = jnp.broadcast_to(packed, (chan_count, packed.shape[1]))
+    gathered = lax.all_to_all(copies, "chan", 0, 0, tiled=True)
+    full = [None] * len(shards)
+    offset = 0
+    for i in MAT:
+        n = shards[i].size
+        full[i] = gathered[:, offset : offset + n].reshape(
+            (chan_count * shards[i].shape[0],) + shards[i].shape[1:]
+        )
+        offset += n
+    piece = shards[SMALL[0]].shape[0]
+    block = gathered[:, offset : offset + len(SMALL) * piece].reshape(chan_count, len(SMALL), piece)
+    block = block.transpose(1, 0, 2).reshape(len(SMALL), chan_count * piece)
+    for k, i in enumerate(SMALL):
+        full[i] = block[k]
     params = tuple(full[:10])
     head = full[10]
 
@@ -180,8 +201,12 @@
 
     lead = tile == 0
     g_head = jnp.where(lead & (chan == 0), g_head, 0.0)
+    all_grads = list(grads) + [g_head]
+    small = jnp.stack([all_grads[i] for i in SMALL]).reshape(len(SMALL), chan_count, -1)
     flat = jnp.concatenate(
-        [g.reshape(chan_count, -1) for g in grads] + [g_head.reshape(chan_count, -1)], axis=1
+        [all_grads[i].reshape(chan_count, -1) for i in MAT]
+        + [small.transpose(1, 0, 2).reshape(chan_count, -1)],
+        axis=1,
     )
     dp_count = lax.psum(1, "dp")
     flat = jnp.concatenate(
@@ -191,13 +216,16 @@
     mine = scatter_sum(flat, ("dp", "chan"))
     mine = psum_steps(mine, ("tx", "tz"))
 
-    outs = []
+    outs = [None] * len(shards)
     offset = 0
-    for s in shards[:10] + shards[10:]:
-        n = s.size
-        outs.append(mine[offset : offset + n].reshape(s.shape))
+    for i in MAT:
+        n = shards[i].size
+        outs[i] = mine[offset : offset + n].reshape(shards[i].shape)
         offset += n
-    outs.append(mine[offset])
+    block = mine[offset : offset + len(SMALL) * piece].reshape(len(SMALL), piece)
+    for k, i in enumerate(SMALL):
+        outs[i] = block[k]
+    outs.append(mine[offset + len(SMALL) * piece])
     return tuple(outs)
 
 

time: 143 us -> 147 us (1.028)
  local copies, waits for them, and re-layouts: 29 us -> 33.2 us
    another operation x0 -> x8, local copies, waits for them, and re-layouts: none -> 4.18 us  [the longest x7 3.37 us: per_device(): jnp.stack([all_grads[i] for i in SMALL]).reshape(len(SMALL), chan_count, -1)]
    reshape x25 -> x20, local copies, waits for them, and re-layouts: 10.6 us -> 7.17 us  [the longest x4 2.76 us: per_device(): outs[i] = mine[offset:offset + n].reshape(shards[i].shape)]
    unnamed x149 -> x142, local copies, waits for them, and re-layouts: 7.24 us -> 10.6 us
  transfers between devices with their start and end apart: 2 -> 2, of which waited for: 2 -> 2; matrix products, arithmetic and copies ran while one was open for 1% -> 0% of each run, Pallas kernels for 0% -> 0%
where the time goes in v7:
time: 147 us; the launch traced here: 146 us
  blocking collectives  60.6 us (41%)
  local copies, waits for them, and re-layouts  33.2 us (23%)
  other arithmetic  14.6 us (10%)
  starting transfers between devices  13.2 us (9%)
  waiting for transfers between devices  12.8 us (9%)
  matrix products  8.33 us (6%)
  between operations  2.93 us (2%)
    all_to_all x2, blocking collectives, spread_sum(): return jnp.sum(lax.all_to_all(copies, axis, 0, 0, tiled=True), axis=0)  31 us
    all_to_all x1, blocking collectives, scatter_sum(): return jnp.sum(lax.all_to_all(value, axis, 0, 0, tiled=True), axis=0)  18.2 us
    all_to_all x1, blocking collectives, gather_rows(): lax.all_to_all(copies, axis, 0, 0, tiled=True)  11.4 us
    unnamed x142, local copies, waits for them, and re-layouts  10.6 us
    all_to_all x1, waiting for transfers between devices, gather_rows(): lax.all_to_all(copies, axis, 0, 0, tiled=True)  8.97 us
    all_to_all x1, starting transfers between devices, gather_rows(): lax.all_to_all(copies, axis, 0, 0, tiled=True)  8.19 us
    all_to_all x1, starting transfers between devices, per_device(): gathered = lax.all_to_all(copies, 'chan', 0, 0, tiled=True)  5 us
    all_to_all x1, waiting for transfers between devices, per_device(): gathered = lax.all_to_all(copies, 'chan', 0, 0, tiled=True)  3.79 us
  transfers between devices with their start and end apart: 2, of which 2 were waited for; matrix products, arithmetic and copies ran while one was open for 0% of the time, Pallas kernels for 0%

profile of v7, /device:TPU:1, one launch (start us, length us, event | category | flops | bytes accessed | tf_op | source)
XLA Modules:
  0.0 145.6 jit_solution(4538584758587097772)
XLA Ops:
  0.7 0.8 stack.48
  1.6 0.8 reshape.522
  2.4 0.8 reshape.523
  4.7 0.9 broadcast_in_dim.220
  5.5 5.0 %all-to-all-start = ((f32[4,1,21000]{2,1,0:T(1,128)}), f32[4,1,21000]{2,1,0:T(1,128)S(1)}, u32[]{:S(2)}, u32[]{:S(2)}) async-start(f32[4,1,21000]{2,1,0:T(1,128)} %broadcast_in_dim.220), calls=%async_computation | async-start | bytes 675840 | tf_op jit(solution)/shard_map/all_to_all | solution.py:140
  12.7 3.8 %all-to-all-done = f32[4,1,21000]{2,1,0:T(1,128)S(1)} async-done(((f32[4,1,21000]{2,1,0:T(1,128)}), f32[4,1,21000]{2,1,0:T(1,128)S(1)}, u32[]{:S(2)}, u32[]{:S(2)}) %all-to-all-start) | async-done | bytes 336032 | tf_op jit(solution)/shard_map/all_to_all | solution.py:140
  20.3 0.9 multiply_reduce_fusion.48
  21.4 1.3 fusion.3
  23.5 11.4 %all_to_all.40 = f32[16,4,99]{2,1,0:T(4,128)S(1)} all-to-all(f32[16,4,99]{2,1,0:T(4,128)S(1)} %broadcast_in_dim.223), channel_id=1, replica_groups=mesh['dp'=2,'tx'=4,'tz'=8,'chan'=4] {'chan','tx'}, dimensions={0} | all-to-all | bytes 50688 | tf_op jit(solution)/shard_map/all_to_all | solution.py:63
  34.8 0.7 broadcast_in_dim.225
  35.5 8.2 %all-to-all-start.2 = ((f32[8,64,99]{2,1,0:T(8,128)}), f32[8,64,99]{2,1,0:T(8,128)S(1)}, u32[]{:S(2)}, u32[]{:S(2)}) async-start(f32[8,64,99]{2,1,0:T(8,128)} %broadcast_in_dim.225), calls=%async_computation.2 | async-start | bytes 524288 | tf_op jit(solution)/shard_map/all_to_all | solution.py:63
  44.2 9.0 %all-to-all-done.2 = f32[8,64,99]{2,1,0:T(8,128)S(1)} async-done(((f32[8,64,99]{2,1,0:T(8,128)}), f32[8,64,99]{2,1,0:T(8,128)S(1)}, u32[]{:S(2)}, u32[]{:S(2)}) %all-to-all-start.2) | async-done | bytes 202784 | tf_op jit(solution)/shard_map/all_to_all | solution.py:63
  53.8 0.8 gather_fusion
  55.0 1.3 multiply_reduce_fusion.53
  57.1 0.8 fusion.11
  57.9 1.2 fusion.52
  59.1 1.1 multiply_reduce_fusion.49
  60.3 0.8 fusion.13
  61.2 0.7 fusion.47
  62.0 0.8 multiply_reduce_fusion.45
  62.8 1.0 multiply_reduce_fusion.46
  63.7 0.9 multiply_reduce_fusion.47
  64.9 1.2 broadcast_multiply_fusion.1
  66.1 1.4 broadcast_multiply_fusion
  76.1 1.5 %pad_add_fusion.7 = f32[96,49]{0,1:T(8,128)} fusion(f32[96,1]{0,1:T(1,128)S(1)} %bitcast.194, f32[96,1]{0,1:T(1,128)S(1)} %bitcast.214, f32[96,1]{0,1:T(1,128)S(1)} %bitcast.215, f32[96,1]{0,1:T(1,128)S(1)} %bitcast.216, f32[96,1]{0,1:T(1,128)S(1)} %bitcast.217, f32[96,1]{0,1:T(1,128)} %bitcast.218, f32[96,1]{0,1:T(1,128)} %bitcast.219, ...), kind=kLoop, calls=%fused_computation.267 | loop fusion | flops 225792 | bytes 37632 | tf_op jit(solution)/shard_map/transpose(jvp())/add_any | solution.py:24
  77.6 0.8 copy.89
  78.5 0.7 reshape.541
  79.3 3.2 %pad_add_fusion = f32[96,4,14,14]{0,3,2,1:T(8,128)S(1)} fusion(f32[96,4,8,8]{0,3,2,1:T(8,128)} %get-tuple-element.142, f32[96,4,8,8]{0,3,2,1:T(8,128)} %get-tuple-element.143, f32[96,4,8,8]{0,3,2,1:T(8,128)} %get-tuple-element.144, f32[96,4,8,8]{0,3,2,1:T(8,128)} %get-tuple-element.145, f32[96,4,8,8]{0,3,2,1:T(8,128)} %get-tuple-element.146, ...), kind=kLoop, calls=%fused_computation.60 | loop fusion | flops 3161088 | bytes 4528128 | tf_op jit(solution)/shard_map/transpose(jvp())/add_any | solution.py:28
  89.0 0.8 all_to_all.30
  89.8 18.2 %all_to_all.41 = f32[8,1,21001]{2,1,0:T(1,128)S(1)} all-to-all(f32[8,1,21001]{2,1,0:T(1,128)S(1)} %all_to_all.30), channel_id=1, replica_groups=mesh['dp'=2,'tx'=4,'tz'=8,'chan'=4] {'dp','chan'}, dimensions={0} | all-to-all | bytes 1344064 | tf_op jit(solution)/shard_map/all_to_all | solution.py:73
  108.7 9.3 %all_to_all.42 = f32[4,1,21001]{2,1,0:T(1,128)S(1)} all-to-all(f32[4,1,21001]{2,1,0:T(1,128)S(1)} %broadcast_in_dim.282), channel_id=1, replica_groups=mesh['dp'=2,'tx'=4,'tz'=8,'chan'=4] {'tx'}, dimensions={0} | all-to-all | bytes 672032 | tf_op jit(solution)/shard_map/all_to_all | solution.py:57
  118.7 21.7 %all_to_all.43 = f32[8,1,21001]{2,1,0:T(1,128)S(1)} all-to-all(f32[8,1,21001]{2,1,0:T(1,128)S(1)} %broadcast_in_dim.283), channel_id=1, replica_groups=mesh['dp'=2,'tx'=4,'tz'=8,'chan'=4] {'tz'}, dimensions={0} | all-to-all | bytes 1344064 | tf_op jit(solution)/shard_map/all_to_all | solution.py:57
  (235 shorter events, 30.7 us)
Async XLA Ops:
  0.6 19.2 %copy-start = (f32[48,1024]{1,0:T(8,128)S(1)}, f32[48,1024]{1,0:T(8,128)}, u32[]{:S(2)}) copy-start(f32[48,1024]{1,0:T(8,128)} %param.17) | copy-start | bytes 589828
  0.7 2.5 %copy-start.13 = (f32[96,96]{1,0:T(8,128)S(1)}, f32[96,96]{1,0:T(8,128)}, u32[]{:S(2)}) copy-start(f32[96,96]{1,0:T(8,128)} %param.26) | copy-start | bytes 110596
  2.3 1.0 copy-start.14
  5.5 10.9 %all-to-all-start = ((f32[4,1,21000]{2,1,0:T(1,128)}), f32[4,1,21000]{2,1,0:T(1,128)S(1)}, u32[]{:S(2)}, u32[]{:S(2)}) async-start(f32[4,1,21000]{2,1,0:T(1,128)} %broadcast_in_dim.220), calls=%async_computation | async-start | bytes 675840 | tf_op jit(solution)/shard_map/all_to_all | solution.py:140
  35.5 17.6 %all-to-all-start.2 = ((f32[8,64,99]{2,1,0:T(8,128)}), f32[8,64,99]{2,1,0:T(8,128)S(1)}, u32[]{:S(2)}, u32[]{:S(2)}) async-start(f32[8,64,99]{2,1,0:T(8,128)} %broadcast_in_dim.225), calls=%async_computation.2 | async-start | bytes 524288 | tf_op jit(solution)/shard_map/all_to_all | solution.py:63
  66.1 1.4 copy-start.61
  69.6 0.7 copy-start.62
  71.0 8.2 %copy-start.5 = (f32[96,4,8,8]{0,3,2,1:T(8,128)S(1)}, f32[96,4,8,8]{0,3,2,1:T(8,128)}, u32[]{:S(2)}) copy-start(f32[96,4,8,8]{0,3,2,1:T(8,128)} %get-tuple-element.162) | copy-start | bytes 294916
  75.1 0.7 copy-start.26
  75.1 0.7 copy-start.27
  75.1 0.7 copy-start.28
  75.1 0.7 copy-start.29
  75.1 0.7 copy-start.30
  75.2 0.7 copy-start.31
  75.2 0.7 copy-start.32
  75.2 0.7 copy-start.33
  75.2 0.7 copy-start.39
  75.3 0.7 copy-start.45
  75.4 3.7 %copy-start.4 = (f32[96,4,8,8]{0,3,2,1:T(8,128)S(1)}, f32[96,4,8,8]{0,3,2,1:T(8,128)}, u32[]{:S(2)}) copy-start(f32[96,4,8,8]{0,3,2,1:T(8,128)} %get-tuple-element.161) | copy-start | bytes 294916
  76.1 3.1 %copy-start.2 = (f32[96,4,8,8]{0,3,2,1:T(8,128)S(1)}, f32[96,4,8,8]{0,3,2,1:T(8,128)}, u32[]{:S(2)}) copy-start(f32[96,4,8,8]{0,3,2,1:T(8,128)} %get-tuple-element.159) | copy-start | bytes 294916
  76.1 3.1 %copy-start.3 = (f32[96,4,8,8]{0,3,2,1:T(8,128)S(1)}, f32[96,4,8,8]{0,3,2,1:T(8,128)}, u32[]{:S(2)}) copy-start(f32[96,4,8,8]{0,3,2,1:T(8,128)} %get-tuple-element.160) | copy-start | bytes 294916
  79.2 3.2 %copy-start.6 = (f32[96,4,8,8]{0,3,2,1:T(8,128)S(1)}, f32[96,4,8,8]{0,3,2,1:T(8,128)}, u32[]{:S(2)}) copy-start(f32[96,4,8,8]{0,3,2,1:T(8,128)} %get-tuple-element.136) | copy-start | bytes 294916
  79.2 3.2 %copy-start.7 = (f32[96,4,8,8]{0,3,2,1:T(8,128)S(1)}, f32[96,4,8,8]{0,3,2,1:T(8,128)}, u32[]{:S(2)}) copy-start(f32[96,4,8,8]{0,3,2,1:T(8,128)} %get-tuple-element.137) | copy-start | bytes 294916
  79.2 3.2 %copy-start.8 = (f32[96,4,8,8]{0,3,2,1:T(8,128)S(1)}, f32[96,4,8,8]{0,3,2,1:T(8,128)}, u32[]{:S(2)}) copy-start(f32[96,4,8,8]{0,3,2,1:T(8,128)} %get-tuple-element.138) | copy-start | bytes 294916
  79.2 3.2 %copy-start.9 = (f32[96,4,8,8]{0,3,2,1:T(8,128)S(1)}, f32[96,4,8,8]{0,3,2,1:T(8,128)}, u32[]{:S(2)}) copy-start(f32[96,4,8,8]{0,3,2,1:T(8,128)} %get-tuple-element.139) | copy-start | bytes 294916
  79.2 3.2 %copy-start.10 = (f32[96,4,8,8]{0,3,2,1:T(8,128)S(1)}, f32[96,4,8,8]{0,3,2,1:T(8,128)}, u32[]{:S(2)}) copy-start(f32[96,4,8,8]{0,3,2,1:T(8,128)} %get-tuple-element.140) | copy-start | bytes 294916
  79.2 3.2 %copy-start.11 = (f32[96,4,8,8]{0,3,2,1:T(8,128)S(1)}, f32[96,4,8,8]{0,3,2,1:T(8,128)}, u32[]{:S(2)}) copy-start(f32[96,4,8,8]{0,3,2,1:T(8,128)} %get-tuple-element.141) | copy-start | bytes 294916
  82.4 0.7 copy-start.16
  83.3 0.7 copy-start.22
  84.0 0.7 copy-start.20
  87.1 0.8 copy-start.12
  87.9 0.7 copy-start.17
  (38 other events, 25.3 us)

commit v8 on v6

--- a/solution.py
+++ b/solution.py
@@ -153,17 +153,16 @@
         ],
         axis=1,
     )
-    rows = gather_rows(gather_rows(rows, ("chan", "tx")), "tz")
+    rows = gather_rows(gather_rows(rows, "tz"), ("chan", "tx"))
     width = pooled.shape[0]
     onehot_all = (
         rows[:, width : width + 1] == jnp.arange(group_slides, dtype=jnp.float32)[None, :]
     ).astype(jnp.float32) * rows[:, width + 1 : width + 2]
     sums = jnp.dot(onehot_all.T, rows[:, :width], precision=highest)
     counts = jnp.maximum(jnp.sum(onehot_all, axis=0), 1.0)
-    x_count = lax.psum(1, "tx")
     z_count = lax.psum(1, "tz")
     tile_of = np.arange(group_slides) // slide_dev
-    where = (tile_of % z_count) * (rows.shape[0] // z_count) + (tile_of // z_count) * slots + (
+    where = (tile_of // z_count) * (slots * z_count) + (tile_of % z_count) * slots + (
         np.arange(group_slides) % slide_dev
     )
     target_all = rows[where, width + 2]

time: 143 us -> 142 us (level)
  blocking collectives: 60.6 us -> 49.4 us
  starting transfers between devices: 13.2 us -> 18.3 us
  waiting for transfers between devices: 12.8 us -> 17.5 us
    all_to_all x1 -> x0, blocking collectives: 11.4 us -> none  [gather_rows(): lax.all_to_all(copies, axis, 0, 0, tiled=True)]
    all_to_all x1 -> x2, starting transfers between devices: 8.19 us -> 13.3 us  [gather_rows(): lax.all_to_all(copies, axis, 0, 0, tiled=True)]
    all_to_all x1 -> x2, waiting for transfers between devices: 8.97 us -> 13.7 us  [gather_rows(): lax.all_to_all(copies, axis, 0, 0, tiled=True)]
  transfers between devices with their start and end apart: 2 -> 3, of which waited for: 2 -> 3; matrix products, arithmetic and copies ran while one was open for 1% -> 1% of each run, Pallas kernels for 0% -> 0%
where the time goes in v8:
time: 142 us; the launch traced here: 141 us
  blocking collectives  49.4 us (35%)
  local copies, waits for them, and re-layouts  29.6 us (21%)
  starting transfers between devices  18.3 us (13%)
  waiting for transfers between devices  17.5 us (12%)
  other arithmetic  14.6 us (10%)
  matrix products  8.33 us (6%)
  between operations  3.07 us (2%)
    all_to_all x2, blocking collectives, spread_sum(): return jnp.sum(lax.all_to_all(copies, axis, 0, 0, tiled=True), axis=0)  31 us
    all_to_all x1, blocking collectives, scatter_sum(): return jnp.sum(lax.all_to_all(value, axis, 0, 0, tiled=True), axis=0)  18.3 us
    all_to_all x2, waiting for transfers between devices, gather_rows(): lax.all_to_all(copies, axis, 0, 0, tiled=True)  13.7 us
    all_to_all x2, starting transfers between devices, gather_rows(): lax.all_to_all(copies, axis, 0, 0, tiled=True)  13.3 us
    unnamed x149, local copies, waits for them, and re-layouts  7.24 us
    all_to_all x1, starting transfers between devices, gather_chan(): gathered = lax.all_to_all(copies, 'chan', 0, 0, tiled=True)  5 us
    reshape x10, local copies, waits for them, and re-layouts, per_device(): g.reshape(chan_count, -1)  4.57 us
    all_to_all x1, waiting for transfers between devices, gather_chan(): gathered = lax.all_to_all(copies, 'chan', 0, 0, tiled=True)  3.79 us
  transfers between devices with their start and end apart: 3, of which 3 were waited for; matrix products, arithmetic and copies ran while one was open for 1% of the time, Pallas kernels for 0%

profile of v8, /device:TPU:1, one launch (start us, length us, event | category | flops | bytes accessed | tf_op | source)
XLA Modules:
  0.0 140.7 jit_solution(5578292550170849740)
XLA Ops:
  0.7 0.8 reshape.513
  1.6 0.9 reshape.519
  4.0 0.9 broadcast_in_dim.220
  4.9 5.0 %all-to-all-start = ((f32[4,1,21000]{2,1,0:T(1,128)}), f32[4,1,21000]{2,1,0:T(1,128)S(1)}, u32[]{:S(2)}, u32[]{:S(2)}) async-start(f32[4,1,21000]{2,1,0:T(1,128)} %broadcast_in_dim.220), calls=%async_computation | async-start | bytes 675840 | tf_op jit(solution)/shard_map/all_to_all | solution.py:78
  12.0 3.8 %all-to-all-done = f32[4,1,21000]{2,1,0:T(1,128)S(1)} async-done(((f32[4,1,21000]{2,1,0:T(1,128)}), f32[4,1,21000]{2,1,0:T(1,128)S(1)}, u32[]{:S(2)}, u32[]{:S(2)}) %all-to-all-start) | async-done | bytes 336032 | tf_op jit(solution)/shard_map/all_to_all | solution.py:78
  19.6 0.9 multiply_reduce_fusion.48
  20.7 1.3 fusion.3
  23.3 8.6 %all-to-all-start.1 = ((f32[8,4,99]{2,1,0:T(4,128)}), f32[8,4,99]{2,1,0:T(4,128)S(1)}, u32[]{:S(2)}, u32[]{:S(2)}) async-start(f32[8,4,99]{2,1,0:T(4,128)} %broadcast_in_dim.223), calls=%async_computation.1 | async-start | bytes 32768 | tf_op jit(solution)/shard_map/all_to_all | solution.py:61
  32.4 6.2 %all-to-all-done.1 = f32[8,4,99]{2,1,0:T(4,128)S(1)} async-done(((f32[8,4,99]{2,1,0:T(4,128)}), f32[8,4,99]{2,1,0:T(4,128)S(1)}, u32[]{:S(2)}, u32[]{:S(2)}) %all-to-all-start.1) | async-done | bytes 12704 | tf_op jit(solution)/shard_map/all_to_all | solution.py:61
  38.6 0.7 broadcast_in_dim.225
  39.3 4.7 %all-to-all-start.2 = ((f32[16,32,99]{2,1,0:T(8,128)}), f32[16,32,99]{2,1,0:T(8,128)S(1)}, u32[]{:S(2)}, u32[]{:S(2)}) async-start(f32[16,32,99]{2,1,0:T(8,128)} %broadcast_in_dim.225), calls=%async_computation.2 | async-start | bytes 524288 | tf_op jit(solution)/shard_map/all_to_all | solution.py:61
  44.0 7.5 %all-to-all-done.2 = f32[16,32,99]{2,1,0:T(8,128)S(1)} async-done(((f32[16,32,99]{2,1,0:T(8,128)}), f32[16,32,99]{2,1,0:T(8,128)S(1)}, u32[]{:S(2)}, u32[]{:S(2)}) %all-to-all-start.2) | async-done | bytes 202784 | tf_op jit(solution)/shard_map/all_to_all | solution.py:61
  52.2 0.8 gather_fusion
  53.4 1.3 multiply_reduce_fusion.53
  55.5 0.8 fusion.11
  56.3 1.2 fusion.53
  57.5 1.1 multiply_reduce_fusion.49
  58.7 0.8 fusion.13
  59.5 0.7 fusion.47
  60.3 0.8 multiply_reduce_fusion.45
  61.2 1.0 multiply_reduce_fusion.46
  62.1 0.9 multiply_reduce_fusion.47
  63.3 1.2 broadcast_multiply_fusion.1
  64.5 1.4 %broadcast_multiply_fusion = (f32[96,4,8,8]{0,3,2,1:T(8,128)}, f32[96,4,8,8]{0,3,2,1:T(8,128)}, f32[96,4,8,8]{0,3,2,1:T(8,128)}, f32[96,4,8,8]{0,3,2,1:T(8,128)}...) fusion(f32[96,4,8,8]{0,3,2,1:T(8,128)S(1)} %bitcast.161, ...), kind=kLoop, calls=%fused_computation.160 | loop fusion | flops 442368 | bytes 1874688 | tf_op jit(solution)/shard_map/transpose(jvp())/mul | solution.py:25
  74.5 1.5 %pad_add_fusion.7 = f32[96,49]{0,1:T(8,128)} fusion(f32[96,1]{0,1:T(1,128)S(1)} %bitcast.188, f32[96,1]{0,1:T(1,128)S(1)} %bitcast.208, f32[96,1]{0,1:T(1,128)S(1)} %bitcast.209, f32[96,1]{0,1:T(1,128)S(1)} %bitcast.210, f32[96,1]{0,1:T(1,128)S(1)} %bitcast.211, f32[96,1]{0,1:T(1,128)} %bitcast.212, f32[96,1]{0,1:T(1,128)} %bitcast.213, ...), kind=kLoop, calls=%fused_computation.267 | loop fusion | flops 225792 | bytes 37632 | tf_op jit(solution)/shard_map/transpose(jvp())/add_any | solution.py:22
  76.0 0.8 copy.134
  76.9 0.7 reshape.538
  77.6 3.2 %pad_add_fusion = f32[96,4,14,14]{0,3,2,1:T(8,128)S(1)} fusion(f32[96,4,8,8]{0,3,2,1:T(8,128)} %get-tuple-element.142, f32[96,4,8,8]{0,3,2,1:T(8,128)} %get-tuple-element.143, f32[96,4,8,8]{0,3,2,1:T(8,128)} %get-tuple-element.144, f32[96,4,8,8]{0,3,2,1:T(8,128)} %get-tuple-element.145, f32[96,4,8,8]{0,3,2,1:T(8,128)} %get-tuple-element.146, ...), kind=kLoop, calls=%fused_computation.60 | loop fusion | flops 3161088 | bytes 4528128 | tf_op jit(solution)/shard_map/transpose(jvp())/add_any | solution.py:26
  84.0 0.8 all_to_all.30
  84.8 18.3 %all_to_all.40 = f32[8,1,21001]{2,1,0:T(1,128)S(1)} all-to-all(f32[8,1,21001]{2,1,0:T(1,128)S(1)} %all_to_all.30), channel_id=1, replica_groups=mesh['dp'=2,'tx'=4,'tz'=8,'chan'=4] {'dp','chan'}, dimensions={0} | all-to-all | bytes 1344064 | tf_op jit(solution)/shard_map/all_to_all | solution.py:71
  103.8 9.3 %all_to_all.41 = f32[4,1,21001]{2,1,0:T(1,128)S(1)} all-to-all(f32[4,1,21001]{2,1,0:T(1,128)S(1)} %broadcast_in_dim.282), channel_id=1, replica_groups=mesh['dp'=2,'tx'=4,'tz'=8,'chan'=4] {'tx'}, dimensions={0} | all-to-all | bytes 672032 | tf_op jit(solution)/shard_map/all_to_all | solution.py:55
  113.8 21.7 %all_to_all.42 = f32[8,1,21001]{2,1,0:T(1,128)S(1)} all-to-all(f32[8,1,21001]{2,1,0:T(1,128)S(1)} %broadcast_in_dim.283), channel_id=1, replica_groups=mesh['dp'=2,'tx'=4,'tz'=8,'chan'=4] {'tz'}, dimensions={0} | all-to-all | bytes 1344064 | tf_op jit(solution)/shard_map/all_to_all | solution.py:55
  (236 shorter events, 27.8 us)
Async XLA Ops:
  0.6 18.4 %copy-start = (f32[48,1024]{1,0:T(8,128)S(1)}, f32[48,1024]{1,0:T(8,128)}, u32[]{:S(2)}) copy-start(f32[48,1024]{1,0:T(8,128)} %param.17) | copy-start | bytes 589828
  0.7 0.8 copy-start.16
  1.5 1.0 copy-start.13
  4.9 10.9 %all-to-all-start = ((f32[4,1,21000]{2,1,0:T(1,128)}), f32[4,1,21000]{2,1,0:T(1,128)S(1)}, u32[]{:S(2)}, u32[]{:S(2)}) async-start(f32[4,1,21000]{2,1,0:T(1,128)} %broadcast_in_dim.220), calls=%async_computation | async-start | bytes 675840 | tf_op jit(solution)/shard_map/all_to_all | solution.py:78
  23.3 15.2 %all-to-all-start.1 = ((f32[8,4,99]{2,1,0:T(4,128)}), f32[8,4,99]{2,1,0:T(4,128)S(1)}, u32[]{:S(2)}, u32[]{:S(2)}) async-start(f32[8,4,99]{2,1,0:T(4,128)} %broadcast_in_dim.223), calls=%async_computation.1 | async-start | bytes 32768 | tf_op jit(solution)/shard_map/all_to_all | solution.py:61
  39.3 12.3 %all-to-all-start.2 = ((f32[16,32,99]{2,1,0:T(8,128)}), f32[16,32,99]{2,1,0:T(8,128)S(1)}, u32[]{:S(2)}, u32[]{:S(2)}) async-start(f32[16,32,99]{2,1,0:T(8,128)} %broadcast_in_dim.225), calls=%async_computation.2 | async-start | bytes 524288 | tf_op jit(solution)/shard_map/all_to_all | solution.py:61
  64.5 1.4 %copy-start.61 = (f32[96]{0:T(128)S(1)}, f32[96]{0:T(128)}, u32[]{:S(2)}) copy-start(f32[96]{0:T(128)} %broadcast_reduce_fusion) | copy-start | bytes 1156
  69.4 8.2 %copy-start.5 = (f32[96,4,8,8]{0,3,2,1:T(8,128)S(1)}, f32[96,4,8,8]{0,3,2,1:T(8,128)}, u32[]{:S(2)}) copy-start(f32[96,4,8,8]{0,3,2,1:T(8,128)} %get-tuple-element.162) | copy-start | bytes 294916
  73.5 0.7 copy-start.26
  73.5 0.7 copy-start.27
  73.5 0.7 copy-start.28
  73.5 0.7 copy-start.29
  73.5 0.7 copy-start.30
  73.5 0.7 copy-start.31
  73.6 0.7 copy-start.32
  73.6 0.7 copy-start.33
  73.7 0.7 copy-start.45
  73.8 3.7 %copy-start.4 = (f32[96,4,8,8]{0,3,2,1:T(8,128)S(1)}, f32[96,4,8,8]{0,3,2,1:T(8,128)}, u32[]{:S(2)}) copy-start(f32[96,4,8,8]{0,3,2,1:T(8,128)} %get-tuple-element.161) | copy-start | bytes 294916
  74.5 3.1 %copy-start.2 = (f32[96,4,8,8]{0,3,2,1:T(8,128)S(1)}, f32[96,4,8,8]{0,3,2,1:T(8,128)}, u32[]{:S(2)}) copy-start(f32[96,4,8,8]{0,3,2,1:T(8,128)} %get-tuple-element.159) | copy-start | bytes 294916
  74.5 3.1 %copy-start.3 = (f32[96,4,8,8]{0,3,2,1:T(8,128)S(1)}, f32[96,4,8,8]{0,3,2,1:T(8,128)}, u32[]{:S(2)}) copy-start(f32[96,4,8,8]{0,3,2,1:T(8,128)} %get-tuple-element.160) | copy-start | bytes 294916
  77.6 3.2 %copy-start.6 = (f32[96,4,8,8]{0,3,2,1:T(8,128)S(1)}, f32[96,4,8,8]{0,3,2,1:T(8,128)}, u32[]{:S(2)}) copy-start(f32[96,4,8,8]{0,3,2,1:T(8,128)} %get-tuple-element.136) | copy-start | bytes 294916
  77.6 3.2 %copy-start.7 = (f32[96,4,8,8]{0,3,2,1:T(8,128)S(1)}, f32[96,4,8,8]{0,3,2,1:T(8,128)}, u32[]{:S(2)}) copy-start(f32[96,4,8,8]{0,3,2,1:T(8,128)} %get-tuple-element.137) | copy-start | bytes 294916
  77.6 3.2 %copy-start.8 = (f32[96,4,8,8]{0,3,2,1:T(8,128)S(1)}, f32[96,4,8,8]{0,3,2,1:T(8,128)}, u32[]{:S(2)}) copy-start(f32[96,4,8,8]{0,3,2,1:T(8,128)} %get-tuple-element.138) | copy-start | bytes 294916
  77.6 3.2 %copy-start.9 = (f32[96,4,8,8]{0,3,2,1:T(8,128)S(1)}, f32[96,4,8,8]{0,3,2,1:T(8,128)}, u32[]{:S(2)}) copy-start(f32[96,4,8,8]{0,3,2,1:T(8,128)} %get-tuple-element.139) | copy-start | bytes 294916
  77.6 3.2 %copy-start.10 = (f32[96,4,8,8]{0,3,2,1:T(8,128)S(1)}, f32[96,4,8,8]{0,3,2,1:T(8,128)}, u32[]{:S(2)}) copy-start(f32[96,4,8,8]{0,3,2,1:T(8,128)} %get-tuple-element.140) | copy-start | bytes 294916
  77.6 3.2 %copy-start.11 = (f32[96,4,8,8]{0,3,2,1:T(8,128)S(1)}, f32[96,4,8,8]{0,3,2,1:T(8,128)}, u32[]{:S(2)}) copy-start(f32[96,4,8,8]{0,3,2,1:T(8,128)} %get-tuple-element.141) | copy-start | bytes 294916
  80.8 0.7 copy-start.15
  81.7 1.2 copy-start.20
  81.7 1.2 copy-start.21
  81.7 1.2 copy-start.22
  82.1 0.8 copy-start.12
  82.2 0.7 copy-start.19
  (45 other events, 30.0 us)

commit v9 on v8

--- a/solution.py
+++ b/solution.py
@@ -186,9 +186,13 @@
     flat = jnp.concatenate(
         [flat, jnp.where(lead & (chan == 0), loss_part, 0.0) * jnp.ones((chan_count, 1))], axis=1
     )
-    flat = jnp.broadcast_to(flat[None], (dp_count,) + flat.shape).reshape(-1, flat.shape[1])
+    length = flat.shape[1]
+    half = -(-length // dp_count)
+    flat = jnp.pad(flat, ((0, 0), (0, half * dp_count - length)))
+    flat = flat.reshape(chan_count, dp_count, half).transpose(1, 0, 2).reshape(-1, half)
     mine = scatter_sum(flat, ("dp", "chan"))
     mine = psum_steps(mine, ("tx", "tz"))
+    mine = gather_rows(mine[None], "dp").reshape(-1)[:length]
 
     outs = []
     offset = 0

time: 142 us -> 135 us (0.951)
  blocking collectives: 49.4 us -> 42.7 us
    all_to_all x2, blocking collectives: 31 us -> 21.6 us  [spread_sum(): return jnp.sum(lax.all_to_all(copies, axis, 0, 0, tiled=True), axis=0)]
    all_to_all x0 -> x1, blocking collectives: none -> 6.18 us  [gather_rows(): lax.all_to_all(copies, axis, 0, 0, tiled=True)]
    all_to_all x1, blocking collectives: 18.3 us -> 15 us  [scatter_sum(): return jnp.sum(lax.all_to_all(value, axis, 0, 0, tiled=True), axis=0)]
where the time goes in v9:
time: 135 us; the launch traced here: 134 us
  blocking collectives  42.7 us (32%)
  local copies, waits for them, and re-layouts  29.5 us (22%)
  starting transfers between devices  18.3 us (14%)
  waiting for transfers between devices  17.5 us (13%)
  other arithmetic  14.2 us (11%)
  matrix products  8.33 us (6%)
  between operations  3.1 us (2%)
    all_to_all x2, blocking collectives, spread_sum(): return jnp.sum(lax.all_to_all(copies, axis, 0, 0, tiled=True), axis=0)  21.6 us
    all_to_all x1, blocking collectives, scatter_sum(): return jnp.sum(lax.all_to_all(value, axis, 0, 0, tiled=True), axis=0)  15 us
    all_to_all x2, waiting for transfers between devices, gather_rows(): lax.all_to_all(copies, axis, 0, 0, tiled=True)  13.7 us
    all_to_all x2, starting transfers between devices, gather_rows(): lax.all_to_all(copies, axis, 0, 0, tiled=True)  13.3 us
    unnamed x149, local copies, waits for them, and re-layouts  7.24 us
    all_to_all x1, blocking collectives, gather_rows(): lax.all_to_all(copies, axis, 0, 0, tiled=True)  6.18 us
    all_to_all x1, starting transfers between devices, gather_chan(): gathered = lax.all_to_all(copies, 'chan', 0, 0, tiled=True)  5 us
    reshape x10, local copies, waits for them, and re-layouts, per_device(): g.reshape(chan_count, -1)  4.57 us
  transfers between devices with their start and end apart: 3, of which 3 were waited for; matrix products, arithmetic and copies ran while one was open for 1% of the time, Pallas kernels for 0%

profile of v9, /device:TPU:1, one launch (start us, length us, event | category | flops | bytes accessed | tf_op | source)
XLA Modules:
  0.0 133.7 jit_solution(3178997116382196579)
XLA Ops:
  0.7 0.8 reshape.518
  1.6 0.9 reshape.524
  4.0 0.9 broadcast_in_dim.219
  4.9 5.0 %all-to-all-start = ((f32[4,1,21000]{2,1,0:T(1,128)}), f32[4,1,21000]{2,1,0:T(1,128)S(1)}, u32[]{:S(2)}, u32[]{:S(2)}) async-start(f32[4,1,21000]{2,1,0:T(1,128)} %broadcast_in_dim.219), calls=%async_computation | async-start | bytes 675840 | tf_op jit(solution)/shard_map/all_to_all | solution.py:78
  12.0 3.8 %all-to-all-done = f32[4,1,21000]{2,1,0:T(1,128)S(1)} async-done(((f32[4,1,21000]{2,1,0:T(1,128)}), f32[4,1,21000]{2,1,0:T(1,128)S(1)}, u32[]{:S(2)}, u32[]{:S(2)}) %all-to-all-start) | async-done | bytes 336032 | tf_op jit(solution)/shard_map/all_to_all | solution.py:78
  19.6 0.9 multiply_reduce_fusion.48
  20.7 1.3 fusion.3
  23.3 8.6 %all-to-all-start.1 = ((f32[8,4,99]{2,1,0:T(4,128)}), f32[8,4,99]{2,1,0:T(4,128)S(1)}, u32[]{:S(2)}, u32[]{:S(2)}) async-start(f32[8,4,99]{2,1,0:T(4,128)} %broadcast_in_dim.222), calls=%async_computation.1 | async-start | bytes 32768 | tf_op jit(solution)/shard_map/all_to_all | solution.py:61
  32.4 6.2 %all-to-all-done.1 = f32[8,4,99]{2,1,0:T(4,128)S(1)} async-done(((f32[8,4,99]{2,1,0:T(4,128)}), f32[8,4,99]{2,1,0:T(4,128)S(1)}, u32[]{:S(2)}, u32[]{:S(2)}) %all-to-all-start.1) | async-done | bytes 12704 | tf_op jit(solution)/shard_map/all_to_all | solution.py:61
  38.6 0.7 broadcast_in_dim.224
  39.3 4.7 %all-to-all-start.2 = ((f32[16,32,99]{2,1,0:T(8,128)}), f32[16,32,99]{2,1,0:T(8,128)S(1)}, u32[]{:S(2)}, u32[]{:S(2)}) async-start(f32[16,32,99]{2,1,0:T(8,128)} %broadcast_in_dim.224), calls=%async_computation.2 | async-start | bytes 524288 | tf_op jit(solution)/shard_map/all_to_all | solution.py:61
  44.0 7.5 %all-to-all-done.2 = f32[16,32,99]{2,1,0:T(8,128)S(1)} async-done(((f32[16,32,99]{2,1,0:T(8,128)}), f32[16,32,99]{2,1,0:T(8,128)S(1)}, u32[]{:S(2)}, u32[]{:S(2)}) %all-to-all-start.2) | async-done | bytes 202784 | tf_op jit(solution)/shard_map/all_to_all | solution.py:61
  52.2 0.8 gather_fusion
  53.4 1.3 multiply_reduce_fusion.53
  55.5 0.8 fusion.11
  56.3 1.2 fusion.53
  57.5 1.1 multiply_reduce_fusion.49
  58.7 0.8 fusion.13
  59.5 0.7 fusion.47
  60.3 0.8 multiply_reduce_fusion.45
  61.2 1.0 multiply_reduce_fusion.46
  62.1 0.9 multiply_reduce_fusion.47
  63.3 1.2 broadcast_multiply_fusion.1
  64.5 1.4 %broadcast_multiply_fusion = (f32[96,4,8,8]{0,3,2,1:T(8,128)}, f32[96,4,8,8]{0,3,2,1:T(8,128)}, f32[96,4,8,8]{0,3,2,1:T(8,128)}, f32[96,4,8,8]{0,3,2,1:T(8,128)}...) fusion(f32[96,4,8,8]{0,3,2,1:T(8,128)S(1)} %bitcast.164, ...), kind=kLoop, calls=%fused_computation.161 | loop fusion | flops 442368 | bytes 1874688 | tf_op jit(solution)/shard_map/transpose(jvp())/mul | solution.py:25
  74.5 1.5 %pad_add_fusion.7 = f32[96,49]{0,1:T(8,128)} fusion(f32[96,1]{0,1:T(1,128)S(1)} %bitcast.192, f32[96,1]{0,1:T(1,128)S(1)} %bitcast.212, f32[96,1]{0,1:T(1,128)S(1)} %bitcast.213, f32[96,1]{0,1:T(1,128)S(1)} %bitcast.214, f32[96,1]{0,1:T(1,128)S(1)} %bitcast.215, f32[96,1]{0,1:T(1,128)} %bitcast.216, f32[96,1]{0,1:T(1,128)} %bitcast.217, ...), kind=kLoop, calls=%fused_computation.268 | loop fusion | flops 225792 | bytes 37632 | tf_op jit(solution)/shard_map/transpose(jvp())/add_any | solution.py:22
  76.0 0.8 copy.140
  76.9 0.7 reshape.543
  77.6 3.2 %pad_add_fusion = f32[96,4,14,14]{0,3,2,1:T(8,128)S(1)} fusion(f32[96,4,8,8]{0,3,2,1:T(8,128)} %get-tuple-element.142, f32[96,4,8,8]{0,3,2,1:T(8,128)} %get-tuple-element.143, f32[96,4,8,8]{0,3,2,1:T(8,128)} %get-tuple-element.144, f32[96,4,8,8]{0,3,2,1:T(8,128)} %get-tuple-element.145, f32[96,4,8,8]{0,3,2,1:T(8,128)} %get-tuple-element.146, ...), kind=kLoop, calls=%fused_computation.60 | loop fusion | flops 3161088 | bytes 4528128 | tf_op jit(solution)/shard_map/transpose(jvp())/add_any | solution.py:26
  84.8 15.0 %all_to_all.46 = f32[8,1,10501]{2,1,0:T(1,128)S(1)} all-to-all(f32[8,1,10501]{2,1,0:T(1,128)S(1)} %all_to_all.38), channel_id=1, replica_groups=mesh['dp'=2,'tx'=4,'tz'=8,'chan'=4] {'dp','chan'}, dimensions={0} | all-to-all | bytes 672064 | tf_op jit(solution)/shard_map/all_to_all | solution.py:71
  100.2 7.4 %all_to_all.47 = f32[4,1,10501]{2,1,0:T(1,128)S(1)} all-to-all(f32[4,1,10501]{2,1,0:T(1,128)S(1)} %broadcast_in_dim.280), channel_id=1, replica_groups=mesh['dp'=2,'tx'=4,'tz'=8,'chan'=4] {'tx'}, dimensions={0} | all-to-all | bytes 336032 | tf_op jit(solution)/shard_map/all_to_all | solution.py:55
  108.0 14.1 %all_to_all.48 = f32[8,1,10501]{2,1,0:T(1,128)S(1)} all-to-all(f32[8,1,10501]{2,1,0:T(1,128)S(1)} %broadcast_in_dim.281), channel_id=1, replica_groups=mesh['dp'=2,'tx'=4,'tz'=8,'chan'=4] {'tz'}, dimensions={0} | all-to-all | bytes 672064 | tf_op jit(solution)/shard_map/all_to_all | solution.py:55
  122.4 6.2 %all_to_all.49 = f32[2,1,10501]{2,1,0:T(1,128)S(1)} all-to-all(f32[2,1,10501]{2,1,0:T(1,128)S(1)} %broadcast_in_dim.282), channel_id=1, replica_groups=mesh['dp'=2,'tx'=4,'tz'=8,'chan'=4] {'dp'}, dimensions={0} | all-to-all | bytes 168016 | tf_op jit(solution)/shard_map/all_to_all | solution.py:61
  (242 shorter events, 28.2 us)
Async XLA Ops:
  0.6 18.4 %copy-start = (f32[48,1024]{1,0:T(8,128)S(1)}, f32[48,1024]{1,0:T(8,128)}, u32[]{:S(2)}) copy-start(f32[48,1024]{1,0:T(8,128)} %param.17) | copy-start | bytes 589828
  0.7 0.8 copy-start.16
  1.5 1.0 copy-start.13
  4.9 10.9 %all-to-all-start = ((f32[4,1,21000]{2,1,0:T(1,128)}), f32[4,1,21000]{2,1,0:T(1,128)S(1)}, u32[]{:S(2)}, u32[]{:S(2)}) async-start(f32[4,1,21000]{2,1,0:T(1,128)} %broadcast_in_dim.219), calls=%async_computation | async-start | bytes 675840 | tf_op jit(solution)/shard_map/all_to_all | solution.py:78
  23.3 15.2 %all-to-all-start.1 = ((f32[8,4,99]{2,1,0:T(4,128)}), f32[8,4,99]{2,1,0:T(4,128)S(1)}, u32[]{:S(2)}, u32[]{:S(2)}) async-start(f32[8,4,99]{2,1,0:T(4,128)} %broadcast_in_dim.222), calls=%async_computation.1 | async-start | bytes 32768 | tf_op jit(solution)/shard_map/all_to_all | solution.py:61
  39.3 12.3 %all-to-all-start.2 = ((f32[16,32,99]{2,1,0:T(8,128)}), f32[16,32,99]{2,1,0:T(8,128)S(1)}, u32[]{:S(2)}, u32[]{:S(2)}) async-start(f32[16,32,99]{2,1,0:T(8,128)} %broadcast_in_dim.224), calls=%async_computation.2 | async-start | bytes 524288 | tf_op jit(solution)/shard_map/all_to_all | solution.py:61
  64.5 1.4 %copy-start.61 = (f32[96]{0:T(128)S(1)}, f32[96]{0:T(128)}, u32[]{:S(2)}) copy-start(f32[96]{0:T(128)} %broadcast_reduce_fusion) | copy-start | bytes 1156
  69.4 8.2 %copy-start.5 = (f32[96,4,8,8]{0,3,2,1:T(8,128)S(1)}, f32[96,4,8,8]{0,3,2,1:T(8,128)}, u32[]{:S(2)}) copy-start(f32[96,4,8,8]{0,3,2,1:T(8,128)} %get-tuple-element.161) | copy-start | bytes 294916
  73.5 0.7 copy-start.26
  73.5 0.7 copy-start.27
  73.5 0.7 copy-start.28
  73.5 0.7 copy-start.29
  73.5 0.7 copy-start.30
  73.5 0.7 copy-start.31
  73.6 0.7 copy-start.32
  73.6 0.7 copy-start.33
  73.7 0.7 copy-start.45
  73.8 3.7 %copy-start.4 = (f32[96,4,8,8]{0,3,2,1:T(8,128)S(1)}, f32[96,4,8,8]{0,3,2,1:T(8,128)}, u32[]{:S(2)}) copy-start(f32[96,4,8,8]{0,3,2,1:T(8,128)} %get-tuple-element.160) | copy-start | bytes 294916
  74.5 3.1 %copy-start.2 = (f32[96,4,8,8]{0,3,2,1:T(8,128)S(1)}, f32[96,4,8,8]{0,3,2,1:T(8,128)}, u32[]{:S(2)}) copy-start(f32[96,4,8,8]{0,3,2,1:T(8,128)} %get-tuple-element.158) | copy-start | bytes 294916
  74.5 3.1 %copy-start.3 = (f32[96,4,8,8]{0,3,2,1:T(8,128)S(1)}, f32[96,4,8,8]{0,3,2,1:T(8,128)}, u32[]{:S(2)}) copy-start(f32[96,4,8,8]{0,3,2,1:T(8,128)} %get-tuple-element.159) | copy-start | bytes 294916
  77.6 3.2 %copy-start.6 = (f32[96,4,8,8]{0,3,2,1:T(8,128)S(1)}, f32[96,4,8,8]{0,3,2,1:T(8,128)}, u32[]{:S(2)}) copy-start(f32[96,4,8,8]{0,3,2,1:T(8,128)} %get-tuple-element.136) | copy-start | bytes 294916
  77.6 3.2 %copy-start.7 = (f32[96,4,8,8]{0,3,2,1:T(8,128)S(1)}, f32[96,4,8,8]{0,3,2,1:T(8,128)}, u32[]{:S(2)}) copy-start(f32[96,4,8,8]{0,3,2,1:T(8,128)} %get-tuple-element.137) | copy-start | bytes 294916
  77.6 3.2 %copy-start.8 = (f32[96,4,8,8]{0,3,2,1:T(8,128)S(1)}, f32[96,4,8,8]{0,3,2,1:T(8,128)}, u32[]{:S(2)}) copy-start(f32[96,4,8,8]{0,3,2,1:T(8,128)} %get-tuple-element.138) | copy-start | bytes 294916
  77.6 3.2 %copy-start.9 = (f32[96,4,8,8]{0,3,2,1:T(8,128)S(1)}, f32[96,4,8,8]{0,3,2,1:T(8,128)}, u32[]{:S(2)}) copy-start(f32[96,4,8,8]{0,3,2,1:T(8,128)} %get-tuple-element.139) | copy-start | bytes 294916
  77.6 3.2 %copy-start.10 = (f32[96,4,8,8]{0,3,2,1:T(8,128)S(1)}, f32[96,4,8,8]{0,3,2,1:T(8,128)}, u32[]{:S(2)}) copy-start(f32[96,4,8,8]{0,3,2,1:T(8,128)} %get-tuple-element.140) | copy-start | bytes 294916
  77.6 3.2 %copy-start.11 = (f32[96,4,8,8]{0,3,2,1:T(8,128)S(1)}, f32[96,4,8,8]{0,3,2,1:T(8,128)}, u32[]{:S(2)}) copy-start(f32[96,4,8,8]{0,3,2,1:T(8,128)} %get-tuple-element.141) | copy-start | bytes 294916
  80.8 0.7 copy-start.15
  81.7 1.2 copy-start.20
  81.7 1.2 copy-start.21
  81.7 1.2 copy-start.22
  82.1 0.8 copy-start.12
  82.2 0.7 copy-start.19
  (45 other events, 30.0 us)

commit v10 on v9

--- a/solution.py
+++ b/solution.py
@@ -153,18 +153,15 @@
         ],
         axis=1,
     )
-    rows = gather_rows(gather_rows(rows, "tz"), ("chan", "tx"))
+    rows = gather_rows(rows, ("chan", "tx", "tz"))
     width = pooled.shape[0]
     onehot_all = (
         rows[:, width : width + 1] == jnp.arange(group_slides, dtype=jnp.float32)[None, :]
     ).astype(jnp.float32) * rows[:, width + 1 : width + 2]
     sums = jnp.dot(onehot_all.T, rows[:, :width], precision=highest)
     counts = jnp.maximum(jnp.sum(onehot_all, axis=0), 1.0)
-    z_count = lax.psum(1, "tz")
     tile_of = np.arange(group_slides) // slide_dev
-    where = (tile_of // z_count) * (slots * z_count) + (tile_of % z_count) * slots + (
-        np.arange(group_slides) % slide_dev
-    )
+    where = tile_of * slots + np.arange(group_slides) % slide_dev
     target_all = rows[where, width + 2]
 
     slide_feat = sums / counts[:, None]

time: 135 us -> 131 us (0.970)
  blocking collectives: 42.7 us -> 41 us
  waiting for transfers between devices: 17.5 us -> 15.9 us
    all_to_all x1, blocking collectives: 15 us -> 13.3 us  [scatter_sum(): return jnp.sum(lax.all_to_all(value, axis, 0, 0, tiled=True), axis=0)]
    all_to_all x2 -> x1, waiting for transfers between devices: 13.7 us -> 12.2 us  [gather_rows(): lax.all_to_all(copies, axis, 0, 0, tiled=True)]
    all_to_all x2 -> x1, starting transfers between devices: 13.3 us -> 14.1 us  [gather_rows(): lax.all_to_all(copies, axis, 0, 0, tiled=True)]
  transfers between devices with their start and end apart: 3 -> 2, of which waited for: 3 -> 2; matrix products, arithmetic and copies ran while one was open for 1% -> 1% of each run, Pallas kernels for 0% -> 0%
where the time goes in v10:
time: 131 us
  blocking collectives  41 us (31%)
  local copies, waits for them, and re-layouts  28.9 us (22%)
  starting transfers between devices  19.1 us (15%)
  waiting for transfers between devices  15.9 us (12%)
  other arithmetic  14.2 us (11%)
  matrix products  8.33 us (6%)
  between operations  3.1 us (2%)
    all_to_all x2, blocking collectives, spread_sum(): return jnp.sum(lax.all_to_all(copies, axis, 0, 0, tiled=True), axis=0)  21.6 us
    all_to_all x1, starting transfers between devices, gather_rows(): lax.all_to_all(copies, axis, 0, 0, tiled=True)  14.1 us
    all_to_all x1, blocking collectives, scatter_sum(): return jnp.sum(lax.all_to_all(value, axis, 0, 0, tiled=True), axis=0)  13.3 us
    all_to_all x1, waiting for transfers between devices, gather_rows(): lax.all_to_all(copies, axis, 0, 0, tiled=True)  12.2 us
    unnamed x149, local copies, waits for them, and re-layouts  7.24 us
    all_to_all x1, blocking collectives, gather_rows(): lax.all_to_all(copies, axis, 0, 0, tiled=True)  6.18 us
    all_to_all x1, starting transfers between devices, gather_chan(): gathered = lax.all_to_all(copies, 'chan', 0, 0, tiled=True)  5 us
    reshape x10, local copies, waits for them, and re-layouts, per_device(): g.reshape(chan_count, -1)  4.57 us
  transfers between devices with their start and end apart: 2, of which 2 were waited for; matrix products, arithmetic and copies ran while one was open for 1% of the time, Pallas kernels for 0%

profile of v10, /device:TPU:1, one launch (start us, length us, event | category | flops | bytes accessed | tf_op | source)
XLA Modules:
  0.0 130.6 jit_solution(12095956495865632630)
XLA Ops:
  0.7 0.8 reshape.517
  1.6 0.9 reshape.523
  4.0 0.9 broadcast_in_dim.212
  4.9 5.0 %all-to-all-start = ((f32[4,1,21000]{2,1,0:T(1,128)}), f32[4,1,21000]{2,1,0:T(1,128)S(1)}, u32[]{:S(2)}, u32[]{:S(2)}) async-start(f32[4,1,21000]{2,1,0:T(1,128)} %broadcast_in_dim.212), calls=%async_computation | async-start | bytes 675840 | tf_op jit(solution)/shard_map/all_to_all | solution.py:78
  12.0 3.8 %all-to-all-done = f32[4,1,21000]{2,1,0:T(1,128)S(1)} async-done(((f32[4,1,21000]{2,1,0:T(1,128)}), f32[4,1,21000]{2,1,0:T(1,128)S(1)}, u32[]{:S(2)}, u32[]{:S(2)}) %all-to-all-start) | async-done | bytes 336032 | tf_op jit(solution)/shard_map/all_to_all | solution.py:78
  16.9 0.7 slice_reduce_fusion.49
  19.6 0.9 multiply_reduce_fusion.48
  20.7 1.3 fusion.3
  22.7 0.7 broadcast_in_dim.215
  23.5 14.1 %all-to-all-start.1 = ((f32[128,4,99]{2,1,0:T(4,128)}), f32[128,4,99]{2,1,0:T(4,128)S(1)}, u32[]{:S(2)}, u32[]{:S(2)}) async-start(f32[128,4,99]{2,1,0:T(4,128)} %broadcast_in_dim.215), calls=%async_computation.1 | async-start | bytes 524288 | tf_op jit(solution)/shard_map/all_to_all | solution.py:61
  38.0 12.2 %all-to-all-done.1 = f32[128,4,99]{2,1,0:T(4,128)S(1)} async-done(((f32[128,4,99]{2,1,0:T(4,128)}), f32[128,4,99]{2,1,0:T(4,128)S(1)}, u32[]{:S(2)}, u32[]{:S(2)}) %all-to-all-start.1) | async-done | bytes 202784 | tf_op jit(solution)/shard_map/all_to_all | solution.py:61
  50.8 0.8 gather_fusion
  52.1 1.3 multiply_reduce_fusion.53
  54.2 0.8 fusion.11
  55.0 1.2 fusion.53
  56.1 1.1 multiply_reduce_fusion.49
  57.3 0.8 fusion.13
  58.2 0.7 fusion.47
  59.0 0.8 multiply_reduce_fusion.45
  59.8 1.0 multiply_reduce_fusion.46
  60.8 0.9 multiply_reduce_fusion.47
  61.9 1.2 broadcast_multiply_fusion.1
  63.1 1.4 %broadcast_multiply_fusion = (f32[96,4,8,8]{0,3,2,1:T(8,128)}, f32[96,4,8,8]{0,3,2,1:T(8,128)}, f32[96,4,8,8]{0,3,2,1:T(8,128)}, f32[96,4,8,8]{0,3,2,1:T(8,128)}...) fusion(f32[96,4,8,8]{0,3,2,1:T(8,128)S(1)} %bitcast.163, ...), kind=kLoop, calls=%fused_computation.161 | loop fusion | flops 442368 | bytes 1874688 | tf_op jit(solution)/shard_map/transpose(jvp())/mul | solution.py:25
  73.1 1.5 %pad_add_fusion.7 = f32[96,49]{0,1:T(8,128)} fusion(f32[96,1]{0,1:T(1,128)S(1)} %bitcast.190, f32[96,1]{0,1:T(1,128)S(1)} %bitcast.210, f32[96,1]{0,1:T(1,128)S(1)} %bitcast.211, f32[96,1]{0,1:T(1,128)S(1)} %bitcast.212, f32[96,1]{0,1:T(1,128)S(1)} %bitcast.213, f32[96,1]{0,1:T(1,128)} %bitcast.214, f32[96,1]{0,1:T(1,128)} %bitcast.215, ...), kind=kLoop, calls=%fused_computation.268 | loop fusion | flops 225792 | bytes 37632 | tf_op jit(solution)/shard_map/transpose(jvp())/add_any | solution.py:22
  74.6 0.8 copy.140
  75.5 0.7 reshape.542
  76.3 3.2 %pad_add_fusion = f32[96,4,14,14]{0,3,2,1:T(8,128)S(1)} fusion(f32[96,4,8,8]{0,3,2,1:T(8,128)} %get-tuple-element.142, f32[96,4,8,8]{0,3,2,1:T(8,128)} %get-tuple-element.143, f32[96,4,8,8]{0,3,2,1:T(8,128)} %get-tuple-element.144, f32[96,4,8,8]{0,3,2,1:T(8,128)} %get-tuple-element.145, f32[96,4,8,8]{0,3,2,1:T(8,128)} %get-tuple-element.146, ...), kind=kLoop, calls=%fused_computation.60 | loop fusion | flops 3161088 | bytes 4528128 | tf_op jit(solution)/shard_map/transpose(jvp())/add_any | solution.py:26
  83.5 13.3 %all_to_all.41 = f32[8,1,10501]{2,1,0:T(1,128)S(1)} all-to-all(f32[8,1,10501]{2,1,0:T(1,128)S(1)} %all_to_all.34), channel_id=1, replica_groups=mesh['dp'=2,'tx'=4,'tz'=8,'chan'=4] {'dp','chan'}, dimensions={0} | all-to-all | bytes 672064 | tf_op jit(solution)/shard_map/all_to_all | solution.py:71
  97.1 7.4 %all_to_all.42 = f32[4,1,10501]{2,1,0:T(1,128)S(1)} all-to-all(f32[4,1,10501]{2,1,0:T(1,128)S(1)} %broadcast_in_dim.271), channel_id=1, replica_groups=mesh['dp'=2,'tx'=4,'tz'=8,'chan'=4] {'tx'}, dimensions={0} | all-to-all | bytes 336032 | tf_op jit(solution)/shard_map/all_to_all | solution.py:55
  104.9 14.1 %all_to_all.43 = f32[8,1,10501]{2,1,0:T(1,128)S(1)} all-to-all(f32[8,1,10501]{2,1,0:T(1,128)S(1)} %broadcast_in_dim.272), channel_id=1, replica_groups=mesh['dp'=2,'tx'=4,'tz'=8,'chan'=4] {'tz'}, dimensions={0} | all-to-all | bytes 672064 | tf_op jit(solution)/shard_map/all_to_all | solution.py:55
  119.3 6.2 %all_to_all.44 = f32[2,1,10501]{2,1,0:T(1,128)S(1)} all-to-all(f32[2,1,10501]{2,1,0:T(1,128)S(1)} %broadcast_in_dim.273), channel_id=1, replica_groups=mesh['dp'=2,'tx'=4,'tz'=8,'chan'=4] {'dp'}, dimensions={0} | all-to-all | bytes 168016 | tf_op jit(solution)/shard_map/all_to_all | solution.py:61
  129.2 0.7 reshape.555
  (239 shorter events, 26.2 us)
Async XLA Ops:
  0.6 18.4 %copy-start = (f32[48,1024]{1,0:T(8,128)S(1)}, f32[48,1024]{1,0:T(8,128)}, u32[]{:S(2)}) copy-start(f32[48,1024]{1,0:T(8,128)} %param.17) | copy-start | bytes 589828
  0.7 0.8 copy-start.16
  1.5 1.0 copy-start.13
  4.9 10.9 %all-to-all-start = ((f32[4,1,21000]{2,1,0:T(1,128)}), f32[4,1,21000]{2,1,0:T(1,128)S(1)}, u32[]{:S(2)}, u32[]{:S(2)}) async-start(f32[4,1,21000]{2,1,0:T(1,128)} %broadcast_in_dim.212), calls=%async_computation | async-start | bytes 675840 | tf_op jit(solution)/shard_map/all_to_all | solution.py:78
  23.5 26.7 %all-to-all-start.1 = ((f32[128,4,99]{2,1,0:T(4,128)}), f32[128,4,99]{2,1,0:T(4,128)S(1)}, u32[]{:S(2)}, u32[]{:S(2)}) async-start(f32[128,4,99]{2,1,0:T(4,128)} %broadcast_in_dim.215), calls=%async_computation.1 | async-start | bytes 524288 | tf_op jit(solution)/shard_map/all_to_all | solution.py:61
  63.1 1.4 %copy-start.61 = (f32[96]{0:T(128)S(1)}, f32[96]{0:T(128)}, u32[]{:S(2)}) copy-start(f32[96]{0:T(128)} %broadcast_reduce_fusion) | copy-start | bytes 1156
  68.0 8.2 %copy-start.5 = (f32[96,4,8,8]{0,3,2,1:T(8,128)S(1)}, f32[96,4,8,8]{0,3,2,1:T(8,128)}, u32[]{:S(2)}) copy-start(f32[96,4,8,8]{0,3,2,1:T(8,128)} %get-tuple-element.161) | copy-start | bytes 294916
  72.1 0.7 copy-start.26
  72.1 0.7 copy-start.27
  72.1 0.7 copy-start.28
  72.1 0.7 copy-start.29
  72.2 0.7 copy-start.30
  72.2 0.7 copy-start.31
  72.2 0.7 copy-start.32
  72.2 0.7 copy-start.33
  72.2 0.7 copy-start.39
  72.3 0.7 copy-start.45
  72.5 3.7 %copy-start.4 = (f32[96,4,8,8]{0,3,2,1:T(8,128)S(1)}, f32[96,4,8,8]{0,3,2,1:T(8,128)}, u32[]{:S(2)}) copy-start(f32[96,4,8,8]{0,3,2,1:T(8,128)} %get-tuple-element.160) | copy-start | bytes 294916
  73.1 3.1 %copy-start.2 = (f32[96,4,8,8]{0,3,2,1:T(8,128)S(1)}, f32[96,4,8,8]{0,3,2,1:T(8,128)}, u32[]{:S(2)}) copy-start(f32[96,4,8,8]{0,3,2,1:T(8,128)} %get-tuple-element.158) | copy-start | bytes 294916
  73.1 3.1 %copy-start.3 = (f32[96,4,8,8]{0,3,2,1:T(8,128)S(1)}, f32[96,4,8,8]{0,3,2,1:T(8,128)}, u32[]{:S(2)}) copy-start(f32[96,4,8,8]{0,3,2,1:T(8,128)} %get-tuple-element.159) | copy-start | bytes 294916
  76.2 3.2 %copy-start.6 = (f32[96,4,8,8]{0,3,2,1:T(8,128)S(1)}, f32[96,4,8,8]{0,3,2,1:T(8,128)}, u32[]{:S(2)}) copy-start(f32[96,4,8,8]{0,3,2,1:T(8,128)} %get-tuple-element.136) | copy-start | bytes 294916
  76.2 3.2 %copy-start.7 = (f32[96,4,8,8]{0,3,2,1:T(8,128)S(1)}, f32[96,4,8,8]{0,3,2,1:T(8,128)}, u32[]{:S(2)}) copy-start(f32[96,4,8,8]{0,3,2,1:T(8,128)} %get-tuple-element.137) | copy-start | bytes 294916
  76.2 3.2 %copy-start.8 = (f32[96,4,8,8]{0,3,2,1:T(8,128)S(1)}, f32[96,4,8,8]{0,3,2,1:T(8,128)}, u32[]{:S(2)}) copy-start(f32[96,4,8,8]{0,3,2,1:T(8,128)} %get-tuple-element.138) | copy-start | bytes 294916
  76.2 3.2 %copy-start.9 = (f32[96,4,8,8]{0,3,2,1:T(8,128)S(1)}, f32[96,4,8,8]{0,3,2,1:T(8,128)}, u32[]{:S(2)}) copy-start(f32[96,4,8,8]{0,3,2,1:T(8,128)} %get-tuple-element.139) | copy-start | bytes 294916
  76.2 3.2 %copy-start.10 = (f32[96,4,8,8]{0,3,2,1:T(8,128)S(1)}, f32[96,4,8,8]{0,3,2,1:T(8,128)}, u32[]{:S(2)}) copy-start(f32[96,4,8,8]{0,3,2,1:T(8,128)} %get-tuple-element.140) | copy-start | bytes 294916
  76.3 3.2 %copy-start.11 = (f32[96,4,8,8]{0,3,2,1:T(8,128)S(1)}, f32[96,4,8,8]{0,3,2,1:T(8,128)}, u32[]{:S(2)}) copy-start(f32[96,4,8,8]{0,3,2,1:T(8,128)} %get-tuple-element.141) | copy-start | bytes 294916
  79.4 0.7 copy-start.15
  80.3 1.2 copy-start.20
  80.3 1.2 copy-start.21
  80.3 1.2 copy-start.22
  80.7 0.8 copy-start.12
  80.8 0.7 copy-start.19
  (44 other events, 29.3 us)

commit v11 on v10

--- a/solution.py
+++ b/solution.py
@@ -184,12 +184,14 @@
         [flat, jnp.where(lead & (chan == 0), loss_part, 0.0) * jnp.ones((chan_count, 1))], axis=1
     )
     length = flat.shape[1]
-    half = -(-length // dp_count)
-    flat = jnp.pad(flat, ((0, 0), (0, half * dp_count - length)))
-    flat = flat.reshape(chan_count, dp_count, half).transpose(1, 0, 2).reshape(-1, half)
-    mine = scatter_sum(flat, ("dp", "chan"))
-    mine = psum_steps(mine, ("tx", "tz"))
-    mine = gather_rows(mine[None], "dp").reshape(-1)[:length]
+    x_count = lax.psum(1, "tx")
+    pieces = dp_count * x_count
+    half = -(-length // pieces)
+    flat = jnp.pad(flat, ((0, 0), (0, half * pieces - length)))
+    flat = flat.reshape(chan_count, dp_count, x_count, half).transpose(1, 0, 2, 3)
+    mine = scatter_sum(flat.reshape(-1, half), ("dp", "chan", "tx"))
+    mine = psum_steps(mine, ("tz",))
+    mine = gather_rows(mine[None], ("dp", "tx")).reshape(-1)[:length]
 
     outs = []
     offset = 0

time: 131 us -> 124 us (0.947)
  blocking collectives: 41 us -> 34.8 us
    all_to_all x2 -> x1, blocking collectives: 21.6 us -> 9.83 us  [spread_sum(): return jnp.sum(lax.all_to_all(copies, axis, 0, 0, tiled=True), axis=0)]
    all_to_all x1, blocking collectives: 6.18 us -> 10 us  [gather_rows(): lax.all_to_all(copies, axis, 0, 0, tiled=True)]
    all_to_all x1, blocking collectives: 13.3 us -> 15 us  [scatter_sum(): return jnp.sum(lax.all_to_all(value, axis, 0, 0, tiled=True), axis=0)]
where the time goes in v11:
time: 124 us
  blocking collectives  34.8 us (28%)
  local copies, waits for them, and re-layouts  28.6 us (23%)
  starting transfers between devices  19.1 us (15%)
  waiting for transfers between devices  15.9 us (13%)
  other arithmetic  13.8 us (11%)
  matrix products  8.33 us (7%)
  between operations  3.09 us (2%)
    all_to_all x1, blocking collectives, scatter_sum(): return jnp.sum(lax.all_to_all(value, axis, 0, 0, tiled=True), axis=0)  15 us
    all_to_all x1, starting transfers between devices, gather_rows(): lax.all_to_all(copies, axis, 0, 0, tiled=True)  14.1 us
    all_to_all x1, waiting for transfers between devices, gather_rows(): lax.all_to_all(copies, axis, 0, 0, tiled=True)  12.2 us
    all_to_all x1, blocking collectives, gather_rows(): lax.all_to_all(copies, axis, 0, 0, tiled=True)  10 us
    all_to_all x1, blocking collectives, spread_sum(): return jnp.sum(lax.all_to_all(copies, axis, 0, 0, tiled=True), axis=0)  9.83 us
    unnamed x149, local copies, waits for them, and re-layouts  7.24 us
    all_to_all x1, starting transfers between devices, gather_chan(): gathered = lax.all_to_all(copies, 'chan', 0, 0, tiled=True)  5 us
    reshape x10, local copies, waits for them, and re-layouts, per_device(): g.reshape(chan_count, -1)  4.57 us
  transfers between devices with their start and end apart: 2, of which 2 were waited for; matrix products, arithmetic and copies ran while one was open for 1% of the time, Pallas kernels for 0%

profile of v11, /device:TPU:1, one launch (start us, length us, event | category | flops | bytes accessed | tf_op | source)
XLA Modules:
  0.0 123.6 jit_solution(10733833108813777426)
XLA Ops:
  0.7 0.8 reshape.511
  1.6 0.9 reshape.517
  4.0 0.9 broadcast_in_dim.206
  4.9 5.0 %all-to-all-start = ((f32[4,1,21000]{2,1,0:T(1,128)}), f32[4,1,21000]{2,1,0:T(1,128)S(1)}, u32[]{:S(2)}, u32[]{:S(2)}) async-start(f32[4,1,21000]{2,1,0:T(1,128)} %broadcast_in_dim.206), calls=%async_computation | async-start | bytes 675840 | tf_op jit(solution)/shard_map/all_to_all | solution.py:78
  12.0 3.8 %all-to-all-done = f32[4,1,21000]{2,1,0:T(1,128)S(1)} async-done(((f32[4,1,21000]{2,1,0:T(1,128)}), f32[4,1,21000]{2,1,0:T(1,128)S(1)}, u32[]{:S(2)}, u32[]{:S(2)}) %all-to-all-start) | async-done | bytes 336032 | tf_op jit(solution)/shard_map/all_to_all | solution.py:78
  16.9 0.7 slice_reduce_fusion.49
  19.6 0.9 multiply_reduce_fusion.48
  20.7 1.3 %fusion.3 = (f32[384,256]{0,1:T(8,128)S(1)}, f32[384,256]{0,1:T(8,128)S(1)}) fusion(f32[384]{0:T(512)S(1)} %add.517, f32[384,96]{1,0:T(8,128)S(1)} %reshape.524, f32[96,256]{0,1:T(8,128)S(1)} %bitcast.177), kind=kOutput, calls=%fused_computation.61 | convolution fusion | flops 119439360 | bytes 1033728 | tf_op jit(solution)/shard_map/jvp()/dot_general | solution.py:46
  22.7 0.7 broadcast_in_dim.209
  23.5 14.1 %all-to-all-start.1 = ((f32[128,4,99]{2,1,0:T(4,128)}), f32[128,4,99]{2,1,0:T(4,128)S(1)}, u32[]{:S(2)}, u32[]{:S(2)}) async-start(f32[128,4,99]{2,1,0:T(4,128)} %broadcast_in_dim.209), calls=%async_computation.1 | async-start | bytes 524288 | tf_op jit(solution)/shard_map/all_to_all | solution.py:61
  38.0 12.2 %all-to-all-done.1 = f32[128,4,99]{2,1,0:T(4,128)S(1)} async-done(((f32[128,4,99]{2,1,0:T(4,128)}), f32[128,4,99]{2,1,0:T(4,128)S(1)}, u32[]{:S(2)}, u32[]{:S(2)}) %all-to-all-start.1) | async-done | bytes 202784 | tf_op jit(solution)/shard_map/all_to_all | solution.py:61
  50.8 0.8 gather_fusion
  52.1 1.3 %multiply_reduce_fusion.53 = (f32[]{:T(128)}, f32[64]{0:T(128)S(1)}, f32[64]{0:T(128)}) fusion(f32[64]{0:T(128)S(1)} %gather_fusion, f32[64,96]{1,0:T(8,128)S(1)} %convolution_divide_fusion, f32[96,1]{0,1:T(1,128)S(1)} %reshape.556), kind=kOutput, calls=%fused_computation.292 | convolution fusion | flops 73983 | bytes 25732 | tf_op jit(solution)/shard_map/dot_general | solution.py:168
  54.2 0.8 fusion.11
  55.0 1.2 fusion.53
  56.1 1.1 multiply_reduce_fusion.49
  57.3 0.8 fusion.13
  58.2 0.7 fusion.47
  59.0 0.8 multiply_reduce_fusion.45
  59.8 1.0 multiply_reduce_fusion.46
  60.8 0.9 multiply_reduce_fusion.47
  61.9 1.2 %broadcast_multiply_fusion.1 = (f32[96,4,8,8]{0,3,2,1:T(8,128)S(1)}, f32[96,4,8,8]{0,3,2,1:T(8,128)S(1)}, f32[96,4,8,8]{0,3,2,1:T(8,128)S(1)}, f32[96,4,8,8]{0,3...) fusion(f32[96,4,8,8]{0,3,2,1:T(8,128)S(1)} %bitcast.162, ...), kind=kLoop, calls=%fused_computation.162 | loop fusion | flops 442368 | bytes 1874688 | tf_op jit(solution)/shard_map/transpose(jvp())/mul | solution.py:25
  63.1 1.4 %broadcast_multiply_fusion = (f32[96,4,8,8]{0,3,2,1:T(8,128)}, f32[96,4,8,8]{0,3,2,1:T(8,128)}, f32[96,4,8,8]{0,3,2,1:T(8,128)}, f32[96,4,8,8]{0,3,2,1:T(8,128)}...) fusion(f32[96,4,8,8]{0,3,2,1:T(8,128)S(1)} %bitcast.163, ...), kind=kLoop, calls=%fused_computation.161 | loop fusion | flops 442368 | bytes 1874688 | tf_op jit(solution)/shard_map/transpose(jvp())/mul | solution.py:25
  73.1 1.5 %pad_add_fusion.7 = f32[96,49]{0,1:T(8,128)} fusion(f32[96,1]{0,1:T(1,128)S(1)} %bitcast.190, f32[96,1]{0,1:T(1,128)S(1)} %bitcast.210, f32[96,1]{0,1:T(1,128)S(1)} %bitcast.211, f32[96,1]{0,1:T(1,128)S(1)} %bitcast.212, f32[96,1]{0,1:T(1,128)S(1)} %bitcast.213, f32[96,1]{0,1:T(1,128)} %bitcast.214, f32[96,1]{0,1:T(1,128)} %bitcast.215, ...), kind=kLoop, calls=%fused_computation.268 | loop fusion | flops 225792 | bytes 37632 | tf_op jit(solution)/shard_map/transpose(jvp())/add_any | solution.py:22
  74.6 0.8 copy.140
  75.5 0.7 reshape.536
  76.3 3.2 %pad_add_fusion = f32[96,4,14,14]{0,3,2,1:T(8,128)S(1)} fusion(f32[96,4,8,8]{0,3,2,1:T(8,128)} %get-tuple-element.142, f32[96,4,8,8]{0,3,2,1:T(8,128)} %get-tuple-element.143, f32[96,4,8,8]{0,3,2,1:T(8,128)} %get-tuple-element.144, f32[96,4,8,8]{0,3,2,1:T(8,128)} %get-tuple-element.145, f32[96,4,8,8]{0,3,2,1:T(8,128)} %get-tuple-element.146, ...), kind=kLoop, calls=%fused_computation.60 | loop fusion | flops 3161088 | bytes 4528128 | tf_op jit(solution)/shard_map/transpose(jvp())/add_any | solution.py:26
  83.4 15.0 %all_to_all.35 = f32[32,1,2626]{2,1,0:T(1,128)S(1)} all-to-all(f32[32,1,2626]{2,1,0:T(1,128)S(1)} %all_to_all.29), channel_id=1, replica_groups=mesh['dp'=2,'tx'=4,'tz'=8,'chan'=4] {'dp','chan','tx'}, dimensions={0} | all-to-all | bytes 672256 | tf_op jit(solution)/shard_map/all_to_all | solution.py:71
  98.6 9.8 %all_to_all.36 = f32[8,1,2626]{2,1,0:T(1,128)S(1)} all-to-all(f32[8,1,2626]{2,1,0:T(1,128)S(1)} %broadcast_in_dim.265), channel_id=1, replica_groups=mesh['dp'=2,'tx'=4,'tz'=8,'chan'=4] {'tz'}, dimensions={0} | all-to-all | bytes 168064 | tf_op jit(solution)/shard_map/all_to_all | solution.py:55
  108.6 10.0 %all_to_all.37 = f32[8,1,2626]{2,1,0:T(1,128)S(1)} all-to-all(f32[8,1,2626]{2,1,0:T(1,128)S(1)} %broadcast_in_dim.266), channel_id=1, replica_groups=mesh['dp'=2,'tx'=4,'tz'=8,'chan'=4] {'dp','tx'}, dimensions={0} | all-to-all | bytes 168064 | tf_op jit(solution)/shard_map/all_to_all | solution.py:61
  122.2 0.7 reshape.549
  122.9 0.7 reshape.548
  (236 shorter events, 24.7 us)
Async XLA Ops:
  0.6 18.4 %copy-start = (f32[48,1024]{1,0:T(8,128)S(1)}, f32[48,1024]{1,0:T(8,128)}, u32[]{:S(2)}) copy-start(f32[48,1024]{1,0:T(8,128)} %param.17) | copy-start | bytes 589828
  0.7 0.8 copy-start.16
  1.5 1.0 copy-start.13
  4.9 10.9 %all-to-all-start = ((f32[4,1,21000]{2,1,0:T(1,128)}), f32[4,1,21000]{2,1,0:T(1,128)S(1)}, u32[]{:S(2)}, u32[]{:S(2)}) async-start(f32[4,1,21000]{2,1,0:T(1,128)} %broadcast_in_dim.206), calls=%async_computation | async-start | bytes 675840 | tf_op jit(solution)/shard_map/all_to_all | solution.py:78
  23.5 26.7 %all-to-all-start.1 = ((f32[128,4,99]{2,1,0:T(4,128)}), f32[128,4,99]{2,1,0:T(4,128)S(1)}, u32[]{:S(2)}, u32[]{:S(2)}) async-start(f32[128,4,99]{2,1,0:T(4,128)} %broadcast_in_dim.209), calls=%async_computation.1 | async-start | bytes 524288 | tf_op jit(solution)/shard_map/all_to_all | solution.py:61
  63.1 1.4 %copy-start.61 = (f32[96]{0:T(128)S(1)}, f32[96]{0:T(128)}, u32[]{:S(2)}) copy-start(f32[96]{0:T(128)} %broadcast_reduce_fusion) | copy-start | bytes 1156
  68.0 8.2 %copy-start.5 = (f32[96,4,8,8]{0,3,2,1:T(8,128)S(1)}, f32[96,4,8,8]{0,3,2,1:T(8,128)}, u32[]{:S(2)}) copy-start(f32[96,4,8,8]{0,3,2,1:T(8,128)} %get-tuple-element.161) | copy-start | bytes 294916
  72.1 0.7 copy-start.26
  72.1 0.7 copy-start.27
  72.1 0.7 copy-start.28
  72.1 0.7 copy-start.29
  72.2 0.7 copy-start.30
  72.2 0.7 copy-start.31
  72.2 0.7 copy-start.32
  72.2 0.7 copy-start.33
  72.2 0.7 copy-start.39
  72.3 0.7 copy-start.45
  72.5 3.7 %copy-start.4 = (f32[96,4,8,8]{0,3,2,1:T(8,128)S(1)}, f32[96,4,8,8]{0,3,2,1:T(8,128)}, u32[]{:S(2)}) copy-start(f32[96,4,8,8]{0,3,2,1:T(8,128)} %get-tuple-element.160) | copy-start | bytes 294916
  73.1 3.1 %copy-start.2 = (f32[96,4,8,8]{0,3,2,1:T(8,128)S(1)}, f32[96,4,8,8]{0,3,2,1:T(8,128)}, u32[]{:S(2)}) copy-start(f32[96,4,8,8]{0,3,2,1:T(8,128)} %get-tuple-element.158) | copy-start | bytes 294916
  73.1 3.1 %copy-start.3 = (f32[96,4,8,8]{0,3,2,1:T(8,128)S(1)}, f32[96,4,8,8]{0,3,2,1:T(8,128)}, u32[]{:S(2)}) copy-start(f32[96,4,8,8]{0,3,2,1:T(8,128)} %get-tuple-element.159) | copy-start | bytes 294916
  76.2 3.2 %copy-start.6 = (f32[96,4,8,8]{0,3,2,1:T(8,128)S(1)}, f32[96,4,8,8]{0,3,2,1:T(8,128)}, u32[]{:S(2)}) copy-start(f32[96,4,8,8]{0,3,2,1:T(8,128)} %get-tuple-element.136) | copy-start | bytes 294916
  76.2 3.2 %copy-start.7 = (f32[96,4,8,8]{0,3,2,1:T(8,128)S(1)}, f32[96,4,8,8]{0,3,2,1:T(8,128)}, u32[]{:S(2)}) copy-start(f32[96,4,8,8]{0,3,2,1:T(8,128)} %get-tuple-element.137) | copy-start | bytes 294916
  76.2 3.2 %copy-start.8 = (f32[96,4,8,8]{0,3,2,1:T(8,128)S(1)}, f32[96,4,8,8]{0,3,2,1:T(8,128)}, u32[]{:S(2)}) copy-start(f32[96,4,8,8]{0,3,2,1:T(8,128)} %get-tuple-element.138) | copy-start | bytes 294916
  76.2 3.2 %copy-start.9 = (f32[96,4,8,8]{0,3,2,1:T(8,128)S(1)}, f32[96,4,8,8]{0,3,2,1:T(8,128)}, u32[]{:S(2)}) copy-start(f32[96,4,8,8]{0,3,2,1:T(8,128)} %get-tuple-element.139) | copy-start | bytes 294916
  76.2 3.2 %copy-start.10 = (f32[96,4,8,8]{0,3,2,1:T(8,128)S(1)}, f32[96,4,8,8]{0,3,2,1:T(8,128)}, u32[]{:S(2)}) copy-start(f32[96,4,8,8]{0,3,2,1:T(8,128)} %get-tuple-element.140) | copy-start | bytes 294916
  76.3 3.2 %copy-start.11 = (f32[96,4,8,8]{0,3,2,1:T(8,128)S(1)}, f32[96,4,8,8]{0,3,2,1:T(8,128)}, u32[]{:S(2)}) copy-start(f32[96,4,8,8]{0,3,2,1:T(8,128)} %get-tuple-element.141) | copy-start | bytes 294916
  79.4 0.7 copy-start.15
  80.3 1.2 copy-start.20
  80.3 1.2 copy-start.21
  80.3 1.2 copy-start.22
  80.7 0.8 copy-start.12
  80.8 0.7 copy-start.19
  (44 other events, 29.3 us)

commit v12 on v11

--- a/solution.py
+++ b/solution.py
@@ -185,13 +185,13 @@
     )
     length = flat.shape[1]
     x_count = lax.psum(1, "tx")
-    pieces = dp_count * x_count
+    z_count = lax.psum(1, "tz")
+    pieces = dp_count * x_count * z_count
     half = -(-length // pieces)
     flat = jnp.pad(flat, ((0, 0), (0, half * pieces - length)))
-    flat = flat.reshape(chan_count, dp_count, x_count, half).transpose(1, 0, 2, 3)
-    mine = scatter_sum(flat.reshape(-1, half), ("dp", "chan", "tx"))
-    mine = psum_steps(mine, ("tz",))
-    mine = gather_rows(mine[None], ("dp", "tx")).reshape(-1)[:length]
+    flat = flat.reshape(chan_count, dp_count, x_count, z_count, half).transpose(1, 0, 2, 3, 4)
+    mine = scatter_sum(flat.reshape(-1, half), ("dp", "chan", "tx", "tz"))
+    mine = gather_rows(mine[None], ("dp", "tx", "tz")).reshape(-1)[:length]
 
     outs = []
     offset = 0

time: 124 us -> 130 us (1.048)
  blocking collectives: 34.8 us -> 40.8 us
    all_to_all x1, blocking collectives: 15 us -> 26.4 us  [scatter_sum(): return jnp.sum(lax.all_to_all(value, axis, 0, 0, tiled=True), axis=0)]
    all_to_all x1 -> x0, blocking collectives: 9.83 us -> none  [spread_sum(): return jnp.sum(lax.all_to_all(copies, axis, 0, 0, tiled=True), axis=0)]
    all_to_all x1, blocking collectives: 10 us -> 14.4 us  [gather_rows(): lax.all_to_all(copies, axis, 0, 0, tiled=True)]
where the time goes in v12:
time: 130 us
  blocking collectives  40.8 us (31%)
  local copies, waits for them, and re-layouts  28.7 us (22%)
  starting transfers between devices  19.1 us (15%)
  waiting for transfers between devices  15.9 us (12%)
  other arithmetic  13.8 us (11%)
  matrix products  8.33 us (6%)
  between operations  3.08 us (2%)
    all_to_all x1, blocking collectives, scatter_sum(): return jnp.sum(lax.all_to_all(value, axis, 0, 0, tiled=True), axis=0)  26.4 us
    all_to_all x1, blocking collectives, gather_rows(): lax.all_to_all(copies, axis, 0, 0, tiled=True)  14.4 us
    all_to_all x1, starting transfers between devices, gather_rows(): lax.all_to_all(copies, axis, 0, 0, tiled=True)  14.1 us
    all_to_all x1, waiting for transfers between devices, gather_rows(): lax.all_to_all(copies, axis, 0, 0, tiled=True)  12.2 us
    unnamed x149, local copies, waits for them, and re-layouts  7.24 us
    all_to_all x1, starting transfers between devices, gather_chan(): gathered = lax.all_to_all(copies, 'chan', 0, 0, tiled=True)  5 us
    reshape x10, local copies, waits for them, and re-layouts, per_device(): g.reshape(chan_count, -1)  4.57 us
    all_to_all x1, waiting for transfers between devices, gather_chan(): gathered = lax.all_to_all(copies, 'chan', 0, 0, tiled=True)  3.79 us
  transfers between devices with their start and end apart: 2, of which 2 were waited for; matrix products, arithmetic and copies ran while one was open for 1% of the time, Pallas kernels for 0%

profile of v12, /device:TPU:1, one launch (start us, length us, event | category | flops | bytes accessed | tf_op | source)
XLA Modules:
  0.0 129.8 jit_solution(8428379182565545440)
XLA Ops:
  0.7 0.8 reshape.505
  1.6 0.9 reshape.511
  4.0 0.9 broadcast_in_dim.200
  4.9 5.0 %all-to-all-start = ((f32[4,1,21000]{2,1,0:T(1,128)}), f32[4,1,21000]{2,1,0:T(1,128)S(1)}, u32[]{:S(2)}, u32[]{:S(2)}) async-start(f32[4,1,21000]{2,1,0:T(1,128)} %broadcast_in_dim.200), calls=%async_computation | async-start | bytes 675840 | tf_op jit(solution)/shard_map/all_to_all | solution.py:78
  12.0 3.8 %all-to-all-done = f32[4,1,21000]{2,1,0:T(1,128)S(1)} async-done(((f32[4,1,21000]{2,1,0:T(1,128)}), f32[4,1,21000]{2,1,0:T(1,128)S(1)}, u32[]{:S(2)}, u32[]{:S(2)}) %all-to-all-start) | async-done | bytes 336032 | tf_op jit(solution)/shard_map/all_to_all | solution.py:78
  16.9 0.7 slice_reduce_fusion.49
  17.6 0.7 slice_reduce_fusion.50
  19.6 0.9 multiply_reduce_fusion.48
  20.7 1.3 fusion.3
  22.7 0.7 broadcast_in_dim.203
  23.5 14.1 %all-to-all-start.1 = ((f32[128,4,99]{2,1,0:T(4,128)}), f32[128,4,99]{2,1,0:T(4,128)S(1)}, u32[]{:S(2)}, u32[]{:S(2)}) async-start(f32[128,4,99]{2,1,0:T(4,128)} %broadcast_in_dim.203), calls=%async_computation.1 | async-start | bytes 524288 | tf_op jit(solution)/shard_map/all_to_all | solution.py:61
  38.0 12.2 %all-to-all-done.1 = f32[128,4,99]{2,1,0:T(4,128)S(1)} async-done(((f32[128,4,99]{2,1,0:T(4,128)}), f32[128,4,99]{2,1,0:T(4,128)S(1)}, u32[]{:S(2)}, u32[]{:S(2)}) %all-to-all-start.1) | async-done | bytes 202784 | tf_op jit(solution)/shard_map/all_to_all | solution.py:61
  50.8 0.8 gather_fusion
  52.1 1.3 multiply_reduce_fusion.53
  54.2 0.8 fusion.11
  55.0 1.2 fusion.53
  56.1 1.1 multiply_reduce_fusion.49
  57.3 0.8 fusion.13
  58.2 0.7 fusion.47
  59.0 0.8 multiply_reduce_fusion.45
  59.8 1.0 multiply_reduce_fusion.46
  60.8 0.9 multiply_reduce_fusion.47
  61.9 1.2 broadcast_multiply_fusion.1
  63.1 1.4 %broadcast_multiply_fusion = (f32[96,4,8,8]{0,3,2,1:T(8,128)}, f32[96,4,8,8]{0,3,2,1:T(8,128)}, f32[96,4,8,8]{0,3,2,1:T(8,128)}, f32[96,4,8,8]{0,3,2,1:T(8,128)}...) fusion(f32[96,4,8,8]{0,3,2,1:T(8,128)S(1)} %bitcast.163, ...), kind=kLoop, calls=%fused_computation.160 | loop fusion | flops 442368 | bytes 1874688 | tf_op jit(solution)/shard_map/transpose(jvp())/mul | solution.py:25
  73.1 1.5 %pad_add_fusion.7 = f32[96,49]{0,1:T(8,128)} fusion(f32[96,1]{0,1:T(1,128)S(1)} %bitcast.190, f32[96,1]{0,1:T(1,128)S(1)} %bitcast.210, f32[96,1]{0,1:T(1,128)S(1)} %bitcast.211, f32[96,1]{0,1:T(1,128)S(1)} %bitcast.212, f32[96,1]{0,1:T(1,128)S(1)} %bitcast.213, f32[96,1]{0,1:T(1,128)} %bitcast.214, f32[96,1]{0,1:T(1,128)} %bitcast.215, ...), kind=kLoop, calls=%fused_computation.267 | loop fusion | flops 225792 | bytes 37632 | tf_op jit(solution)/shard_map/transpose(jvp())/add_any | solution.py:22
  74.6 0.8 copy.127
  75.5 0.7 reshape.530
  76.3 3.2 %pad_add_fusion = f32[96,4,14,14]{0,3,2,1:T(8,128)S(1)} fusion(f32[96,4,8,8]{0,3,2,1:T(8,128)} %get-tuple-element.142, f32[96,4,8,8]{0,3,2,1:T(8,128)} %get-tuple-element.143, f32[96,4,8,8]{0,3,2,1:T(8,128)} %get-tuple-element.144, f32[96,4,8,8]{0,3,2,1:T(8,128)} %get-tuple-element.145, f32[96,4,8,8]{0,3,2,1:T(8,128)} %get-tuple-element.146, ...), kind=kLoop, calls=%fused_computation.60 | loop fusion | flops 3161088 | bytes 4528128 | tf_op jit(solution)/shard_map/transpose(jvp())/add_any | solution.py:26
  83.5 26.4 %all_to_all.28 = f32[256,1,329]{2,1,0:T(1,128)S(1)} all-to-all(f32[256,1,329]{2,1,0:T(1,128)S(1)} %copy.131), channel_id=1, replica_groups=mesh['dp'=2,'tx'=4,'tz'=8,'chan'=4] {'dp','chan','tx','tz'}, dimensions={0} | all-to-all | bytes 673792 | tf_op jit(solution)/shard_map/all_to_all | solution.py:71
  110.2 14.4 %all_to_all.29 = f32[64,1,329]{2,1,0:T(1,128)S(1)} all-to-all(f32[64,1,329]{2,1,0:T(1,128)S(1)} %broadcast_in_dim.259), channel_id=1, replica_groups=mesh['dp'=2,'tx'=4,'tz'=8,'chan'=4] {'dp','tx','tz'}, dimensions={0} | all-to-all | bytes 168448 | tf_op jit(solution)/shard_map/all_to_all | solution.py:61
  128.4 0.7 reshape.543
  129.1 0.7 reshape.542
  (233 shorter events, 24.2 us)
Async XLA Ops:
  0.6 18.4 %copy-start = (f32[48,1024]{1,0:T(8,128)S(1)}, f32[48,1024]{1,0:T(8,128)}, u32[]{:S(2)}) copy-start(f32[48,1024]{1,0:T(8,128)} %param.17) | copy-start | bytes 589828
  0.7 0.8 copy-start.16
  1.5 1.0 copy-start.13
  4.9 10.9 %all-to-all-start = ((f32[4,1,21000]{2,1,0:T(1,128)}), f32[4,1,21000]{2,1,0:T(1,128)S(1)}, u32[]{:S(2)}, u32[]{:S(2)}) async-start(f32[4,1,21000]{2,1,0:T(1,128)} %broadcast_in_dim.200), calls=%async_computation | async-start | bytes 675840 | tf_op jit(solution)/shard_map/all_to_all | solution.py:78
  23.5 26.7 %all-to-all-start.1 = ((f32[128,4,99]{2,1,0:T(4,128)}), f32[128,4,99]{2,1,0:T(4,128)S(1)}, u32[]{:S(2)}, u32[]{:S(2)}) async-start(f32[128,4,99]{2,1,0:T(4,128)} %broadcast_in_dim.203), calls=%async_computation.1 | async-start | bytes 524288 | tf_op jit(solution)/shard_map/all_to_all | solution.py:61
  63.1 1.4 %copy-start.61 = (f32[96]{0:T(128)S(1)}, f32[96]{0:T(128)}, u32[]{:S(2)}) copy-start(f32[96]{0:T(128)} %broadcast_reduce_fusion) | copy-start | bytes 1156
  68.0 8.2 %copy-start.5 = (f32[96,4,8,8]{0,3,2,1:T(8,128)S(1)}, f32[96,4,8,8]{0,3,2,1:T(8,128)}, u32[]{:S(2)}) copy-start(f32[96,4,8,8]{0,3,2,1:T(8,128)} %get-tuple-element.161) | copy-start | bytes 294916
  72.1 0.7 copy-start.26
  72.1 0.7 copy-start.27
  72.1 0.7 copy-start.28
  72.1 0.7 copy-start.29
  72.2 0.7 copy-start.30
  72.2 0.7 copy-start.31
  72.2 0.7 copy-start.32
  72.2 0.7 copy-start.33
  72.2 0.7 copy-start.39
  72.3 0.7 copy-start.45
  72.5 3.7 %copy-start.4 = (f32[96,4,8,8]{0,3,2,1:T(8,128)S(1)}, f32[96,4,8,8]{0,3,2,1:T(8,128)}, u32[]{:S(2)}) copy-start(f32[96,4,8,8]{0,3,2,1:T(8,128)} %get-tuple-element.160) | copy-start | bytes 294916
  73.1 3.1 %copy-start.2 = (f32[96,4,8,8]{0,3,2,1:T(8,128)S(1)}, f32[96,4,8,8]{0,3,2,1:T(8,128)}, u32[]{:S(2)}) copy-start(f32[96,4,8,8]{0,3,2,1:T(8,128)} %get-tuple-element.158) | copy-start | bytes 294916
  73.1 3.1 %copy-start.3 = (f32[96,4,8,8]{0,3,2,1:T(8,128)S(1)}, f32[96,4,8,8]{0,3,2,1:T(8,128)}, u32[]{:S(2)}) copy-start(f32[96,4,8,8]{0,3,2,1:T(8,128)} %get-tuple-element.159) | copy-start | bytes 294916
  76.2 3.2 %copy-start.6 = (f32[96,4,8,8]{0,3,2,1:T(8,128)S(1)}, f32[96,4,8,8]{0,3,2,1:T(8,128)}, u32[]{:S(2)}) copy-start(f32[96,4,8,8]{0,3,2,1:T(8,128)} %get-tuple-element.136) | copy-start | bytes 294916
  76.2 3.2 %copy-start.7 = (f32[96,4,8,8]{0,3,2,1:T(8,128)S(1)}, f32[96,4,8,8]{0,3,2,1:T(8,128)}, u32[]{:S(2)}) copy-start(f32[96,4,8,8]{0,3,2,1:T(8,128)} %get-tuple-element.137) | copy-start | bytes 294916
  76.2 3.2 %copy-start.8 = (f32[96,4,8,8]{0,3,2,1:T(8,128)S(1)}, f32[96,4,8,8]{0,3,2,1:T(8,128)}, u32[]{:S(2)}) copy-start(f32[96,4,8,8]{0,3,2,1:T(8,128)} %get-tuple-element.138) | copy-start | bytes 294916
  76.2 3.2 %copy-start.9 = (f32[96,4,8,8]{0,3,2,1:T(8,128)S(1)}, f32[96,4,8,8]{0,3,2,1:T(8,128)}, u32[]{:S(2)}) copy-start(f32[96,4,8,8]{0,3,2,1:T(8,128)} %get-tuple-element.139) | copy-start | bytes 294916
  76.2 3.2 %copy-start.10 = (f32[96,4,8,8]{0,3,2,1:T(8,128)S(1)}, f32[96,4,8,8]{0,3,2,1:T(8,128)}, u32[]{:S(2)}) copy-start(f32[96,4,8,8]{0,3,2,1:T(8,128)} %get-tuple-element.140) | copy-start | bytes 294916
  76.3 3.2 %copy-start.11 = (f32[96,4,8,8]{0,3,2,1:T(8,128)S(1)}, f32[96,4,8,8]{0,3,2,1:T(8,128)}, u32[]{:S(2)}) copy-start(f32[96,4,8,8]{0,3,2,1:T(8,128)} %get-tuple-element.141) | copy-start | bytes 294916
  79.4 0.7 copy-start.15
  80.3 1.2 copy-start.20
  80.3 1.2 copy-start.21
  80.3 1.2 copy-start.22
  80.7 0.8 copy-start.12
  80.8 0.7 copy-start.19
  (44 other events, 29.3 us)
